TPU v7x, 32 devices: a whole 2x2x4 slice. The times are simulated.
32 devices in a mesh: cells: 8 (over z, y), feat: 4 (over x, core).
Axes of the slice: x: 2, y: 2, z: 4, core: 2. Of those that a mesh axis runs over, the one named last changes fastest.
Arguments:
- expression: bfloat16 [256, 16384], P('feat', 'cells'), may hold values from -6 to 6
- tiles: bfloat16 [128, 8, 128, 128], P('cells'), may hold values from 0.0009994507 to 1
- tile_cols: int32 [128, 8], P('cells'), may hold values from 0 to 127, as said below
- tile_counts: int32 [128], P('cells'), may hold values from 3 to 8
- archetypes: int32 [48], replicated, may hold values from 0 to 16383, as said below
Outputs:
- diffused: bfloat16 [256, 16384], P('feat', 'cells')
- coords: float32 [48, 16384], P(None, 'cells')
Inputs may be any that keep to these rules, and one draw needn't show every extreme that they name: tile_cols[b, 0] = b; slots 1 and 2 hold b - 16 and b + 16 in either order, one that is not a block replaced by the other; every entry lies within 16 of b; slots j >= tile_counts[b] hold b. `archetypes`: distinct cells.
All inputs are finite; a program needn't handle non-finite values.
Results may differ from a plain program's by a relative error of at most 0.0159.
Values may be sent and summed in bfloat16 or wider, within the bound.
No kernel may reach another device: no remote copies, remote signals or barrier semaphores. Data moves between devices by JAX's collectives and lax.ppermute only.
A program may use at most 64 MiB of HBM per device.

v0:
```python
import jax
import jax.numpy as jnp
from jax import lax
from jax.sharding import PartitionSpec as P

F = 256
TILE = 128
NBT = 8


def extended_2(array, sides, width):
    for axis, dim in sides:
        size, length = (lax.axis_size(axis), array.shape[dim])
        up = [(i, (i + 1) % size) for i in range(size - 1)]
        down = [(j, i) for i, j in up]
        last = lax.slice_in_dim(array, length - width, length, axis=dim)
        leading = lax.slice_in_dim(array, 0, width, axis=dim)
        before = lax.ppermute(last, axis, up)
        after = lax.ppermute(leading, axis, down)
        array = jnp.concatenate([before, array, after], axis=dim)
    return array


def diffuse(matrix, tiles, local_cols, kept_mask, degree):
    width = matrix.shape[1]
    blocks = tiles.shape[0]
    extended = extended_2(matrix, (("cells", 1),), width)
    grid = extended.reshape(matrix.shape[0], 3 * blocks, TILE)
    picked = jnp.take(grid, local_cols, axis=1) * kept_mask[None, :, :, None]
    summed = jnp.einsum("fbjc,bjrc->fbr", picked, tiles, preferred_element_type=jnp.float32)
    summed = summed / degree[None, :, :]
    return summed.reshape(matrix.shape[0], width).astype(jnp.bfloat16)


def finish_rows(proj, squares, lower):
    solved = lax.linalg.triangular_solve(lower, proj, left_side=True, lower=True)
    return solved * lax.rsqrt(squares / F + 1e-05)[None, :]


def on_device(expression, tiles, tile_cols, tile_counts, archetypes):
    blocks = tiles.shape[0]
    rows = expression.shape[1]
    kept_mask = (jnp.arange(NBT, dtype=jnp.int32)[None, :] < tile_counts[:, None]).astype(
        jnp.bfloat16
    )
    degree = jnp.einsum("bjrc,bj->br", tiles, kept_mask, preferred_element_type=jnp.float32)
    first_block = lax.axis_index("cells") * blocks
    local_cols = tile_cols - first_block + blocks
    current = expression
    for step in range(2):
        current = diffuse(current, tiles, local_cols, kept_mask, degree)
    local_ids = archetypes - lax.axis_index("cells") * rows
    selector = (jnp.arange(rows, dtype=jnp.int32)[:, None] == local_ids[None, :]).astype(
        jnp.bfloat16
    )
    picked = jnp.dot(current, selector, preferred_element_type=jnp.float32)
    arch_part = lax.psum(picked, "cells")
    arch_local = arch_part.T.astype(jnp.bfloat16)
    partial_gram = jnp.dot(arch_local, arch_local.T, preferred_element_type=jnp.float32)
    gram = lax.psum(partial_gram, "feat")
    lower = jnp.linalg.cholesky(gram)
    proj = jnp.dot(arch_local, current, preferred_element_type=jnp.float32)
    values = current.astype(jnp.float32)
    squares = jnp.sum(values * values, axis=0)
    proj_sum, square_sum = lax.psum((proj, squares), "feat")
    coords = finish_rows(proj_sum, square_sum, lower)
    return (current, coords)


def solution(mesh):
    return jax.shard_map(
        on_device,
        mesh=mesh,
        in_specs=(
            P("feat", "cells"),
            P("cells", None, None, None),
            P("cells", None),
            P("cells"),
            P(),
        ),
        out_specs=(P("feat", "cells"), P(None, "cells")),
        check_vma=False,
    )
```

profile of v0, /device:TPU:0, one launch (start us, length us, event | category | flops | bytes accessed | tf_op | source)
XLA Modules:
  0.0 147.4 jit_solution(15856204020431653385)
XLA Ops:
  7.2 4.9 %collective-permute-start = (bf16[64,2048]{1,0:T(8,128)(2,1)}, bf16[64,2048]{1,0:T(8,128)(2,1)S(1)}, u32[]{:S(2)}, u32[]{:S(2)}) collective-permute-start(bf16[64,2048]{1,0:T(8,128)(2,1)} %param.7), channel_id=1, source_target_pairs={{0,4},{4,8},{8,12},{12,16},{16,20},{20,24},{24,28},{1,5},{5,9},{9,... | collective-permute-start | bytes 786440 | tf_op jit(solution)/shard_map/ppermute | solution.py:18
  12.1 1.3 collective-permute-start.1
  13.4 0.7 fusion.24
  14.1 0.7 compare_and_fusion
  15.0 3.4 %convert_reduce_fusion = bf16[16,8,128]{2,1,0:T(8,128)(2,1)S(1)} fusion(bf16[16,8,128,128]{3,2,1,0:T(8,128)(2,1)} %param.8), kind=kLoop, calls=%fused_computation.2 | loop fusion | flops 4177920 | bytes 4227072 | tf_op jit(solution)/shard_map/bjrc,bj->br/reduce_sum | solution.py:46
  18.7 4.9 %collective-permute-done = bf16[64,2048]{1,0:T(8,128)(2,1)S(1)} collective-permute-done((bf16[64,2048]{1,0:T(8,128)(2,1)}, bf16[64,2048]{1,0:T(8,128)(2,1)S(1)}, u32[]{:S(2)}, u32[]{:S(2)}) %collective-permute-start) | collective-permute-done | bytes 262176 | tf_op jit(solution)/shard_map/ppermute | solution.py:18
  23.8 1.0 gather_fusion
  24.8 3.8 %fusion.17 = bf16[16,8,8,128]{3,2,1,0:T(8,128)(2,1)S(1)} fusion(bf16[16,8,128,128]{3,2,1,0:T(8,128)(2,1)} %param.8, bf16[16,8,64,128]{3,2,1,0:T(8,128)(2,1)S(1)} %bitcast.86, pred[16,8]{1,0:T(8,128)(4,1)S(1)} %copy.22, bf16[16,8]{1,0:T(8,128)(2,1)S(1)} %get-tuple-element.8, f32[16,128]{1,0:T(8,128)S(1)} %bitcast.91), kind=kOutput, calls=%fused_computation.24 | convolution fusion | flops 270794752 | bytes 6562176 | tf_op jit(solution)/shard_map/fbjc,bjrc->fbr/dot_general | solution.py:30
  28.6 1.3 collective-permute-start.3
  29.9 4.9 %collective-permute-start.2 = (bf16[64,2048]{1,0:T(8,128)(2,1)S(1)}, bf16[64,2048]{1,0:T(8,128)(2,1)S(1)}, u32[]{:S(2)}, u32[]{:S(2)}) collective-permute-start(bf16[64,2048]{1,0:T(8,128)(2,1)S(1)} %bitcast.88), channel_id=1, source_target_pairs={{0,4},{4,8},{8,12},{12,16},{16,20},{20,24},{24,28},{1,5},{5,9},{9,... | collective-permute-start | bytes 786440 | tf_op jit(solution)/shard_map/ppermute | solution.py:18
  34.9 3.5 %collective-permute-done.3 = bf16[64,2048]{1,0:T(8,128)(2,1)S(1)} collective-permute-done((bf16[64,2048]{1,0:T(8,128)(2,1)S(1)}, bf16[64,2048]{1,0:T(8,128)(2,1)S(1)}, u32[]{:S(2)}, u32[]{:S(2)}) %collective-permute-start.3) | collective-permute-done | bytes 262176 | tf_op jit(solution)/shard_map/ppermute | solution.py:19
  38.3 6.6 %collective-permute-done.2 = bf16[64,2048]{1,0:T(8,128)(2,1)S(1)} collective-permute-done((bf16[64,2048]{1,0:T(8,128)(2,1)S(1)}, bf16[64,2048]{1,0:T(8,128)(2,1)S(1)}, u32[]{:S(2)}, u32[]{:S(2)}) %collective-permute-start.2) | collective-permute-done | bytes 262176 | tf_op jit(solution)/shard_map/ppermute | solution.py:18
  45.2 1.0 gather_fusion.1
  46.1 3.8 %multiply_reduce_fusion = (f32[16,128]{1,0:T(8,128)S(1)}, bf16[16,64,128]{2,1,0:T(8,128)(2,1)S(1)}) fusion(f32[16,128]{1,0:T(8,128)S(1)} %bitcast.92, bf16[16,8,128,128]{3,2,1,0:T(8,128)(2,1)} %param.8, bf16[16,8,64,128]{3,2,1,0:T(8,128)(2,1)S(1)} %bitcast.85, pred[16,8]{1,0:T(8,128)(4,1)S(1)} %copy.22, bf16[16,8]{1,0:T(8,128)(2,1)S(1)} %get-tuple-element.8), kind=kOutput, calls=%fused_computation.29 | convolution fusion | flops 271185920 | bytes 6570368 | tf_op jit(solution)/shard_map/fbjc,bjrc->fbr/dot_general | solution.py:30
  50.0 0.4 fusion.12
  50.4 36.7 %psum.28 = bf16[64,48]{0,1:T(8,128)(2,1)S(1)} all-reduce(f32[64,48]{0,1:T(8,128)S(1)} %fusion.12), channel_id=1, replica_groups=mesh['cells'=8,'feat'=4] {'cells'}, use_global_device_ids=true, to_apply=%region_1.0 | all-reduce | flops 3072 | bytes 18432 | tf_op jit(solution)/shard_map/psum | solution.py:57
  87.2 0.9 fusion.32
  88.2 10.3 %all-reduce = (f32[2048]{0:T(1024)S(1)}, f32[48,48]{0,1:T(8,128)S(1)}) all-reduce(f32[2048]{0:T(1024)S(1)} %bitcast.90, f32[48,48]{0,1:T(8,128)S(1)} %fusion.33), channel_id=1, replica_groups=mesh['cells'=8,'feat'=4] {'feat'}, use_global_device_ids=true, to_apply=%region_7.9 | all-reduce | flops 4352 | bytes 34816 | tf_op jit(solution)/shard_map/psum | solution.py:65
  98.6 4.4 %cholesky.16 = f32[48,48]{1,0:T(8,128)S(1)} custom-call(f32[48,48]{1,0:T(8,128)S(1)} %fusion.23), custom_call_target="Cholesky" | custom-call | tf_op jit(solution)/shard_map/jit(cholesky)/cholesky | solution.py:61
  103.0 0.7 compare_reduce_fusion
  103.7 0.7 fusion.21
  104.4 3.7 %custom-call.6 = f32[1,48,48]{1,2,0:T(8,128)S(1)} custom-call(f32[1,48,48]{2,1,0:T(8,128)S(1)} %fusion.21), custom_call_target="InvertDiagBlocksLowerTriangular" | custom-call | tf_op jit(solution)/shard_map/triangular_solve | solution.py:36
  108.1 30.1 %all-reduce.3.cloned.1.call-done = f32[48,2048]{1,0:T(8,128)} async-done(((f32[48,2048]{1,0:T(8,128)}), f32[48,2048]{1,0:T(8,128)}) %all-reduce.3.cloned.1.call-update) | async-done | bytes 393232 | tf_op jit(solution)/shard_map/psum | solution.py:65
  138.2 2.3 %convolution_multiply_fusion = f32[48,2048]{1,0:T(8,128)} fusion(f32[48,2048]{1,0:T(8,128)} %all-reduce.3.cloned.1.call-done, f32[2048]{0:T(1024)S(1)} %add_rsqrt_fusion, f32[1,48,48]{1,2,0:T(8,128)S(1)} %custom-call.6), kind=kOutput, calls=%fused_computation.3 | convolution fusion | flops 56721408 | bytes 803840 | tf_op jit(solution)/shard_map/triangular_solve | solution.py:36
  (24 shorter events, 1.2 us)
Async XLA Ops:
  7.2 131.1 %all-reduce.3.cloned.1.call-start = ((), (), s32[]{:S(2)}) async-start(), calls=%async_computation | async-start | bytes 786432 | tf_op jit(solution)/shard_map/psum | solution.py:65
  7.2 16.4 %collective-permute-start = (bf16[64,2048]{1,0:T(8,128)(2,1)}, bf16[64,2048]{1,0:T(8,128)(2,1)S(1)}, u32[]{:S(2)}, u32[]{:S(2)}) collective-permute-start(bf16[64,2048]{1,0:T(8,128)(2,1)} %param.7), channel_id=1, source_target_pairs={{0,4},{4,8},{8,12},{12,16},{16,20},{20,24},{24,28},{1,5},{5,9},{9,... | collective-permute-start | bytes 786440 | tf_op jit(solution)/shard_map/ppermute | solution.py:18
  12.1 11.5 %collective-permute-start.1 = (bf16[64,2048]{1,0:T(8,128)(2,1)}, bf16[64,2048]{1,0:T(8,128)(2,1)S(1)}, u32[]{:S(2)}, u32[]{:S(2)}) collective-permute-start(bf16[64,2048]{1,0:T(8,128)(2,1)} %param.7), channel_id=1, source_target_pairs={{4,0},{8,4},{12,8},{16,12},{20,16},{24,20},{28,24},{5,1},{9,5},{13... | collective-permute-start | bytes 786440 | tf_op jit(solution)/shard_map/ppermute | solution.py:19
  15.0 8.6 %copy-start.1 = (bf16[64,2048]{1,0:T(8,128)(2,1)S(1)}, bf16[64,2048]{1,0:T(8,128)(2,1)}, u32[]{:S(2)}) copy-start(bf16[64,2048]{1,0:T(8,128)(2,1)} %param.7) | copy-start | bytes 786436
  24.8 10.1 %copy-start.2 = (s32[48]{0:T(128)S(1)}, s32[48]{0:T(128)}, u32[]{:S(2)}) copy-start(s32[48]{0:T(128)} %param.11) | copy-start | bytes 580
  28.6 9.7 %collective-permute-start.3 = (bf16[64,2048]{1,0:T(8,128)(2,1)S(1)}, bf16[64,2048]{1,0:T(8,128)(2,1)S(1)}, u32[]{:S(2)}, u32[]{:S(2)}) collective-permute-start(bf16[64,2048]{1,0:T(8,128)(2,1)S(1)} %bitcast.87), channel_id=1, source_target_pairs={{4,0},{8,4},{12,8},{16,12},{20,16},{24,20},{28,24},{5,1},{9,5},{13... | collective-permute-start | bytes 786440 | tf_op jit(solution)/shard_map/ppermute | solution.py:19
  29.9 15.0 %collective-permute-start.2 = (bf16[64,2048]{1,0:T(8,128)(2,1)S(1)}, bf16[64,2048]{1,0:T(8,128)(2,1)S(1)}, u32[]{:S(2)}, u32[]{:S(2)}) collective-permute-start(bf16[64,2048]{1,0:T(8,128)(2,1)S(1)} %bitcast.88), channel_id=1, source_target_pairs={{0,4},{4,8},{8,12},{12,16},{16,20},{20,24},{24,28},{1,5},{5,9},{9,... | collective-permute-start | bytes 786440 | tf_op jit(solution)/shard_map/ppermute | solution.py:18
  50.0 90.5 %copy-start = (bf16[64,2048]{1,0:T(8,128)(2,1)}, bf16[64,2048]{1,0:T(8,128)(2,1)S(1)}, u32[]{:S(2)}) copy-start(bf16[64,2048]{1,0:T(8,128)(2,1)S(1)} %copy_bitcast_fusion.2) | copy-start | bytes 786436
Sparse Core Ops, SparseCore 0:
  108.2 29.9 all-reduce.2
where the time goes:
time: 148 us; the launch traced here: 147 us
  blocking collectives  46.9 us (32%)
  waiting for transfers between devices  45.1 us (30%)
  other arithmetic  14.8 us (10%)
  between operations  14.2 us (10%)
  starting transfers between devices  12.4 us (8%)
  matrix products  11.5 us (8%)
  local copies, waits for them, and re-layouts  2.32 us (2%)
    psum x1, blocking collectives, on_device(): arch_part = lax.psum(picked, 'cells')  36.7 us
    psum x1, waiting for transfers between devices, on_device(): proj_sum, square_sum = lax.psum((proj, squares), 'feat')  30.1 us
    ppermute x2, waiting for transfers between devices, extended_2(): before = lax.ppermute(last, axis, up)  11.5 us
    psum x1, blocking collectives, on_device(): proj_sum, square_sum = lax.psum((proj, squares), 'feat')  10.3 us
    ppermute x2, starting transfers between devices, extended_2(): before = lax.ppermute(last, axis, up)  9.81 us
    dot_general x2, matrix products, diffuse(): jnp.einsum('fbjc,bjrc->fbr', picked, tiles, preferred_element_type=jnp.fl...  7.61 us
    another operation x3, other arithmetic, on_device(): lower = jnp.linalg.cholesky(gram)  5.13 us
    another operation x2, other arithmetic, finish_rows(): lax.linalg.triangular_solve(lower, proj, left_side=True, lower=True)  4.38 us
  transfers between devices with their start and end apart: 5, of which 4 were waited for; matrix products, arithmetic and copies ran while one was open for 4% of the time, Pallas kernels for 0%

commit v1 on v0

v1 whole, which is shorter than its diff:
```python
import functools
import jax
import jax.numpy as jnp
from jax import lax
from jax.experimental import pallas as pl
from jax.experimental.pallas import tpu as pltpu
from jax.sharding import PartitionSpec as P

F = 256
TILE = 128
NBT = 8
EPS = 1e-05

VMEM = pl.BlockSpec(memory_space=pltpu.VMEM)
SMEM = pl.BlockSpec(memory_space=pltpu.SMEM)
LAST = (((1,), (1,)), ((), ()))


def dot_last(a, b):
    return lax.dot_general(a, b, LAST, preferred_element_type=jnp.float32)


def lanes(block):
    return pl.ds(pl.multiple_of(block * TILE, TILE), TILE)


def wide_tile(tiles_ref, b, slots):
    return jnp.concatenate([tiles_ref[b, j] for j in slots], axis=1)


def own_kernel(with_degree, meta_ref, cols_ref, counts_ref, tiles_ref, v_ref, acc_ref, *deg_ref):
    blocks = tiles_ref.shape[0]
    first_block = meta_ref[0]
    feats = v_ref.shape[0]
    for b in range(blocks):
        parts = []
        slots = [j for j in range(NBT) if j not in (1, 2)] if not with_degree else list(range(NBT))
        ones = []
        for j in slots:
            local = cols_ref[b, j] - first_block
            used = j < counts_ref[b]
            mine = jnp.logical_and(used, jnp.logical_and(local >= 0, local < blocks))
            x = v_ref[:, lanes(jnp.clip(local, 0, blocks - 1))]
            parts.append(jnp.where(mine, x, jnp.zeros_like(x)))
            ones.append(jnp.full((16, TILE), jnp.where(used, 1.0, 0.0), jnp.float32).astype(jnp.bfloat16))
        wide = wide_tile(tiles_ref, b, slots)
        lhs = jnp.concatenate(parts, axis=1)
        if with_degree:
            lhs = jnp.concatenate([lhs, jnp.concatenate(ones, axis=1)], axis=0)
        out = dot_last(lhs, wide)
        acc_ref[:, b * TILE:(b + 1) * TILE] = out[:feats]
        if with_degree:
            deg_ref[0][b] = out[feats:feats + 8]


def rest_kernel(meta_ref, cols_ref, counts_ref, tiles_ref, even_ref, odd_ref, acc_ref, deg_ref, out_ref):
    blocks = tiles_ref.shape[0]
    first_block, odd = meta_ref[0], meta_ref[1]
    feats = acc_ref.shape[0]
    for b in range(blocks):
        parts = []
        slots = list(range(1, NBT))
        for j in slots:
            local = cols_ref[b, j] - first_block
            lower, upper = local < 0, local >= blocks
            used = jnp.logical_and(j < counts_ref[b], jnp.logical_or(lower, upper))
            at = jnp.where(lower, local + blocks, jnp.where(upper, local - blocks, 0))
            partner = jnp.where(odd == 1, lower, upper)
            x = jnp.where(partner, even_ref[:, lanes(at)], odd_ref[:, lanes(at)])
            parts.append(jnp.where(used, x, jnp.zeros_like(x)))
        out = dot_last(jnp.concatenate(parts, axis=1), wide_tile(tiles_ref, b, slots))
        out = out + acc_ref[:, b * TILE:(b + 1) * TILE]
        out = out / deg_ref[b][:1]
        out_ref[:, b * TILE:(b + 1) * TILE] = out.astype(jnp.bfloat16)


def call(kernel, out_shape, n_smem, args, flops, nbytes):
    single = not isinstance(out_shape, (list, tuple))
    return pl.pallas_call(
        kernel,
        out_shape=out_shape,
        in_specs=[SMEM] * n_smem + [VMEM] * (len(args) - n_smem),
        out_specs=VMEM if single else [VMEM] * len(out_shape),
        compiler_params=pltpu.CompilerParams(vmem_limit_bytes=32 << 20),
        cost_estimate=pl.CostEstimate(flops=flops, bytes_accessed=nbytes, transcendentals=0),
    )(*args)


def exchange(matrix):
    size = lax.axis_size("cells")
    pairs = [(i, i ^ 1) for i in range(size)]
    others = [(i, i + 1) for i in range(1, size - 1, 2)]
    others = others + [(j, i) for i, j in others]
    return lax.ppermute(matrix, "cells", pairs), lax.ppermute(matrix, "cells", others)


def solve_kernel(a0, a1, a2, a3, q_ref, work_ref):
    pieces = [a0, a1, a2, a3]
    n = a0.shape[0]
    gram = sum(dot_last(p[...], p[...]) for p in pieces)
    row = lax.broadcasted_iota(jnp.int32, (n, n), 0)
    col = lax.broadcasted_iota(jnp.int32, (n, n), 1)
    aug = jnp.concatenate([gram, jnp.where(row == col, 1.0, 0.0)], axis=1)
    rows = lax.broadcasted_iota(jnp.int32, (n, 1), 0)
    for k in range(n):
        pivot = aug[k:k + 1, :]
        inv = lax.rsqrt(pivot[:, k:k + 1])
        inv = inv * (1.5 - 0.5 * pivot[:, k:k + 1] * inv * inv)
        scaled = pivot * inv
        factor = aug[:, k:k + 1] * inv
        aug = jnp.where(rows == k, scaled, jnp.where(rows > k, aug - factor * scaled, aug))
    inverse = aug[:, n:]
    high = inverse.astype(jnp.bfloat16)
    low = (inverse - high.astype(jnp.float32)).astype(jnp.bfloat16)
    lower = (inverse - high.astype(jnp.float32) - low.astype(jnp.float32)).astype(jnp.bfloat16)
    lhs = jnp.concatenate([high, low, lower], axis=0)
    for i, p in enumerate(pieces):
        q = lax.dot_general(lhs, p[...], (((1,), (0,)), ((), ())), preferred_element_type=jnp.float32)
        q = q[:n] + q[n:2 * n] + q[2 * n:]
        q_high = q.astype(jnp.bfloat16)
        q_low = (q - q_high.astype(jnp.float32)).astype(jnp.bfloat16)
        q_ref[i] = jnp.concatenate([q_high, q_low], axis=0)


def finish_kernel(meta_ref, q_ref, d0, d1, d2, d3, out_ref):
    n = out_ref.shape[0]
    width = out_ref.shape[1]
    me = meta_ref[2]
    flip1, flip2 = (me & 1) == 1, (me & 2) == 2
    q = jnp.concatenate([q_ref[i] for i in range(4)], axis=1)
    step = 256
    for c in range(0, width, step):
        p = [d[:, c:c + step] for d in (d0, d1, d2, d3)]
        p = [jnp.where(flip1, p[i ^ 1], p[i]) for i in range(4)]
        p = [jnp.where(flip2, p[i ^ 2], p[i]) for i in range(4)]
        d = jnp.concatenate(p, axis=0)
        z = lax.dot_general(q, d, (((1,), (0,)), ((), ())), preferred_element_type=jnp.float32)
        wide = d.astype(jnp.float32)
        sq = jnp.sum(wide * wide, axis=0, keepdims=True)
        out_ref[:, c:c + step] = (z[:n] + z[n:]) * lax.rsqrt(sq / F + EPS)


def gather_feat(x):
    size = lax.axis_size("feat")
    near = lax.ppermute(x, "feat", [(i, i ^ 1) for i in range(size)])
    far = lax.ppermute(x, "feat", [(i, i ^ 2) for i in range(size)])
    both = lax.ppermute(far, "feat", [(i, i ^ 1) for i in range(size)])
    return x, near, far, both


def on_device(expression, tiles, tile_cols, tile_counts, archetypes):
    blocks = tiles.shape[0]
    feats, rows = expression.shape
    narch = archetypes.shape[0]
    cell, feat = lax.axis_index("cells"), lax.axis_index("feat")
    meta = jnp.stack([cell * blocks, cell & 1, feat]).astype(jnp.int32)
    tile_flops = 2 * feats * TILE * TILE * NBT * blocks
    tile_bytes = 2 * TILE * TILE * NBT * blocks
    scalars = (meta, tile_cols, tile_counts)
    acc_shape = jax.ShapeDtypeStruct((feats, rows), jnp.float32)

    pair, other = exchange(expression)
    acc, degree = call(
        functools.partial(own_kernel, True),
        [acc_shape, jax.ShapeDtypeStruct((blocks, 8, TILE), jnp.float32)],
        3, (*scalars, tiles, expression), tile_flops, tile_bytes)
    out_bf16 = jax.ShapeDtypeStruct((feats, rows), jnp.bfloat16)
    first = call(rest_kernel, out_bf16, 3, (*scalars, tiles, pair, other, acc, degree), tile_flops, tile_bytes)
    pair, other = exchange(first)
    acc = call(functools.partial(own_kernel, False), acc_shape, 3, (*scalars, tiles, first), tile_flops, tile_bytes)
    diffused = call(rest_kernel, out_bf16, 3, (*scalars, tiles, pair, other, acc, degree), tile_flops, tile_bytes)

    pieces = gather_feat(diffused)

    local_ids = archetypes - cell * rows
    selector = (local_ids[:, None] == jnp.arange(rows, dtype=jnp.int32)[None, :]).astype(jnp.bfloat16)
    picked = lax.dot_general(selector, diffused, LAST, preferred_element_type=jnp.float32)
    picked = picked.astype(jnp.bfloat16)
    size = lax.axis_size("cells")
    spread = lax.all_to_all(jnp.broadcast_to(picked[None], (size, *picked.shape)), "cells", 0, 0)
    arch = jnp.sum(spread.astype(jnp.float32), axis=0).astype(jnp.bfloat16)
    near = lax.ppermute(arch, "feat", [(i, i ^ 1) for i in range(4)])
    far = lax.ppermute(arch, "feat", [(i, i ^ 2) for i in range(4)])
    both = lax.ppermute(arch, "feat", [(i, i ^ 3) for i in range(4)])
    parts = [arch, near, far, both]
    parts = [jnp.where((feat & 1) == 1, parts[i ^ 1], parts[i]) for i in range(4)]
    parts = [jnp.where((feat & 2) == 2, parts[i ^ 2], parts[i]) for i in range(4)]
    q = pl.pallas_call(
        solve_kernel,
        out_shape=jax.ShapeDtypeStruct((4, 2 * narch, feats), jnp.bfloat16),
        in_specs=[VMEM] * 4, out_specs=VMEM,
        scratch_shapes=[pltpu.VMEM((narch, 2 * narch), jnp.float32)],
        cost_estimate=pl.CostEstimate(flops=1 << 20, bytes_accessed=1 << 17, transcendentals=0),
    )(*parts)
    coords = call(finish_kernel, jax.ShapeDtypeStruct((narch, rows), jnp.float32), 1,
                  (meta, q, *pieces), 2 * 2 * narch * F * rows, 4 * narch * rows)
    return diffused, coords


def solution(mesh):
    return jax.shard_map(
        on_device,
        mesh=mesh,
        in_specs=(
            P("feat", "cells"),
            P("cells", None, None, None),
            P("cells", None),
            P("cells"),
            P(),
        ),
        out_specs=(P("feat", "cells"), P(None, "cells")),
        check_vma=False,
    )
```

time: 148 us -> 66.9 us (0.45)
  blocking collectives: 46.9 us -> 0 us
  waiting for transfers between devices: 45.1 us -> 17.7 us
  Pallas kernels: 0 us -> 17.2 us
  other arithmetic: 14.8 us -> 0.74 us
  between operations: 14.2 us -> 0.75 us
  matrix products: 11.5 us -> 1.24 us
  local copies, waits for them, and re-layouts: 2.32 us -> 9.47 us
  starting transfers between devices: 12.4 us -> 19.3 us
    psum x2 -> x0, blocking collectives: 46.9 us -> none  [the longest x1 36.7 us: on_device(): arch_part = lax.psum(picked, 'cells')]
    psum x1 -> x0, waiting for transfers between devices: 30.1 us -> none  [on_device(): proj_sum, square_sum = lax.psum((proj, squares), 'feat')]
    pallas_call x0 -> x6, Pallas kernels: none -> 17.2 us  [the longest x5 10.9 us: call(): pl.pallas_call(kernel, out_shape=out_shape, in_specs=[SMEM] * n_smem + [V...]
    another operation x5 -> x1, other arithmetic: 9.52 us -> 0.08 us  [on_device(): meta = jnp.stack([cell * blocks, cell & 1, feat]).astype(jnp.int32)]
    unnamed x6 -> x19, local copies, waits for them, and re-layouts: 0.02 us -> 9.45 us
    dot_general x6 -> x1, matrix products: 9.24 us -> 1.24 us  [on_device(): lax.dot_general(selector, diffused, LAST, preferred_element_type=jnp.floa...]
    all_to_all x0 -> x1, waiting for transfers between devices: none -> 6.28 us  [on_device(): lax.all_to_all(jnp.broadcast_to(picked[None], (size, *picked.shape)), 'ce...]
    all_to_all x0 -> x1, starting transfers between devices: none -> 5.85 us  [on_device(): lax.all_to_all(jnp.broadcast_to(picked[None], (size, *picked.shape)), 'ce...]
  transfers between devices with their start and end apart: 5 -> 11, of which waited for: 4 -> 4; matrix products, arithmetic and copies ran while one was open for 4% -> 5% of each run, Pallas kernels for 0% -> 16%
where the time goes in v1:
time: 66.9 us; the launch traced here: 66.4 us
  starting transfers between devices  19.3 us (29%)
  waiting for transfers between devices  17.7 us (26%)
  Pallas kernels  17.2 us (26%)
  local copies, waits for them, and re-layouts  9.47 us (14%)
  matrix products  1.24 us (2%)
  between operations  0.75 us (1%)
  other arithmetic  0.74 us (1%)
    pallas_call x5, Pallas kernels, call(): pl.pallas_call(kernel, out_shape=out_shape, in_specs=[SMEM] * n_smem + [V...  10.9 us
    unnamed x19, local copies, waits for them, and re-layouts  9.45 us
    ppermute x2, waiting for transfers between devices, exchange(): lax.ppermute(matrix, 'cells', pairs)  9.42 us
    ppermute x2, starting transfers between devices, exchange(): lax.ppermute(matrix, 'cells', pairs)  8.23 us
    all_to_all x1, waiting for transfers between devices, on_device(): lax.all_to_all(jnp.broadcast_to(picked[None], (size, *picked.shape)), 'ce...  6.28 us
    pallas_call x1, Pallas kernels, on_device(): pl.pallas_call(solve_kernel, out_shape=jax.ShapeDtypeStruct((4, 2 * narch...  6.23 us
    all_to_all x1, starting transfers between devices, on_device(): lax.all_to_all(jnp.broadcast_to(picked[None], (size, *picked.shape)), 'ce...  5.85 us
    ppermute x1, waiting for transfers between devices, on_device(): far = lax.ppermute(arch, 'feat', [(i, i ^ 2) for i in range(4)])  1.98 us
  transfers between devices with their start and end apart: 11, of which 4 were waited for; matrix products, arithmetic and copies ran while one was open for 5% of the time, Pallas kernels for 16%

profile of v1, /device:TPU:0, one launch (start us, length us, event | category | flops | bytes accessed | tf_op | source)
XLA Modules:
  0.0 66.4 jit_solution(7034708373800588717)
XLA Ops:
  0.6 3.0 %collective-permute-start = (bf16[64,2048]{1,0:T(8,128)(2,1)}, bf16[64,2048]{1,0:T(8,128)(2,1)S(1)}, u32[]{:S(2)}, u32[]{:S(2)}) collective-permute-start(bf16[64,2048]{1,0:T(8,128)(2,1)} %v_ref.1), channel_id=1, source_target_pairs={{0,4},{4,0},{8,12},{12,8},{16,20},{20,16},{24,28},{28,24},{1,5},{5... | collective-permute-start | bytes 786440 | tf_op jit(solution)/shard_map/ppermute | solution.py:94
  4.3 0.8 %copy.14.cols_ref = s32[16,8]{1,0:T(8,128)S(1)} copy(s32[16,8]{0,1:T(8,128)} %param.7) | data formatting | bytes 1024 | tf_op args[2]
  5.2 2.2 %copy-done = bf16[16,8,128,128]{3,2,1,0:T(8,128)(2,1)S(1)} copy-done((bf16[16,8,128,128]{3,2,1,0:T(8,128)(2,1)S(1)}, bf16[16,8,128,128]{3,2,1,0:T(8,128)(2,1)}, u32[]{:S(2)}) %copy-start) | copy-done | bytes 4194328
  7.4 0.9 %copy-done.4 = bf16[64,2048]{1,0:T(8,128)(2,1)S(1)} copy-done((bf16[64,2048]{1,0:T(8,128)(2,1)S(1)}, bf16[64,2048]{1,0:T(8,128)(2,1)}, u32[]{:S(2)}) %copy-start.4) | copy-done | bytes 262168
  9.0 2.3 %shard_map.68 = (f32[64,2048]{1,0:T(8,128)S(1)}, f32[16,8,128]{2,1,0:T(8,128)S(1)}) custom-call(s32[3]{0:T(128)S(1)} %pad_add_fusion.meta_ref, s32[16,8]{1,0:T(8,128)S(1)} %copy.14.cols_ref, s32[16]{0:T(128)S(1)} %copy-done.5, bf16[16,8,128,128]{3,2,1,0:T(8,128)(2,1)S(1)} %copy-done, bf16[64,2048]{1,0:T(8,128)(2,1)S(1)} %copy-done.4), custom_call_target="tpu_custom_call" | custom-call | flops 268435456 | bytes 4194304 | tf_op jit(solution)/shard_map/pallas_call | solution.py:79
  11.2 3.9 %collective-permute-done.even_ref = bf16[64,2048]{1,0:T(8,128)(2,1)S(1)} collective-permute-done((bf16[64,2048]{1,0:T(8,128)(2,1)}, bf16[64,2048]{1,0:T(8,128)(2,1)S(1)}, u32[]{:S(2)}, u32[]{:S(2)}) %collective-permute-start) | collective-permute-done | bytes 262176 | tf_op jit(solution)/shard_map/ppermute | solution.py:94
  15.2 2.2 %shard_map.69.v_ref = bf16[64,2048]{1,0:T(8,128)(2,1)S(1)} custom-call(s32[3]{0:T(128)S(1)} %pad_add_fusion.meta_ref, s32[16,8]{1,0:T(8,128)S(1)} %copy.14.cols_ref, s32[16]{0:T(128)S(1)} %copy-done.5, bf16[16,8,128,128]{3,2,1,0:T(8,128)(2,1)S(1)} %copy-done, bf16[64,2048]{1,0:T(8,128)(2,1)S(1)} %collective-permute-done.even_ref, ...), custom_call_target="tpu_custom_call" | custom-call | flops 268435456 | bytes 4194304 | tf_op jit(solution)/shard_map/pallas_call | solution.py:79
  17.3 0.7 %collective-permute-start.3 = (bf16[64,2048]{1,0:T(8,128)(2,1)S(1)}, bf16[64,2048]{1,0:T(8,128)(2,1)S(1)}, u32[]{:S(2)}, u32[]{:S(2)}) collective-permute-start(bf16[64,2048]{1,0:T(8,128)(2,1)S(1)} %shard_map.69.v_ref), channel_id=1, source_target_pairs={{4,8},{12,16},{20,24},{8,4},{16,12},{24,20},{5,9},{13,17},{21,25},... | collective-permute-start | bytes 786440 | tf_op jit(solution)/shard_map/ppermute | solution.py:94
  18.0 5.2 %collective-permute-start.2 = (bf16[64,2048]{1,0:T(8,128)(2,1)S(1)}, bf16[64,2048]{1,0:T(8,128)(2,1)S(1)}, u32[]{:S(2)}, u32[]{:S(2)}) collective-permute-start(bf16[64,2048]{1,0:T(8,128)(2,1)S(1)} %shard_map.69.v_ref), channel_id=1, source_target_pairs={{0,4},{4,0},{8,12},{12,8},{16,20},{20,16},{24,28},{28,24},{1,5},{5... | collective-permute-start | bytes 786440 | tf_op jit(solution)/shard_map/ppermute | solution.py:94
  23.2 2.2 %copy-done.1 = bf16[16,8,128,128]{3,2,1,0:T(8,128)(2,1)S(1)} copy-done((bf16[16,8,128,128]{3,2,1,0:T(8,128)(2,1)S(1)}, bf16[16,8,128,128]{3,2,1,0:T(8,128)(2,1)}, u32[]{:S(2)}) %copy-start.1) | copy-done | bytes 4194328
  25.4 1.9 %shard_map.70.acc_ref = f32[64,2048]{1,0:T(8,128)S(1)} custom-call(s32[3]{0:T(128)S(1)} %pad_add_fusion.meta_ref, s32[16,8]{1,0:T(8,128)S(1)} %copy.14.cols_ref, s32[16]{0:T(128)S(1)} %copy-done.6, bf16[16,8,128,128]{3,2,1,0:T(8,128)(2,1)S(1)} %copy-done.1, bf16[64,2048]{1,0:T(8,128)(2,1)S(1)} %shard_map.69.v_ref), custom_call_target="tpu_custom_call" | custom-call | flops 268435456 | bytes 4194304 | tf_op jit(solution)/shard_map/pallas_call | solution.py:79
  27.3 5.5 %collective-permute-done.2.even_ref = bf16[64,2048]{1,0:T(8,128)(2,1)S(1)} collective-permute-done((bf16[64,2048]{1,0:T(8,128)(2,1)S(1)}, bf16[64,2048]{1,0:T(8,128)(2,1)S(1)}, u32[]{:S(2)}, u32[]{:S(2)}) %collective-permute-start.2) | collective-permute-done | bytes 262176 | tf_op jit(solution)/shard_map/ppermute | solution.py:94
  32.8 2.9 %shard_map.71.d0 = bf16[64,2048]{1,0:T(8,128)(2,1)} custom-call(s32[3]{0:T(128)S(1)} %pad_add_fusion.meta_ref, s32[16,8]{1,0:T(8,128)S(1)} %copy.14.cols_ref, s32[16]{0:T(128)S(1)} %copy-done.6, bf16[16,8,128,128]{3,2,1,0:T(8,128)(2,1)S(1)} %copy-done.1, bf16[64,2048]{1,0:T(8,128)(2,1)S(1)} %collective-permute-done.2.even_ref, ...), custom_call_target="tpu_custom_call" | custom-call | flops 268435456 | bytes 4194304 | tf_op jit(solution)/shard_map/pallas_call | solution.py:79
  35.7 1.5 %collective-permute-start.8 = (bf16[64,2048]{1,0:T(8,128)(2,1)}, bf16[64,2048]{1,0:T(8,128)(2,1)S(1)}, u32[]{:S(2)}, u32[]{:S(2)}) collective-permute-start(bf16[64,2048]{1,0:T(8,128)(2,1)} %shard_map.71.d0), channel_id=1, source_target_pairs={{0,2},{1,3},{2,0},{3,1},{4,6},{5,7},{6,4},{7,5},{8,10},{9,11},{10,... | collective-permute-start | bytes 786440 | tf_op jit(solution)/shard_map/ppermute | solution.py:146
  37.2 1.2 %convolution_convert_fusion = bf16[48,64]{1,0:T(8,128)(2,1)S(1)} fusion(bf16[64,2048]{1,0:T(8,128)(2,1)} %shard_map.71.d0, s32[48]{0:T(128)S(1)} %broadcast_subtract_fusion), kind=kOutput, calls=%fused_computation | convolution fusion | flops 12684288 | bytes 268480 | tf_op jit(solution)/shard_map/dot_general | solution.py:177
  38.4 0.7 %reshape.6 = bf16[8,2,1536]{2,1,0:T(2,128)(2,1)} reshape(bf16[8,48,64]{2,1,0:T(8,128)(2,1)S(1)} %broadcast_in_dim.2) | data formatting | bytes 98304
  39.2 5.8 %all-to-all-start = ((bf16[8,2,1536]{2,1,0:T(2,128)(2,1)}), bf16[8,2,1536]{2,1,0:T(2,128)(2,1)S(1)}, u32[]{:S(2)}, u32[]{:S(2)}) async-start(bf16[8,2,1536]{2,1,0:T(2,128)(2,1)} %reshape.6), calls=%async_computation | async-start | bytes 98304 | tf_op jit(solution)/shard_map/all_to_all | solution.py:180
  45.5 6.3 %all-to-all-done = bf16[8,2,1536]{2,1,0:T(2,128)(2,1)S(1)} async-done(((bf16[8,2,1536]{2,1,0:T(2,128)(2,1)}), bf16[8,2,1536]{2,1,0:T(2,128)(2,1)S(1)}, u32[]{:S(2)}, u32[]{:S(2)}) %all-to-all-start) | async-done | bytes 49184 | tf_op jit(solution)/shard_map/all_to_all | solution.py:180
  52.7 1.3 %collective-permute-start.4 = (bf16[48,64]{1,0:T(8,128)(2,1)S(1)}, bf16[48,64]{1,0:T(8,128)(2,1)S(1)}, u32[]{:S(2)}, u32[]{:S(2)}) collective-permute-start(bf16[48,64]{1,0:T(8,128)(2,1)S(1)} %reduce_sum.12), channel_id=1, source_target_pairs={{0,3},{1,2},{2,1},{3,0},{4,7},{5,6},{6,5},{7,4},{8,11},{9,10},{10,... | collective-permute-start | bytes 18440 | tf_op jit(solution)/shard_map/ppermute | solution.py:184
  53.9 2.0 %collective-permute-done.5 = bf16[48,64]{1,0:T(8,128)(2,1)S(1)} collective-permute-done((bf16[48,64]{1,0:T(8,128)(2,1)S(1)}, bf16[48,64]{1,0:T(8,128)(2,1)S(1)}, u32[]{:S(2)}, u32[]{:S(2)}) %collective-permute-start.5) | collective-permute-done | bytes 6176 | tf_op jit(solution)/shard_map/ppermute | solution.py:183
  56.6 6.2 %shard_map.72.q_ref = bf16[4,96,64]{2,1,0:T(8,128)(2,1)} custom-call(bf16[48,64]{1,0:T(8,128)(2,1)} %get-tuple-element.9.a0, bf16[48,64]{1,0:T(8,128)(2,1)} %get-tuple-element.7.a1, bf16[48,64]{1,0:T(8,128)(2,1)} %get-tuple-element.8.a2, bf16[48,64]{1,0:T(8,128)(2,1)} %get-tuple-element.6.a3), custom_call_target="tpu_custom_call" | custom-call | flops 1048576 | bytes 131072 | tf_op jit(solution)/shard_map/pallas_call | solution.py:188
  62.8 0.9 %copy-done.2 = bf16[64,2048]{1,0:T(8,128)(2,1)S(1)} copy-done((bf16[64,2048]{1,0:T(8,128)(2,1)S(1)}, bf16[64,2048]{1,0:T(8,128)(2,1)}, u32[]{:S(2)}) %copy-start.2) | copy-done | bytes 262168
  63.7 0.9 %copy-done.3 = bf16[4,96,64]{2,1,0:T(8,128)(2,1)S(1)} copy-done((bf16[4,96,64]{2,1,0:T(8,128)(2,1)S(1)}, bf16[4,96,64]{2,1,0:T(8,128)(2,1)}, u32[]{:S(2)}) %copy-start.3) | copy-done | bytes 49176
  64.6 1.8 %shard_map.73 = f32[48,2048]{1,0:T(8,128)} custom-call(s32[3]{0:T(128)S(1)} %pad_add_fusion.meta_ref, bf16[4,96,64]{2,1,0:T(8,128)(2,1)S(1)} %copy-done.3, bf16[64,2048]{1,0:T(8,128)(2,1)S(1)} %copy-done.2, bf16[64,2048]{1,0:T(8,128)(2,1)S(1)} %collective-permute-done.7.d1, bf16[64,2048]{1,0:T(8,128)(2,1)S(1)} %collective-permute-done.8.d2, ...), custom_call_target="tpu_custom_call" | custom-call | flops 100663296 | bytes 393216 | tf_op jit(solution)/shard_map/pallas_call | solution.py:79
  (29 shorter events, 3.4 us)
Async XLA Ops:
  0.6 14.5 %collective-permute-start = (bf16[64,2048]{1,0:T(8,128)(2,1)}, bf16[64,2048]{1,0:T(8,128)(2,1)S(1)}, u32[]{:S(2)}, u32[]{:S(2)}) collective-permute-start(bf16[64,2048]{1,0:T(8,128)(2,1)} %v_ref.1), channel_id=1, source_target_pairs={{0,4},{4,0},{8,12},{12,8},{16,20},{20,16},{24,28},{28,24},{1,5},{5... | collective-permute-start | bytes 786440 | tf_op jit(solution)/shard_map/ppermute | solution.py:94
  3.7 11.5 %collective-permute-start.1 = (bf16[64,2048]{1,0:T(8,128)(2,1)}, bf16[64,2048]{1,0:T(8,128)(2,1)S(1)}, u32[]{:S(2)}, u32[]{:S(2)}) collective-permute-start(bf16[64,2048]{1,0:T(8,128)(2,1)} %v_ref.1), channel_id=1, source_target_pairs={{4,8},{12,16},{20,24},{8,4},{16,12},{24,20},{5,9},{13,17},{21,25},... | collective-permute-start | bytes 786440 | tf_op jit(solution)/shard_map/ppermute | solution.py:94
  5.2 2.2 %copy-start = (bf16[16,8,128,128]{3,2,1,0:T(8,128)(2,1)S(1)}, bf16[16,8,128,128]{3,2,1,0:T(8,128)(2,1)}, u32[]{:S(2)}) copy-start(bf16[16,8,128,128]{3,2,1,0:T(8,128)(2,1)} %tiles_ref.7) | copy-start | bytes 12582916
  7.4 0.9 %copy-start.4 = (bf16[64,2048]{1,0:T(8,128)(2,1)S(1)}, bf16[64,2048]{1,0:T(8,128)(2,1)}, u32[]{:S(2)}) copy-start(bf16[64,2048]{1,0:T(8,128)(2,1)} %v_ref.1) | copy-start | bytes 786436
  8.3 0.7 copy-start.5
  9.0 14.2 %copy-start.7 = (s32[48]{0:T(128)S(1)}, s32[48]{0:T(128)}, u32[]{:S(2)}) copy-start(s32[48]{0:T(128)} %param.9) | copy-start | bytes 580
  9.0 14.2 %copy-start.6 = (s32[16]{0:T(128)S(1)}, s32[16]{0:T(128)}, u32[]{:S(2)}) copy-start(s32[16]{0:T(128)} %counts_ref.7) | copy-start | bytes 196
  17.3 10.0 %collective-permute-start.3 = (bf16[64,2048]{1,0:T(8,128)(2,1)S(1)}, bf16[64,2048]{1,0:T(8,128)(2,1)S(1)}, u32[]{:S(2)}, u32[]{:S(2)}) collective-permute-start(bf16[64,2048]{1,0:T(8,128)(2,1)S(1)} %shard_map.69.v_ref), channel_id=1, source_target_pairs={{4,8},{12,16},{20,24},{8,4},{16,12},{24,20},{5,9},{13,17},{21,25},... | collective-permute-start | bytes 786440 | tf_op jit(solution)/shard_map/ppermute | solution.py:94
  18.0 14.8 %collective-permute-start.2 = (bf16[64,2048]{1,0:T(8,128)(2,1)S(1)}, bf16[64,2048]{1,0:T(8,128)(2,1)S(1)}, u32[]{:S(2)}, u32[]{:S(2)}) collective-permute-start(bf16[64,2048]{1,0:T(8,128)(2,1)S(1)} %shard_map.69.v_ref), channel_id=1, source_target_pairs={{0,4},{4,0},{8,12},{12,8},{16,20},{20,16},{24,28},{28,24},{1,5},{5... | collective-permute-start | bytes 786440 | tf_op jit(solution)/shard_map/ppermute | solution.py:94
  23.2 2.2 %copy-start.1 = (bf16[16,8,128,128]{3,2,1,0:T(8,128)(2,1)S(1)}, bf16[16,8,128,128]{3,2,1,0:T(8,128)(2,1)}, u32[]{:S(2)}) copy-start(bf16[16,8,128,128]{3,2,1,0:T(8,128)(2,1)} %tiles_ref.7) | copy-start | bytes 12582916
  35.7 9.4 %collective-permute-start.8 = (bf16[64,2048]{1,0:T(8,128)(2,1)}, bf16[64,2048]{1,0:T(8,128)(2,1)S(1)}, u32[]{:S(2)}, u32[]{:S(2)}) collective-permute-start(bf16[64,2048]{1,0:T(8,128)(2,1)} %shard_map.71.d0), channel_id=1, source_target_pairs={{0,2},{1,3},{2,0},{3,1},{4,6},{5,7},{6,4},{7,5},{8,10},{9,11},{10,... | collective-permute-start | bytes 786440 | tf_op jit(solution)/shard_map/ppermute | solution.py:146
  39.2 12.6 %all-to-all-start = ((bf16[8,2,1536]{2,1,0:T(2,128)(2,1)}), bf16[8,2,1536]{2,1,0:T(2,128)(2,1)S(1)}, u32[]{:S(2)}, u32[]{:S(2)}) async-start(bf16[8,2,1536]{2,1,0:T(2,128)(2,1)} %reshape.6), calls=%async_computation | async-start | bytes 98304 | tf_op jit(solution)/shard_map/all_to_all | solution.py:180
  45.0 17.8 %collective-permute-start.7 = (bf16[64,2048]{1,0:T(8,128)(2,1)}, bf16[64,2048]{1,0:T(8,128)(2,1)S(1)}, u32[]{:S(2)}, u32[]{:S(2)}) collective-permute-start(bf16[64,2048]{1,0:T(8,128)(2,1)} %shard_map.71.d0), channel_id=1, source_target_pairs={{0,1},{1,0},{2,3},{3,2},{4,5},{5,4},{6,7},{7,6},{8,9},{9,8},{10,11... | collective-permute-start | bytes 786440 | tf_op jit(solution)/shard_map/ppermute | solution.py:145
  45.0 17.7 %collective-permute-start.9 = (bf16[64,2048]{1,0:T(8,128)(2,1)S(1)}, bf16[64,2048]{1,0:T(8,128)(2,1)S(1)}, u32[]{:S(2)}, u32[]{:S(2)}) collective-permute-start(bf16[64,2048]{1,0:T(8,128)(2,1)S(1)} %collective-permute-done.8.d2), channel_id=1, source_target_pairs={{0,1},{1,0},{2,3},{3,2},{4,5},{5,4},{6,7},{7,6},{8,9},{9,8},{10,11... | collective-permute-start | bytes 786440 | tf_op jit(solution)/shard_map/ppermute | solution.py:147
  52.0 1.9 %collective-permute-start.6 = (bf16[48,64]{1,0:T(8,128)(2,1)S(1)}, bf16[48,64]{1,0:T(8,128)(2,1)S(1)}, u32[]{:S(2)}, u32[]{:S(2)}) collective-permute-start(bf16[48,64]{1,0:T(8,128)(2,1)S(1)} %reduce_sum.12), channel_id=1, source_target_pairs={{0,1},{1,0},{2,3},{3,2},{4,5},{5,4},{6,7},{7,6},{8,9},{9,8},{10,11... | collective-permute-start | bytes 18440 | tf_op jit(solution)/shard_map/ppermute | solution.py:182
  52.1 3.9 %collective-permute-start.5 = (bf16[48,64]{1,0:T(8,128)(2,1)S(1)}, bf16[48,64]{1,0:T(8,128)(2,1)S(1)}, u32[]{:S(2)}, u32[]{:S(2)}) collective-permute-start(bf16[48,64]{1,0:T(8,128)(2,1)S(1)} %reduce_sum.12), channel_id=1, source_target_pairs={{0,2},{1,3},{2,0},{3,1},{4,6},{5,7},{6,4},{7,5},{8,10},{9,11},{10,... | collective-permute-start | bytes 18440 | tf_op jit(solution)/shard_map/ppermute | solution.py:183
  52.7 3.3 %collective-permute-start.4 = (bf16[48,64]{1,0:T(8,128)(2,1)S(1)}, bf16[48,64]{1,0:T(8,128)(2,1)S(1)}, u32[]{:S(2)}, u32[]{:S(2)}) collective-permute-start(bf16[48,64]{1,0:T(8,128)(2,1)S(1)} %reduce_sum.12), channel_id=1, source_target_pairs={{0,3},{1,2},{2,1},{3,0},{4,7},{5,6},{6,5},{7,4},{8,11},{9,10},{10,... | collective-permute-start | bytes 18440 | tf_op jit(solution)/shard_map/ppermute | solution.py:184
  62.8 1.0 %copy-start.2 = (bf16[64,2048]{1,0:T(8,128)(2,1)S(1)}, bf16[64,2048]{1,0:T(8,128)(2,1)}, u32[]{:S(2)}) copy-start(bf16[64,2048]{1,0:T(8,128)(2,1)} %shard_map.71.d0) | copy-start | bytes 786436
  63.7 0.9 %copy-start.3 = (bf16[4,96,64]{2,1,0:T(8,128)(2,1)S(1)}, bf16[4,96,64]{2,1,0:T(8,128)(2,1)}, u32[]{:S(2)}) copy-start(bf16[4,96,64]{2,1,0:T(8,128)(2,1)} %shard_map.72.q_ref) | copy-start | bytes 147460

commit v2 on v0

v2 whole, which is shorter than its diff:
```python
import functools
import jax
import jax.numpy as jnp
from jax import lax
from jax.experimental import pallas as pl
from jax.experimental.pallas import tpu as pltpu
from jax.sharding import PartitionSpec as P

F = 256
TILE = 128
NBT = 8
EPS = 1e-05
COLS, ARCH, COUNTS, META = range(4)

VMEM = pl.BlockSpec(memory_space=pltpu.VMEM)
SMEM = pl.BlockSpec(memory_space=pltpu.SMEM)
ANY = pl.BlockSpec(memory_space=pl.ANY)
HBM = pl.BlockSpec(memory_space=pltpu.HBM)


def dot_last(a, b):
    return lax.dot_general(a, b, (((1,), (1,)), ((), ())), preferred_element_type=jnp.float32)


def dot(a, b):
    return lax.dot_general(a, b, (((1,), (0,)), ((), ())), preferred_element_type=jnp.float32)


def lanes(block):
    return pl.ds(pl.multiple_of(block * TILE, TILE), TILE)


def wide_tile(tiles_ref, b, slots):
    return jnp.concatenate([tiles_ref[b, j] for j in slots], axis=1)


def halves(x):
    high = x.astype(jnp.bfloat16)
    return high, (x - high.astype(jnp.float32)).astype(jnp.bfloat16)


def column(row, narch):
    at = lax.broadcasted_iota(jnp.int32, (narch, narch), 0) == lax.broadcasted_iota(jnp.int32, (narch, narch), 1)
    return jnp.sum(jnp.where(at, row.astype(jnp.float32), 0.0), axis=1, keepdims=True).astype(jnp.int32)


def rows_kernel(info_ref, table_ref, tiles_ref, rows_ref, held_ref, sem):
    blocks = tiles_ref.shape[0]
    narch = rows_ref.shape[0]
    first_block, first_slot = info_ref[META, 0], 2 * info_ref[META, 2]
    copies = []
    for i in range(2):
        copies.append(pltpu.make_async_copy(tiles_ref.at[:, first_slot + i], held_ref.at[:, i], sem.at[i]))
        copies[-1].start()
    local = column(table_ref[ARCH:ARCH + 1, :narch], narch) - first_block * TILE
    at = lax.broadcasted_iota(jnp.int32, (narch, TILE), 1)
    hits = [(local - b * TILE) == at for b in range(blocks)]
    owner = lax.broadcasted_iota(jnp.int32, (narch, blocks), 1) == lax.div(local, TILE)
    owner = jnp.where(jnp.logical_and(owner, local >= 0), 1.0, 0.0).astype(jnp.bfloat16)
    cols = jnp.concatenate([table_ref[COLS:COLS + 1, j * blocks:(j + 1) * blocks] for j in range(NBT)], axis=0)
    steps = cols - first_block - lax.broadcasted_iota(jnp.int32, cols.shape, 1)
    steps = dot_last(owner, steps.astype(jnp.float32).astype(jnp.bfloat16))
    rows_ref[:, 2 * TILE:] = jnp.zeros((narch, TILE), jnp.bfloat16)
    rows_ref[:, 2 * TILE:2 * TILE + NBT] = steps.astype(jnp.bfloat16)
    for i in range(2):
        sel = [
            jnp.where(hit, jnp.where(first_slot + i < info_ref[COUNTS, b], 1.0, 0.0), 0.0).astype(jnp.bfloat16)
            for b, hit in enumerate(hits)
        ]
        copies[i].wait()
        tall = jnp.concatenate([held_ref[b, i] for b in range(blocks)], axis=0)
        row = dot(jnp.concatenate(sel, axis=1), tall)
        rows_ref[:, i * TILE:(i + 1) * TILE] = row.astype(jnp.bfloat16)


def step_block(info_ref, tiles_ref, own_ref, pair_ref, other_ref, b, with_degree):
    blocks = own_ref.shape[1] // TILE
    first_block, odd = info_ref[META, 0], info_ref[META, 1]
    parts, ones = [], []
    for j in range(NBT):
        local = info_ref[COLS, j * blocks + b] - first_block
        lower, upper = local < 0, local >= blocks
        at = lanes(jnp.where(lower, local + blocks, jnp.where(upper, local - blocks, local)))
        used = j < info_ref[COUNTS, b]
        x = own_ref[:, at]
        if j > 0:
            near = jnp.logical_or(jnp.logical_and(lower, odd == 1), jnp.logical_and(upper, odd == 0))
            beside = jnp.where(near, pair_ref[:, at], other_ref[:, at])
            x = beside if j < 3 else jnp.where(jnp.logical_or(lower, upper), beside, x)
        if j >= 3:
            x = jnp.where(used, x, jnp.zeros_like(x))
        parts.append(x)
        ones.append(jnp.full((16, TILE), jnp.where(used, 1.0, 0.0), jnp.float32).astype(jnp.bfloat16))
    lhs = jnp.concatenate(parts, axis=1)
    if with_degree:
        lhs = jnp.concatenate([lhs, jnp.concatenate(ones, axis=1)], axis=0)
    return dot_last(lhs, jnp.concatenate([tiles_ref[b, j] for j in range(NBT)], axis=1))


def first_kernel(info_ref, tiles_ref, own_ref, pair_ref, other_ref, out_ref, inv_ref):
    feats = own_ref.shape[0]
    for b in range(tiles_ref.shape[0]):
        out = step_block(info_ref, tiles_ref, own_ref, pair_ref, other_ref, b, True)
        inv = 1.0 / out[feats:feats + 8]
        inv_ref[b] = inv
        out_ref[:, b * TILE:(b + 1) * TILE] = (out[:feats] * inv[:1]).astype(jnp.bfloat16)


def second_kernel(begin, info_ref, tiles_ref, own_ref, pair_ref, other_ref, inv_ref, extra_ref, out_ref):
    for i in range(out_ref.shape[1] // TILE):
        b = begin + i
        out = step_block(info_ref, tiles_ref, own_ref, pair_ref, other_ref, b, False)
        out_ref[:, i * TILE:(i + 1) * TILE] = (out * inv_ref[b][:1]).astype(jnp.bfloat16)


def arch_kernel(info_ref, table_ref, r0, r1, r2, r3, v_ref, out_ref):
    blocks = v_ref.shape[1] // TILE
    narch = r0.shape[0]
    me = info_ref[META, 2]
    block = lax.div(column(table_ref[ARCH:ARCH + 1, :narch], narch), TILE) - info_ref[META, 0]
    offsets = r0[:, 2 * TILE:].astype(jnp.float32)
    lane = lax.broadcasted_iota(jnp.int32, offsets.shape, 1)
    rows, places = [], []
    for p, r in enumerate((r0, r1, r2, r3)):
        for i in range(2):
            rows.append(r[:, i * TILE:(i + 1) * TILE].astype(jnp.float32))
            here = jnp.where(lane == 2 * (me ^ p) + i, offsets, 0.0)
            places.append(jnp.sum(here, axis=1, keepdims=True).astype(jnp.int32) + block)
    degree = jnp.sum(sum(rows), axis=1, keepdims=True)
    inv = jnp.where(degree > 0.0, 1.0 / degree, 0.0)
    rows = [r * inv for r in rows]
    weights = []
    for b in range(blocks):
        w = jnp.zeros((narch, TILE), jnp.float32)
        for r, place in zip(rows, places):
            w = w + jnp.where(place == b, r, 0.0)
        weights.append(jnp.concatenate(halves(w), axis=0))
    both = dot_last(jnp.concatenate(weights, axis=1), v_ref[...])
    part = both[:narch] + both[narch:]
    half = narch // 2
    out_ref[...] = jnp.concatenate([part[:half], part[half:]], axis=1)


def splat(x, shape):
    return jnp.broadcast_to(x, shape)


def solve_kernel(info_ref, a_ref, b_ref, d0, d1, q_ref, copy_ref):
    total = (a_ref[...] + b_ref[...]).astype(jnp.bfloat16)
    feats, half = d0.shape
    n = total.shape[0] // 2
    copy_ref[:, :half] = d0[...]
    copy_ref[:, half:] = d1[...]
    part = n // 2
    pieces = [total[p * part:(p + 1) * part] for p in range(4)]
    pieces = [jnp.concatenate([p[:, :feats], p[:, feats:]], axis=0) for p in pieces]
    pieces = in_order(info_ref[META, 2], pieces)
    arch = jnp.concatenate(pieces, axis=1)
    shape = (n, TILE)
    row = lax.broadcasted_iota(jnp.int32, shape, 0)
    col = lax.broadcasted_iota(jnp.int32, shape, 1)
    aug = jnp.concatenate([dot_last(arch, arch), jnp.zeros((n, TILE - n), jnp.float32)], axis=1)
    aug = aug + jnp.where(row + n == col, 1.0, 0.0)
    scale = jnp.zeros(shape, jnp.float32)
    group = 4
    for start in range(0, n, group):
        columns = [splat(aug[:, start + m:start + m + 1], shape) for m in range(group)]
        for m in range(group):
            k = start + m
            pivot = splat(columns[m][k:k + 1], shape)
            scale = jnp.where(row == k, pivot, scale)
            factor = jnp.where(row > k, columns[m] * (1.0 / pivot), 0.0)
            for later in range(m + 1, group):
                columns[later] = columns[later] - factor * splat(columns[later][k:k + 1], shape)
            aug = aug - factor * splat(aug[k:k + 1], shape)
    inverse = aug[:, n:2 * n] / jnp.sqrt(scale[:, :n])
    high, low = halves(inverse)
    third = (inverse - high.astype(jnp.float32) - low.astype(jnp.float32)).astype(jnp.bfloat16)
    q = dot(jnp.concatenate([high, low, third], axis=0), arch)
    high, low = halves(q[:n] + q[n:2 * n] + q[2 * n:])
    q_ref[:n] = high
    q_ref[n:] = low


def in_order(me, pieces):
    for bit in (1, 2):
        flip = (me & bit) == bit
        pieces = [jnp.where(flip, pieces[i ^ bit], pieces[i]) for i in range(4)]
    return pieces


def finish_kernel(info_ref, q_ref, *refs):
    pieces, out_ref = refs[:-1], refs[-1]
    n = out_ref.shape[0]
    half = pieces[0].shape[1]
    me = info_ref[META, 2]
    step = 256
    for h in range(2):
        for c in range(0, half, step):
            d = jnp.concatenate(in_order(me, [d[:, c:c + step] for d in pieces[4 * h:4 * h + 4]]), axis=0)
            z = dot(q_ref[...], d)
            wide = d.astype(jnp.float32)
            sq = jnp.sum(wide * wide, axis=0, keepdims=True)
            at = h * half + c
            out_ref[:, at:at + step] = (z[:n] + z[n:]) * lax.rsqrt(sq / F + EPS)


def call(kernel, out_shape, kinds, args, flops, nbytes, scratch=(), limit=16):
    single = not isinstance(out_shape, (list, tuple))
    spec = {"s": SMEM, "v": VMEM, "a": ANY, "h": HBM}
    return pl.pallas_call(
        kernel,
        out_shape=out_shape,
        in_specs=[spec[k] for k in kinds],
        out_specs=VMEM if single else [VMEM] * len(out_shape),
        scratch_shapes=scratch,
        compiler_params=pltpu.CompilerParams(vmem_limit_bytes=limit << 20),
        cost_estimate=pl.CostEstimate(flops=flops, bytes_accessed=nbytes, transcendentals=0),
    )(*args)


def exchange(matrix):
    size = lax.axis_size("cells")
    pairs = [(i, i ^ 1) for i in range(size)]
    others = [(i, i + 1) for i in range(1, size - 1, 2)]
    others = others + [(j, i) for i, j in others]
    return lax.ppermute(matrix, "cells", pairs), lax.ppermute(matrix, "cells", others)


def flip_feat(x, bits):
    return lax.ppermute(x, "feat", [(i, i ^ bits) for i in range(lax.axis_size("feat"))])


def on_device(expression, tiles, tile_cols, tile_counts, archetypes):
    blocks = tiles.shape[0]
    feats, rows = expression.shape
    narch = archetypes.shape[0]
    size = lax.axis_size("cells")
    cell, feat = lax.axis_index("cells"), lax.axis_index("feat")
    shape = jax.ShapeDtypeStruct
    bf16, f32 = jnp.bfloat16, jnp.float32
    line = lambda x: jnp.pad(x.reshape(-1), (0, TILE - x.size))
    numbers = jnp.stack([cell * blocks, cell & 1, feat]).astype(jnp.int32)
    info = jnp.concatenate([line(tile_cols.T), line(archetypes), line(tile_counts), line(numbers)]).reshape(4, TILE)
    flops = 2 * feats * TILE * TILE * NBT * blocks
    nbytes = 2 * TILE * TILE * NBT * blocks
    half = rows // 2
    half_shape = shape((feats, half), bf16)

    pair, other = exchange(expression)
    arch_rows = call(rows_kernel, shape((narch, 3 * TILE), bf16), "svh", (info, info, tiles), 0, 0,
                     [pltpu.VMEM((blocks, 2, TILE, TILE), bf16), pltpu.SemaphoreType.DMA((2,))], 52)
    first, inv = call(first_kernel, [shape((feats, rows), bf16), shape((blocks, 8, TILE), f32)], "svvvv",
                      (info, tiles, expression, pair, other), flops, nbytes)

    row_pair, row_other = exchange(arch_rows)
    own_rows, _ = lax.optimization_barrier((arch_rows, pair))
    near_rows, _ = lax.optimization_barrier((own_rows + row_pair + row_other, first))
    r = [near_rows] + [flip_feat(near_rows, p) for p in (1, 2, 3)]
    pair, other = exchange(first)
    part = call(arch_kernel, shape((narch // 2, 2 * feats), f32), "svvvvvv", (info, info, *r, first), 0, 0)
    part = jnp.concatenate([part] + [flip_feat(part, p) for p in (1, 2, 3)], axis=0)
    step = (info, tiles, first, pair, other, inv, part)
    left = call(functools.partial(second_kernel, 0), half_shape, "svvvvva", step, flops * 16, 0)
    right = call(functools.partial(second_kernel, blocks // 2), half_shape, "svvvvva", step, flops // 2, nbytes // 2)

    pieces = []
    for d in (left, right):
        near, far = flip_feat(d, 1), flip_feat(d, 2)
        pieces += [d, near, far, flip_feat(far, 1)]
    sums = (part, jnp.zeros_like(part))
    for level in range((size - 1).bit_length()):
        total = sums[0] + sums[1] if level else part
        sums = (total, lax.ppermute(total, "cells", [(i, i ^ (1 << level)) for i in range(size)]))
    q, diffused = call(solve_kernel, [shape((2 * narch, 4 * feats), bf16), shape((feats, rows), bf16)], "svvvv",
                       (info, *sums, left, right), 1 << 24, 1 << 19)
    coords = call(finish_kernel, shape((narch, rows), f32), "sv" + "v" * 8, (info, q, *pieces),
                  4 * narch * F * rows, 4 * narch * rows)
    return diffused, coords


def solution(mesh):
    return jax.shard_map(
        on_device,
        mesh=mesh,
        in_specs=(
            P("feat", "cells"),
            P("cells", None, None, None),
            P("cells", None),
            P("cells"),
            P(),
        ),
        out_specs=(P("feat", "cells"), P(None, "cells")),
        check_vma=False,
    )
```

time: 148 us -> 60.1 us (0.41)
  blocking collectives: 46.9 us -> 0 us
  waiting for transfers between devices: 45.1 us -> 13.4 us
  starting transfers between devices: 12.4 us -> 28.8 us
  Pallas kernels: 0 us -> 14.3 us
  other arithmetic: 14.8 us -> 0.94 us
  between operations: 14.2 us -> 0.77 us
  matrix products: 11.5 us -> 0 us
    psum x2 -> x0, blocking collectives: 46.9 us -> none  [the longest x1 36.7 us: on_device(): arch_part = lax.psum(picked, 'cells')]
    psum x1 -> x0, waiting for transfers between devices: 30.1 us -> none  [on_device(): proj_sum, square_sum = lax.psum((proj, squares), 'feat')]
    ppermute x4 -> x21, starting transfers between devices: 12.4 us -> 28.8 us  [the longest x3 11.1 us: exchange(): lax.ppermute(matrix, 'cells', pairs)]
    pallas_call x0 -> x7, Pallas kernels: none -> 14.3 us  [call(): pl.pallas_call(kernel, out_shape=out_shape, in_specs=[spec[k] for k in ki...]
    another operation x5 -> x1, other arithmetic: 9.52 us -> 0.08 us  [on_device(): numbers = jnp.stack([cell * blocks, cell & 1, feat]).astype(jnp.int32)]
    dot_general x6 -> x0, matrix products: 9.24 us -> none  [the longest x2 7.61 us: diffuse(): jnp.einsum('fbjc,bjrc->fbr', picked, tiles, preferred_element_type=jnp.fl...]
    reduce_sum x1 -> x0, other arithmetic: 3.41 us -> none  [on_device(): jnp.einsum('bjrc,bj->br', tiles, kept_mask, preferred_element_type=jnp.fl...]
    another operation x1 -> x0, matrix products: 2.26 us -> none  [finish_rows(): lax.linalg.triangular_solve(lower, proj, left_side=True, lower=True)]
  transfers between devices with their start and end apart: 5 -> 21, of which waited for: 4 -> 8; matrix products, arithmetic and copies ran while one was open for 4% -> 3% of each run, Pallas kernels for 0% -> 18%
where the time goes in v2:
time: 60.1 us; the launch traced here: 59.9 us
  starting transfers between devices  28.8 us (48%)
  Pallas kernels  14.3 us (24%)
  waiting for transfers between devices  13.4 us (22%)
  local copies, waits for them, and re-layouts  1.72 us (3%)
  other arithmetic  0.94 us (2%)
  between operations  0.77 us (1%)
    pallas_call x7, Pallas kernels, call(): pl.pallas_call(kernel, out_shape=out_shape, in_specs=[spec[k] for k in ki...  14.3 us
    ppermute x3, starting transfers between devices, exchange(): lax.ppermute(matrix, 'cells', pairs)  11.1 us
    ppermute x3, starting transfers between devices, on_device(): lax.ppermute(total, 'cells', [(i, i ^ 1 << level) for i in range(size)])  8.75 us
    ppermute x12, starting transfers between devices, flip_feat(): lax.ppermute(x, 'feat', [(i, i ^ bits) for i in range(lax.axis_size('feat...  7 us
    ppermute x3, waiting for transfers between devices, on_device(): lax.ppermute(total, 'cells', [(i, i ^ 1 << level) for i in range(size)])  6.2 us
    ppermute x12, waiting for transfers between devices, flip_feat(): lax.ppermute(x, 'feat', [(i, i ^ bits) for i in range(lax.axis_size('feat...  5.68 us
    ppermute x3, starting transfers between devices, exchange(): lax.ppermute(matrix, 'cells', others)  1.99 us
    ppermute x3, waiting for transfers between devices, exchange(): lax.ppermute(matrix, 'cells', pairs)  1.49 us
  transfers between devices with their start and end apart: 21, of which 8 were waited for; matrix products, arithmetic and copies ran while one was open for 3% of the time, Pallas kernels for 18%

profile of v2, /device:TPU:0, one launch (start us, length us, event | category | flops | bytes accessed | tf_op | source)
XLA Modules:
  0.0 59.9 jit_solution(13799499385381956081)
XLA Ops:
  0.6 3.0 %collective-permute-start = (bf16[64,2048]{1,0:T(8,128)(2,1)}, bf16[64,2048]{1,0:T(8,128)(2,1)S(1)}, u32[]{:S(2)}, u32[]{:S(2)}) collective-permute-start(bf16[64,2048]{1,0:T(8,128)(2,1)} %own_ref.1), channel_id=1, source_target_pairs={{0,4},{4,0},{8,12},{12,8},{16,20},{20,16},{24,28},{28,24},{1,5},{5... | collective-permute-start | bytes 786440 | tf_op jit(solution)/shard_map/ppermute | solution.py:227
  6.0 2.2 %shard_map.68 = bf16[48,384]{1,0:T(8,128)(2,1)S(1)} custom-call(s32[4,128]{1,0:T(4,128)S(1)} %fusion.info_ref.table_ref, s32[4,128]{1,0:T(4,128)S(1)} %fusion.info_ref.table_ref, bf16[16,8,128,128]{3,2,1,0:T(8,128)(2,1)} %tiles_ref.7), custom_call_target="tpu_custom_call" | custom-call | tf_op jit(solution)/shard_map/pallas_call | solution.py:211
  8.9 5.6 %collective-permute-start.1 = (bf16[48,384]{1,0:T(8,128)(2,1)S(1)}, bf16[48,384]{1,0:T(8,128)(2,1)S(1)}, u32[]{:S(2)}, u32[]{:S(2)}) collective-permute-start(bf16[48,384]{1,0:T(8,128)(2,1)S(1)} %shard_map.68), channel_id=1, source_target_pairs={{0,4},{4,0},{8,12},{12,8},{16,20},{20,16},{24,28},{28,24},{1,5},{5... | collective-permute-start | bytes 110600 | tf_op jit(solution)/shard_map/ppermute | solution.py:227
  14.5 1.5 %collective-permute-done.pair_ref = bf16[64,2048]{1,0:T(8,128)(2,1)S(1)} collective-permute-done((bf16[64,2048]{1,0:T(8,128)(2,1)}, bf16[64,2048]{1,0:T(8,128)(2,1)S(1)}, u32[]{:S(2)}, u32[]{:S(2)}) %collective-permute-start) | collective-permute-done | bytes 262176 | tf_op jit(solution)/shard_map/ppermute | solution.py:227
  16.9 2.4 %shard_map.69 = (bf16[64,2048]{1,0:T(8,128)(2,1)S(1)}, f32[16,8,128]{2,1,0:T(8,128)S(1)}) custom-call(s32[4,128]{1,0:T(4,128)S(1)} %fusion.info_ref.table_ref, bf16[16,8,128,128]{3,2,1,0:T(8,128)(2,1)S(1)} %copy-done, bf16[64,2048]{1,0:T(8,128)(2,1)S(1)} %copy-done.1, bf16[64,2048]{1,0:T(8,128)(2,1)S(1)} %collective-permute-done.pair_ref, ...), custom_call_target="tpu_custom_call" | custom-call | flops 268435456 | bytes 4194304 | tf_op jit(solution)/shard_map/pallas_call | solution.py:211
  19.3 2.4 %collective-permute-start.13 = (bf16[64,2048]{1,0:T(8,128)(2,1)S(1)}, bf16[64,2048]{1,0:T(8,128)(2,1)S(1)}, u32[]{:S(2)}, u32[]{:S(2)}) collective-permute-start(bf16[64,2048]{1,0:T(8,128)(2,1)S(1)} %get-tuple-element.9.v_ref.own_ref), channel_id=1, source_target_pairs={{0,4},{4,0},{8,12},{12,8},{16,20},{20,16},{24,28},{28,24},{1,5},{5... | collective-permute-start | bytes 786440 | tf_op jit(solution)/shard_map/ppermute | solution.py:227
  22.5 1.6 %collective-permute-start.5 = (bf16[48,384]{1,0:T(8,128)(2,1)S(1)}, bf16[48,384]{1,0:T(8,128)(2,1)S(1)}, u32[]{:S(2)}, u32[]{:S(2)}) collective-permute-start(bf16[48,384]{1,0:T(8,128)(2,1)S(1)} %add_add_fusion.r0), channel_id=1, source_target_pairs={{0,2},{1,3},{2,0},{3,1},{4,6},{5,7},{6,4},{7,5},{8,10},{9,11},{10,... | collective-permute-start | bytes 110600 | tf_op jit(solution)/shard_map/ppermute | solution.py:231
  24.4 2.2 %collective-permute-done.5.r2 = bf16[48,384]{1,0:T(8,128)(2,1)S(1)} collective-permute-done((bf16[48,384]{1,0:T(8,128)(2,1)S(1)}, bf16[48,384]{1,0:T(8,128)(2,1)S(1)}, u32[]{:S(2)}, u32[]{:S(2)}) %collective-permute-start.5) | collective-permute-done | bytes 36896 | tf_op jit(solution)/shard_map/ppermute | solution.py:231
  27.5 1.2 %shard_map.70 = f32[24,128]{1,0:T(8,128)S(1)} custom-call(s32[4,128]{1,0:T(4,128)S(1)} %fusion.info_ref.table_ref, s32[4,128]{1,0:T(4,128)S(1)} %fusion.info_ref.table_ref, bf16[48,384]{1,0:T(8,128)(2,1)S(1)} %add_add_fusion.r0, bf16[48,384]{1,0:T(8,128)(2,1)S(1)} %collective-permute-done.4.r1, bf16[48,384]{1,0:T(8,128)(2,1)S(1)} %collective-permute-done.5.r2, ...), custom_call_target="tpu_custom_call" | custom-call | tf_op jit(solution)/shard_map/pallas_call | solution.py:211
  29.5 1.1 %collective-permute-start.8 = (f32[24,128]{1,0:T(8,128)S(1)}, f32[24,128]{1,0:T(8,128)S(1)}, u32[]{:S(2)}, u32[]{:S(2)}) collective-permute-start(f32[24,128]{1,0:T(8,128)S(1)} %shard_map.70), channel_id=1, source_target_pairs={{0,2},{1,3},{2,0},{3,1},{4,6},{5,7},{6,4},{7,5},{8,10},{9,11},{10,... | collective-permute-start | bytes 36872 | tf_op jit(solution)/shard_map/ppermute | solution.py:231
  30.6 1.3 %collective-permute-done.9 = f32[24,128]{1,0:T(8,128)S(1)} collective-permute-done((f32[24,128]{1,0:T(8,128)S(1)}, f32[24,128]{1,0:T(8,128)S(1)}, u32[]{:S(2)}, u32[]{:S(2)}) %collective-permute-start.9) | collective-permute-done | bytes 12320 | tf_op jit(solution)/shard_map/ppermute | solution.py:231
  31.9 1.3 %collective-permute-done.8 = f32[24,128]{1,0:T(8,128)S(1)} collective-permute-done((f32[24,128]{1,0:T(8,128)S(1)}, f32[24,128]{1,0:T(8,128)S(1)}, u32[]{:S(2)}, u32[]{:S(2)}) %collective-permute-start.8) | collective-permute-done | bytes 12320 | tf_op jit(solution)/shard_map/ppermute | solution.py:231
  33.2 1.5 %shard_map.71.d0.refs_0_ = bf16[64,1024]{1,0:T(8,128)(2,1)S(1)} custom-call(s32[4,128]{1,0:T(4,128)S(1)} %fusion.info_ref.table_ref, bf16[16,8,128,128]{3,2,1,0:T(8,128)(2,1)S(1)} %copy-done, bf16[64,2048]{1,0:T(8,128)(2,1)S(1)} %get-tuple-element.9.v_ref.own_ref, bf16[64,2048]{1,0:T(8,128)(2,1)S(1)} %collective-permute-done.13.pair_ref, ...), custom_call_target="tpu_custom_call" | custom-call | flops 4294967296 | tf_op jit(solution)/shard_map/pallas_call | solution.py:211
  34.7 1.2 %collective-permute-start.16 = (bf16[64,1024]{1,0:T(8,128)(2,1)S(1)}, bf16[64,1024]{1,0:T(8,128)(2,1)S(1)}, u32[]{:S(2)}, u32[]{:S(2)}) collective-permute-start(bf16[64,1024]{1,0:T(8,128)(2,1)S(1)} %shard_map.71.d0.refs_0_), channel_id=1, source_target_pairs={{0,2},{1,3},{2,0},{3,1},{4,6},{5,7},{6,4},{7,5},{8,10},{9,11},{10,... | collective-permute-start | bytes 393224 | tf_op jit(solution)/shard_map/ppermute | solution.py:231
  35.9 1.5 %shard_map.72.d1.refs_4_ = bf16[64,1024]{1,0:T(8,128)(2,1)S(1)} custom-call(s32[4,128]{1,0:T(4,128)S(1)} %fusion.info_ref.table_ref, bf16[16,8,128,128]{3,2,1,0:T(8,128)(2,1)S(1)} %copy-done, bf16[64,2048]{1,0:T(8,128)(2,1)S(1)} %get-tuple-element.9.v_ref.own_ref, bf16[64,2048]{1,0:T(8,128)(2,1)S(1)} %collective-permute-done.13.pair_ref, ...), custom_call_target="tpu_custom_call" | custom-call | flops 134217728 | bytes 2097152 | tf_op jit(solution)/shard_map/pallas_call | solution.py:211
  37.4 1.0 %collective-permute-start.19 = (bf16[64,1024]{1,0:T(8,128)(2,1)S(1)}, bf16[64,1024]{1,0:T(8,128)(2,1)S(1)}, u32[]{:S(2)}, u32[]{:S(2)}) collective-permute-start(bf16[64,1024]{1,0:T(8,128)(2,1)S(1)} %shard_map.72.d1.refs_4_), channel_id=1, source_target_pairs={{0,2},{1,3},{2,0},{3,1},{4,6},{5,7},{6,4},{7,5},{8,10},{9,11},{10,... | collective-permute-start | bytes 393224 | tf_op jit(solution)/shard_map/ppermute | solution.py:231
  38.4 4.5 %collective-permute-start.10 = (f32[96,128]{1,0:T(8,128)S(1)}, f32[96,128]{1,0:T(8,128)S(1)}, u32[]{:S(2)}, u32[]{:S(2)}) collective-permute-start(f32[96,128]{1,0:T(8,128)S(1)} %pad_maximum_fusion.extra_ref), channel_id=1, source_target_pairs={{0,4},{4,0},{8,12},{12,8},{16,20},{20,16},{24,28},{28,24},{1,5},{5... | collective-permute-start | bytes 147464 | tf_op jit(solution)/shard_map/ppermute | solution.py:274
  44.0 1.0 %collective-permute-done.10 = f32[96,128]{1,0:T(8,128)S(1)} collective-permute-done((f32[96,128]{1,0:T(8,128)S(1)}, f32[96,128]{1,0:T(8,128)S(1)}, u32[]{:S(2)}, u32[]{:S(2)}) %collective-permute-start.10) | collective-permute-done | bytes 49184 | tf_op jit(solution)/shard_map/ppermute | solution.py:274
  45.0 1.6 %collective-permute-start.11 = (f32[96,128]{1,0:T(8,128)S(1)}, f32[96,128]{1,0:T(8,128)S(1)}, u32[]{:S(2)}, u32[]{:S(2)}) collective-permute-start(f32[96,128]{1,0:T(8,128)S(1)} %fusion.1), channel_id=1, source_target_pairs={{0,8},{4,12},{8,0},{12,4},{16,24},{20,28},{24,16},{28,20},{1,9},{5... | collective-permute-start | bytes 147464 | tf_op jit(solution)/shard_map/ppermute | solution.py:274
  46.7 2.5 %collective-permute-done.11 = f32[96,128]{1,0:T(8,128)S(1)} collective-permute-done((f32[96,128]{1,0:T(8,128)S(1)}, f32[96,128]{1,0:T(8,128)S(1)}, u32[]{:S(2)}, u32[]{:S(2)}) %collective-permute-start.11) | collective-permute-done | bytes 49184 | tf_op jit(solution)/shard_map/ppermute | solution.py:274
  49.2 2.6 %collective-permute-start.12 = (f32[96,128]{1,0:T(8,128)S(1)}, f32[96,128]{1,0:T(8,128)S(1)}, u32[]{:S(2)}, u32[]{:S(2)}) collective-permute-start(f32[96,128]{1,0:T(8,128)S(1)} %add.21.a_ref), channel_id=1, source_target_pairs={{0,16},{4,20},{8,24},{12,28},{16,0},{20,4},{24,8},{28,12},{1,17},{... | collective-permute-start | bytes 147464 | tf_op jit(solution)/shard_map/ppermute | solution.py:274
  51.8 2.6 %collective-permute-done.12.b_ref = f32[96,128]{1,0:T(8,128)S(1)} collective-permute-done((f32[96,128]{1,0:T(8,128)S(1)}, f32[96,128]{1,0:T(8,128)S(1)}, u32[]{:S(2)}, u32[]{:S(2)}) %collective-permute-start.12) | collective-permute-done | bytes 49184 | tf_op jit(solution)/shard_map/ppermute | solution.py:274
  54.4 3.6 %shard_map.73 = (bf16[96,256]{1,0:T(8,128)(2,1)S(1)}, bf16[64,2048]{1,0:T(8,128)(2,1)}) custom-call(s32[4,128]{1,0:T(4,128)S(1)} %fusion.info_ref.table_ref, f32[96,128]{1,0:T(8,128)S(1)} %add.21.a_ref, f32[96,128]{1,0:T(8,128)S(1)} %collective-permute-done.12.b_ref, bf16[64,1024]{1,0:T(8,128)(2,1)S(1)} %shard_map.71.d0.refs_0_, ...), custom_call_target="tpu_custom_call" | custom-call | flops 16777216 | bytes 524288 | tf_op jit(solution)/shard_map/pallas_call | solution.py:211
  58.0 1.8 %shard_map.74 = f32[48,2048]{1,0:T(8,128)} custom-call(s32[4,128]{1,0:T(4,128)S(1)} %fusion.info_ref.table_ref, bf16[96,256]{1,0:T(8,128)(2,1)S(1)} %get-tuple-element.13.q_ref, bf16[64,1024]{1,0:T(8,128)(2,1)S(1)} %shard_map.71.d0.refs_0_, bf16[64,1024]{1,0:T(8,128)(2,1)S(1)} %collective-permute-done.15.refs_1_, ...), custom_call_target="tpu_custom_call" | custom-call | flops 100663296 | bytes 393216 | tf_op jit(solution)/shard_map/pallas_call | solution.py:211
  (36 shorter events, 7.8 us)
Async XLA Ops:
  0.6 15.3 %collective-permute-start = (bf16[64,2048]{1,0:T(8,128)(2,1)}, bf16[64,2048]{1,0:T(8,128)(2,1)S(1)}, u32[]{:S(2)}, u32[]{:S(2)}) collective-permute-start(bf16[64,2048]{1,0:T(8,128)(2,1)} %own_ref.1), channel_id=1, source_target_pairs={{0,4},{4,0},{8,12},{12,8},{16,20},{20,16},{24,28},{28,24},{1,5},{5... | collective-permute-start | bytes 786440 | tf_op jit(solution)/shard_map/ppermute | solution.py:227
  3.7 12.3 %collective-permute-start.3 = (bf16[64,2048]{1,0:T(8,128)(2,1)}, bf16[64,2048]{1,0:T(8,128)(2,1)S(1)}, u32[]{:S(2)}, u32[]{:S(2)}) collective-permute-start(bf16[64,2048]{1,0:T(8,128)(2,1)} %own_ref.1), channel_id=1, source_target_pairs={{4,8},{12,16},{20,24},{8,4},{16,12},{24,20},{5,9},{13,17},{21,25},... | collective-permute-start | bytes 786440 | tf_op jit(solution)/shard_map/ppermute | solution.py:227
  5.1 10.8 %copy-start = (bf16[16,8,128,128]{3,2,1,0:T(8,128)(2,1)S(1)}, bf16[16,8,128,128]{3,2,1,0:T(8,128)(2,1)}, u32[]{:S(2)}) copy-start(bf16[16,8,128,128]{3,2,1,0:T(8,128)(2,1)} %tiles_ref.7) | copy-start | bytes 12582916
  8.2 14.2 %collective-permute-start.2 = (bf16[48,384]{1,0:T(8,128)(2,1)S(1)}, bf16[48,384]{1,0:T(8,128)(2,1)S(1)}, u32[]{:S(2)}, u32[]{:S(2)}) collective-permute-start(bf16[48,384]{1,0:T(8,128)(2,1)S(1)} %shard_map.68), channel_id=1, source_target_pairs={{4,8},{12,16},{20,24},{8,4},{16,12},{24,20},{5,9},{13,17},{21,25},... | collective-permute-start | bytes 110600 | tf_op jit(solution)/shard_map/ppermute | solution.py:227
  8.9 13.6 %collective-permute-start.1 = (bf16[48,384]{1,0:T(8,128)(2,1)S(1)}, bf16[48,384]{1,0:T(8,128)(2,1)S(1)}, u32[]{:S(2)}, u32[]{:S(2)}) collective-permute-start(bf16[48,384]{1,0:T(8,128)(2,1)S(1)} %shard_map.68), channel_id=1, source_target_pairs={{0,4},{4,0},{8,12},{12,8},{16,20},{20,16},{24,28},{28,24},{1,5},{5... | collective-permute-start | bytes 110600 | tf_op jit(solution)/shard_map/ppermute | solution.py:227
  16.0 1.0 %copy-start.1 = (bf16[64,2048]{1,0:T(8,128)(2,1)S(1)}, bf16[64,2048]{1,0:T(8,128)(2,1)}, u32[]{:S(2)}) copy-start(bf16[64,2048]{1,0:T(8,128)(2,1)} %own_ref.1) | copy-start | bytes 786436
  19.3 13.9 %collective-permute-start.13 = (bf16[64,2048]{1,0:T(8,128)(2,1)S(1)}, bf16[64,2048]{1,0:T(8,128)(2,1)S(1)}, u32[]{:S(2)}, u32[]{:S(2)}) collective-permute-start(bf16[64,2048]{1,0:T(8,128)(2,1)S(1)} %get-tuple-element.9.v_ref.own_ref), channel_id=1, source_target_pairs={{0,4},{4,0},{8,12},{12,8},{16,20},{20,16},{24,28},{28,24},{1,5},{5... | collective-permute-start | bytes 786440 | tf_op jit(solution)/shard_map/ppermute | solution.py:227
  21.7 11.5 %collective-permute-start.14 = (bf16[64,2048]{1,0:T(8,128)(2,1)S(1)}, bf16[64,2048]{1,0:T(8,128)(2,1)S(1)}, u32[]{:S(2)}, u32[]{:S(2)}) collective-permute-start(bf16[64,2048]{1,0:T(8,128)(2,1)S(1)} %get-tuple-element.9.v_ref.own_ref), channel_id=1, source_target_pairs={{4,8},{12,16},{20,24},{8,4},{16,12},{24,20},{5,9},{13,17},{21,25},... | collective-permute-start | bytes 786440 | tf_op jit(solution)/shard_map/ppermute | solution.py:227
  22.5 1.9 %collective-permute-start.4 = (bf16[48,384]{1,0:T(8,128)(2,1)S(1)}, bf16[48,384]{1,0:T(8,128)(2,1)S(1)}, u32[]{:S(2)}, u32[]{:S(2)}) collective-permute-start(bf16[48,384]{1,0:T(8,128)(2,1)S(1)} %add_add_fusion.r0), channel_id=1, source_target_pairs={{0,1},{1,0},{2,3},{3,2},{4,5},{5,4},{6,7},{7,6},{8,9},{9,8},{10,11... | collective-permute-start | bytes 110600 | tf_op jit(solution)/shard_map/ppermute | solution.py:231
  22.5 4.0 %collective-permute-start.5 = (bf16[48,384]{1,0:T(8,128)(2,1)S(1)}, bf16[48,384]{1,0:T(8,128)(2,1)S(1)}, u32[]{:S(2)}, u32[]{:S(2)}) collective-permute-start(bf16[48,384]{1,0:T(8,128)(2,1)S(1)} %add_add_fusion.r0), channel_id=1, source_target_pairs={{0,2},{1,3},{2,0},{3,1},{4,6},{5,7},{6,4},{7,5},{8,10},{9,11},{10,... | collective-permute-start | bytes 110600 | tf_op jit(solution)/shard_map/ppermute | solution.py:231
  24.1 3.4 %collective-permute-start.6 = (bf16[48,384]{1,0:T(8,128)(2,1)S(1)}, bf16[48,384]{1,0:T(8,128)(2,1)S(1)}, u32[]{:S(2)}, u32[]{:S(2)}) collective-permute-start(bf16[48,384]{1,0:T(8,128)(2,1)S(1)} %add_add_fusion.r0), channel_id=1, source_target_pairs={{0,3},{1,2},{2,1},{3,0},{4,7},{5,6},{6,5},{7,4},{8,11},{9,10},{10,... | collective-permute-start | bytes 110600 | tf_op jit(solution)/shard_map/ppermute | solution.py:231
  28.8 3.1 %collective-permute-start.9 = (f32[24,128]{1,0:T(8,128)S(1)}, f32[24,128]{1,0:T(8,128)S(1)}, u32[]{:S(2)}, u32[]{:S(2)}) collective-permute-start(f32[24,128]{1,0:T(8,128)S(1)} %shard_map.70), channel_id=1, source_target_pairs={{0,3},{1,2},{2,1},{3,0},{4,7},{5,6},{6,5},{7,4},{8,11},{9,10},{10,... | collective-permute-start | bytes 36872 | tf_op jit(solution)/shard_map/ppermute | solution.py:231
  29.5 3.7 %collective-permute-start.8 = (f32[24,128]{1,0:T(8,128)S(1)}, f32[24,128]{1,0:T(8,128)S(1)}, u32[]{:S(2)}, u32[]{:S(2)}) collective-permute-start(f32[24,128]{1,0:T(8,128)S(1)} %shard_map.70), channel_id=1, source_target_pairs={{0,2},{1,3},{2,0},{3,1},{4,6},{5,7},{6,4},{7,5},{8,10},{9,11},{10,... | collective-permute-start | bytes 36872 | tf_op jit(solution)/shard_map/ppermute | solution.py:231
  30.6 2.6 %collective-permute-start.7 = (f32[24,128]{1,0:T(8,128)S(1)}, f32[24,128]{1,0:T(8,128)S(1)}, u32[]{:S(2)}, u32[]{:S(2)}) collective-permute-start(f32[24,128]{1,0:T(8,128)S(1)} %shard_map.70), channel_id=1, source_target_pairs={{0,1},{1,0},{2,3},{3,2},{4,5},{5,4},{6,7},{7,6},{8,9},{9,8},{10,11... | collective-permute-start | bytes 36872 | tf_op jit(solution)/shard_map/ppermute | solution.py:231
  34.7 8.7 %collective-permute-start.16 = (bf16[64,1024]{1,0:T(8,128)(2,1)S(1)}, bf16[64,1024]{1,0:T(8,128)(2,1)S(1)}, u32[]{:S(2)}, u32[]{:S(2)}) collective-permute-start(bf16[64,1024]{1,0:T(8,128)(2,1)S(1)} %shard_map.71.d0.refs_0_), channel_id=1, source_target_pairs={{0,2},{1,3},{2,0},{3,1},{4,6},{5,7},{6,4},{7,5},{8,10},{9,11},{10,... | collective-permute-start | bytes 393224 | tf_op jit(solution)/shard_map/ppermute | solution.py:231
  37.4 6.1 %collective-permute-start.19 = (bf16[64,1024]{1,0:T(8,128)(2,1)S(1)}, bf16[64,1024]{1,0:T(8,128)(2,1)S(1)}, u32[]{:S(2)}, u32[]{:S(2)}) collective-permute-start(bf16[64,1024]{1,0:T(8,128)(2,1)S(1)} %shard_map.72.d1.refs_4_), channel_id=1, source_target_pairs={{0,2},{1,3},{2,0},{3,1},{4,6},{5,7},{6,4},{7,5},{8,10},{9,11},{10,... | collective-permute-start | bytes 393224 | tf_op jit(solution)/shard_map/ppermute | solution.py:231
  38.4 6.6 %collective-permute-start.10 = (f32[96,128]{1,0:T(8,128)S(1)}, f32[96,128]{1,0:T(8,128)S(1)}, u32[]{:S(2)}, u32[]{:S(2)}) collective-permute-start(f32[96,128]{1,0:T(8,128)S(1)} %pad_maximum_fusion.extra_ref), channel_id=1, source_target_pairs={{0,4},{4,0},{8,12},{12,8},{16,20},{20,16},{24,28},{28,24},{1,5},{5... | collective-permute-start | bytes 147464 | tf_op jit(solution)/shard_map/ppermute | solution.py:274
  43.0 15.1 %collective-permute-start.15 = (bf16[64,1024]{1,0:T(8,128)(2,1)S(1)}, bf16[64,1024]{1,0:T(8,128)(2,1)S(1)}, u32[]{:S(2)}, u32[]{:S(2)}) collective-permute-start(bf16[64,1024]{1,0:T(8,128)(2,1)S(1)} %shard_map.71.d0.refs_0_), channel_id=1, source_target_pairs={{0,1},{1,0},{2,3},{3,2},{4,5},{5,4},{6,7},{7,6},{8,9},{9,8},{10,11... | collective-permute-start | bytes 393224 | tf_op jit(solution)/shard_map/ppermute | solution.py:231
  43.0 15.1 %collective-permute-start.18 = (bf16[64,1024]{1,0:T(8,128)(2,1)S(1)}, bf16[64,1024]{1,0:T(8,128)(2,1)S(1)}, u32[]{:S(2)}, u32[]{:S(2)}) collective-permute-start(bf16[64,1024]{1,0:T(8,128)(2,1)S(1)} %shard_map.72.d1.refs_4_), channel_id=1, source_target_pairs={{0,1},{1,0},{2,3},{3,2},{4,5},{5,4},{6,7},{7,6},{8,9},{9,8},{10,11... | collective-permute-start | bytes 393224 | tf_op jit(solution)/shard_map/ppermute | solution.py:231
  43.5 14.5 %collective-permute-start.17 = (bf16[64,1024]{1,0:T(8,128)(2,1)S(1)}, bf16[64,1024]{1,0:T(8,128)(2,1)S(1)}, u32[]{:S(2)}, u32[]{:S(2)}) collective-permute-start(bf16[64,1024]{1,0:T(8,128)(2,1)S(1)} %collective-permute-done.16.refs_2_), channel_id=1, source_target_pairs={{0,1},{1,0},{2,3},{3,2},{4,5},{5,4},{6,7},{7,6},{8,9},{9,8},{10,11... | collective-permute-start | bytes 393224 | tf_op jit(solution)/shard_map/ppermute | solution.py:231
  43.5 14.5 %collective-permute-start.20 = (bf16[64,1024]{1,0:T(8,128)(2,1)S(1)}, bf16[64,1024]{1,0:T(8,128)(2,1)S(1)}, u32[]{:S(2)}, u32[]{:S(2)}) collective-permute-start(bf16[64,1024]{1,0:T(8,128)(2,1)S(1)} %collective-permute-done.19.refs_6_), channel_id=1, source_target_pairs={{0,1},{1,0},{2,3},{3,2},{4,5},{5,4},{6,7},{7,6},{8,9},{9,8},{10,11... | collective-permute-start | bytes 393224 | tf_op jit(solution)/shard_map/ppermute | solution.py:231
  45.0 4.1 %collective-permute-start.11 = (f32[96,128]{1,0:T(8,128)S(1)}, f32[96,128]{1,0:T(8,128)S(1)}, u32[]{:S(2)}, u32[]{:S(2)}) collective-permute-start(f32[96,128]{1,0:T(8,128)S(1)} %fusion.1), channel_id=1, source_target_pairs={{0,8},{4,12},{8,0},{12,4},{16,24},{20,28},{24,16},{28,20},{1,9},{5... | collective-permute-start | bytes 147464 | tf_op jit(solution)/shard_map/ppermute | solution.py:274
  49.2 5.2 %collective-permute-start.12 = (f32[96,128]{1,0:T(8,128)S(1)}, f32[96,128]{1,0:T(8,128)S(1)}, u32[]{:S(2)}, u32[]{:S(2)}) collective-permute-start(f32[96,128]{1,0:T(8,128)S(1)} %add.21.a_ref), channel_id=1, source_target_pairs={{0,16},{4,20},{8,24},{12,28},{16,0},{20,4},{24,8},{28,12},{1,17},{... | collective-permute-start | bytes 147464 | tf_op jit(solution)/shard_map/ppermute | solution.py:274

commit v3 on v2

--- a/solution.py
+++ b/solution.py
@@ -44,10 +44,12 @@
     return jnp.sum(jnp.where(at, row.astype(jnp.float32), 0.0), axis=1, keepdims=True).astype(jnp.int32)
 
 
-def rows_kernel(info_ref, table_ref, tiles_ref, rows_ref, held_ref, sem):
+def rows_kernel(info_ref, table_ref, tiles_ref, v_ref, rows_ref, own_ref, held_ref, sem):
     blocks = tiles_ref.shape[0]
     narch = rows_ref.shape[0]
     first_block, first_slot = info_ref[META, 0], 2 * info_ref[META, 2]
+    whole = pltpu.make_async_copy(v_ref, own_ref, sem.at[2])
+    whole.start()
     copies = []
     for i in range(2):
         copies.append(pltpu.make_async_copy(tiles_ref.at[:, first_slot + i], held_ref.at[:, i], sem.at[i]))
@@ -71,6 +73,7 @@
         tall = jnp.concatenate([held_ref[b, i] for b in range(blocks)], axis=0)
         row = dot(jnp.concatenate(sel, axis=1), tall)
         rows_ref[:, i * TILE:(i + 1) * TILE] = row.astype(jnp.bfloat16)
+    whole.wait()
 
 
 def step_block(info_ref, tiles_ref, own_ref, pair_ref, other_ref, b, with_degree):
@@ -145,8 +148,8 @@
     return jnp.broadcast_to(x, shape)
 
 
-def solve_kernel(info_ref, a_ref, b_ref, d0, d1, q_ref, copy_ref):
-    total = (a_ref[...] + b_ref[...]).astype(jnp.bfloat16)
+def solve_kernel(info_ref, total_ref, d0, d1, q_ref, copy_ref):
+    total = total_ref[...].astype(jnp.bfloat16)
     feats, half = d0.shape
     n = total.shape[0] // 2
     copy_ref[:, :half] = d0[...]
@@ -248,32 +251,43 @@
     half_shape = shape((feats, half), bf16)
 
     pair, other = exchange(expression)
-    arch_rows = call(rows_kernel, shape((narch, 3 * TILE), bf16), "svh", (info, info, tiles), 0, 0,
-                     [pltpu.VMEM((blocks, 2, TILE, TILE), bf16), pltpu.SemaphoreType.DMA((2,))], 52)
+    arch_rows, own = call(rows_kernel, [shape((narch, 3 * TILE), bf16), shape((feats, rows), bf16)], "svhh",
+                     (info, info, tiles, expression), 0, 0,
+                     [pltpu.VMEM((blocks, 2, TILE, TILE), bf16), pltpu.SemaphoreType.DMA((3,))], 52)
     first, inv = call(first_kernel, [shape((feats, rows), bf16), shape((blocks, 8, TILE), f32)], "svvvv",
-                      (info, tiles, expression, pair, other), flops, nbytes)
+                      (info, tiles, own, pair, other), flops, nbytes)
 
     row_pair, row_other = exchange(arch_rows)
     own_rows, _ = lax.optimization_barrier((arch_rows, pair))
     near_rows, _ = lax.optimization_barrier((own_rows + row_pair + row_other, first))
-    r = [near_rows] + [flip_feat(near_rows, p) for p in (1, 2, 3)]
+    r = [near_rows] + [flip_feat(near_rows[:, :2 * TILE], p) for p in (1, 2, 3)]
     pair, other = exchange(first)
     part = call(arch_kernel, shape((narch // 2, 2 * feats), f32), "svvvvvv", (info, info, *r, first), 0, 0)
+    partial = part
     part = jnp.concatenate([part] + [flip_feat(part, p) for p in (1, 2, 3)], axis=0)
-    step = (info, tiles, first, pair, other, inv, part)
-    left = call(functools.partial(second_kernel, 0), half_shape, "svvvvva", step, flops * 16, 0)
-    right = call(functools.partial(second_kernel, blocks // 2), half_shape, "svvvvva", step, flops // 2, nbytes // 2)
+    levels = (size - 1).bit_length()
+    flip_cells = lambda x, bits: lax.ppermute(x, "cells", [(i, i ^ bits) for i in range(size)])
+    level = levels % 2
+    summed = part
+    seen = flip_cells(part, 1) if level else None
+    step = (info, tiles, first, pair, other, inv)
+    left = call(functools.partial(second_kernel, 0), half_shape, "svvvvva", (*step, summed), flops * 16, 0)
+    if level:
+        seen, left = lax.optimization_barrier((seen, left))
+        part = part + seen
+    right = call(functools.partial(second_kernel, blocks // 2), half_shape, "svvvvva", (*step, part),
+                 flops // 2, nbytes // 2)
 
     pieces = []
     for d in (left, right):
         near, far = flip_feat(d, 1), flip_feat(d, 2)
         pieces += [d, near, far, flip_feat(far, 1)]
-    sums = (part, jnp.zeros_like(part))
-    for level in range((size - 1).bit_length()):
-        total = sums[0] + sums[1] if level else part
-        sums = (total, lax.ppermute(total, "cells", [(i, i ^ (1 << level)) for i in range(size)]))
-    q, diffused = call(solve_kernel, [shape((2 * narch, 4 * feats), bf16), shape((feats, rows), bf16)], "svvvv",
-                       (info, *sums, left, right), 1 << 24, 1 << 19)
+    while level < levels:
+        near, far, both = (flip_cells(part, b << level) for b in (1, 2, 3))
+        part = (part + near) + (far + both)
+        level += 2
+    q, diffused = call(solve_kernel, [shape((2 * narch, 4 * feats), bf16), shape((feats, rows), bf16)], "svvv",
+                       (info, part, left, right), 1 << 24, 1 << 19)
     coords = call(finish_kernel, shape((narch, rows), f32), "sv" + "v" * 8, (info, q, *pieces),
                   4 * narch * F * rows, 4 * narch * rows)
     return diffused, coords

time: 60.1 us -> 56.2 us (0.935)
  waiting for transfers between devices: 13.4 us -> 10.7 us
  starting transfers between devices: 28.8 us -> 27.4 us
    ppermute x3, waiting for transfers between devices: 1.49 us -> 0.01 us  [exchange(): lax.ppermute(matrix, 'cells', pairs)]
    ppermute x3 -> x4, waiting for transfers between devices: 6.2 us -> 5.1 us  [on_device(): lax.ppermute(x, 'cells', [(i, i ^ bits) for i in range(size)])]
    ppermute x3 -> x4, starting transfers between devices: 8.75 us -> 8.26 us  [on_device(): lax.ppermute(x, 'cells', [(i, i ^ bits) for i in range(size)])]
  transfers between devices with their start and end apart: 21 -> 22, of which waited for: 8 -> 7; matrix products, arithmetic and copies ran while one was open for 3% -> 3% of each run, Pallas kernels for 18% -> 22%
where the time goes in v3:
time: 56.2 us; the launch traced here: 56 us
  starting transfers between devices  27.4 us (49%)
  Pallas kernels  14.2 us (25%)
  waiting for transfers between devices  10.7 us (19%)
  local copies, waits for them, and re-layouts  1.93 us (3%)
  other arithmetic  0.95 us (2%)
  between operations  0.77 us (1%)
    pallas_call x7, Pallas kernels, call(): pl.pallas_call(kernel, out_shape=out_shape, in_specs=[spec[k] for k in ki...  14.2 us
    ppermute x3, starting transfers between devices, exchange(): lax.ppermute(matrix, 'cells', pairs)  10.7 us
    ppermute x4, starting transfers between devices, on_device(): lax.ppermute(x, 'cells', [(i, i ^ bits) for i in range(size)])  8.26 us
    ppermute x12, starting transfers between devices, flip_feat(): lax.ppermute(x, 'feat', [(i, i ^ bits) for i in range(lax.axis_size('feat...  6.5 us
    ppermute x12, waiting for transfers between devices, flip_feat(): lax.ppermute(x, 'feat', [(i, i ^ bits) for i in range(lax.axis_size('feat...  5.57 us
    ppermute x4, waiting for transfers between devices, on_device(): lax.ppermute(x, 'cells', [(i, i ^ bits) for i in range(size)])  5.1 us
    ppermute x3, starting transfers between devices, exchange(): lax.ppermute(matrix, 'cells', others)  1.99 us
    unnamed x4, local copies, waits for them, and re-layouts  1.16 us
  transfers between devices with their start and end apart: 22, of which 7 were waited for; matrix products, arithmetic and copies ran while one was open for 3% of the time, Pallas kernels for 22%

profile of v3, /device:TPU:0, one launch (start us, length us, event | category | flops | bytes accessed | tf_op | source)
XLA Modules:
  0.0 56.0 jit_solution(10120105555396320340)
XLA Ops:
  0.6 3.0 %collective-permute-start = (bf16[64,2048]{1,0:T(8,128)(2,1)}, bf16[64,2048]{1,0:T(8,128)(2,1)S(1)}, u32[]{:S(2)}, u32[]{:S(2)}) collective-permute-start(bf16[64,2048]{1,0:T(8,128)(2,1)} %v_ref.1), channel_id=1, source_target_pairs={{0,4},{4,0},{8,12},{12,8},{16,20},{20,16},{24,28},{28,24},{1,5},{5... | collective-permute-start | bytes 786440 | tf_op jit(solution)/shard_map/ppermute | solution.py:230
  6.0 1.2 %copy-done.1 = bf16[64,2048]{1,0:T(8,128)(2,1)S(1)} copy-done((bf16[64,2048]{1,0:T(8,128)(2,1)S(1)}, bf16[64,2048]{1,0:T(8,128)(2,1)}, u32[]{:S(2)}) %copy-start.1) | copy-done | bytes 262168
  7.2 2.1 %shard_map.68 = (bf16[48,384]{1,0:T(8,128)(2,1)S(1)}, bf16[64,2048]{1,0:T(8,128)(2,1)S(1)}) custom-call(s32[4,128]{1,0:T(4,128)S(1)} %fusion.info_ref.table_ref, s32[4,128]{1,0:T(4,128)S(1)} %fusion.info_ref.table_ref, bf16[16,8,128,128]{3,2,1,0:T(8,128)(2,1)} %tiles_ref.7, bf16[64,2048]{1,0:T(8,128)(2,1)S(1)} %copy-done.1), custom_call_target="tpu_custom_call" | custom-call | tf_op jit(solution)/shard_map/pallas_call | solution.py:214
  10.0 5.6 %collective-permute-start.1 = (bf16[48,384]{1,0:T(8,128)(2,1)S(1)}, bf16[48,384]{1,0:T(8,128)(2,1)S(1)}, u32[]{:S(2)}, u32[]{:S(2)}) collective-permute-start(bf16[48,384]{1,0:T(8,128)(2,1)S(1)} %get-tuple-element.13), channel_id=1, source_target_pairs={{0,4},{4,0},{8,12},{12,8},{16,20},{20,16},{24,28},{28,24},{1,5},{5... | collective-permute-start | bytes 110600 | tf_op jit(solution)/shard_map/ppermute | solution.py:230
  15.6 2.4 %shard_map.69 = (bf16[64,2048]{1,0:T(8,128)(2,1)S(1)}, f32[16,8,128]{2,1,0:T(8,128)S(1)}) custom-call(s32[4,128]{1,0:T(4,128)S(1)} %fusion.info_ref.table_ref, bf16[16,8,128,128]{3,2,1,0:T(8,128)(2,1)S(1)} %copy-done, bf16[64,2048]{1,0:T(8,128)(2,1)S(1)} %get-tuple-element.14.own_ref, bf16[64,2048]{1,0:T(8,128)(2,1)S(1)} %collective-permute-done.pair_ref, ...), custom_call_target="tpu_custom_call" | custom-call | flops 268435456 | bytes 4194304 | tf_op jit(solution)/shard_map/pallas_call | solution.py:214
  18.0 2.1 %collective-permute-start.11 = (bf16[64,2048]{1,0:T(8,128)(2,1)S(1)}, bf16[64,2048]{1,0:T(8,128)(2,1)S(1)}, u32[]{:S(2)}, u32[]{:S(2)}) collective-permute-start(bf16[64,2048]{1,0:T(8,128)(2,1)S(1)} %get-tuple-element.15.v_ref.own_ref), channel_id=1, source_target_pairs={{0,4},{4,0},{8,12},{12,8},{16,20},{20,16},{24,28},{28,24},{1,5},{5... | collective-permute-start | bytes 786440 | tf_op jit(solution)/shard_map/ppermute | solution.py:230
  20.8 1.5 %collective-permute-start.5 = (bf16[48,256]{1,0:T(8,128)(2,1)S(1)}, bf16[48,256]{1,0:T(8,128)(2,1)S(1)}, u32[]{:S(2)}, u32[]{:S(2)}) collective-permute-start(bf16[48,256]{1,0:T(8,128)(2,1)S(1)} %slice.2), channel_id=1, source_target_pairs={{0,2},{1,3},{2,0},{3,1},{4,6},{5,7},{6,4},{7,5},{8,10},{9,11},{10,... | collective-permute-start | bytes 73736 | tf_op jit(solution)/shard_map/ppermute | solution.py:234
  22.7 2.0 %collective-permute-done.5.r2 = bf16[48,256]{1,0:T(8,128)(2,1)S(1)} collective-permute-done((bf16[48,256]{1,0:T(8,128)(2,1)S(1)}, bf16[48,256]{1,0:T(8,128)(2,1)S(1)}, u32[]{:S(2)}, u32[]{:S(2)}) %collective-permute-start.5) | collective-permute-done | bytes 24608 | tf_op jit(solution)/shard_map/ppermute | solution.py:234
  24.7 0.9 %collective-permute-done.6.r3 = bf16[48,256]{1,0:T(8,128)(2,1)S(1)} collective-permute-done((bf16[48,256]{1,0:T(8,128)(2,1)S(1)}, bf16[48,256]{1,0:T(8,128)(2,1)S(1)}, u32[]{:S(2)}, u32[]{:S(2)}) %collective-permute-start.6) | collective-permute-done | bytes 24608 | tf_op jit(solution)/shard_map/ppermute | solution.py:234
  25.6 1.2 %shard_map.70 = f32[24,128]{1,0:T(8,128)S(1)} custom-call(s32[4,128]{1,0:T(4,128)S(1)} %fusion.info_ref.table_ref, s32[4,128]{1,0:T(4,128)S(1)} %fusion.info_ref.table_ref, bf16[48,384]{1,0:T(8,128)(2,1)S(1)} %add_add_fusion.1.r0, bf16[48,256]{1,0:T(8,128)(2,1)S(1)} %collective-permute-done.4.r1, bf16[48,256]{1,0:T(8,128)(2,1)S(1)} %collective-permute-done.5.r2, ...), custom_call_target="tpu_custom_call" | custom-call | tf_op jit(solution)/shard_map/pallas_call | solution.py:214
  26.8 0.8 %collective-permute-start.9 = (f32[24,128]{1,0:T(8,128)S(1)}, f32[24,128]{1,0:T(8,128)S(1)}, u32[]{:S(2)}, u32[]{:S(2)}) collective-permute-start(f32[24,128]{1,0:T(8,128)S(1)} %shard_map.70), channel_id=1, source_target_pairs={{0,3},{1,2},{2,1},{3,0},{4,7},{5,6},{6,5},{7,4},{8,11},{9,10},{10,... | collective-permute-start | bytes 36872 | tf_op jit(solution)/shard_map/ppermute | solution.py:234
  27.7 1.0 %collective-permute-start.8 = (f32[24,128]{1,0:T(8,128)S(1)}, f32[24,128]{1,0:T(8,128)S(1)}, u32[]{:S(2)}, u32[]{:S(2)}) collective-permute-start(f32[24,128]{1,0:T(8,128)S(1)} %shard_map.70), channel_id=1, source_target_pairs={{0,2},{1,3},{2,0},{3,1},{4,6},{5,7},{6,4},{7,5},{8,10},{9,11},{10,... | collective-permute-start | bytes 36872 | tf_op jit(solution)/shard_map/ppermute | solution.py:234
  28.7 1.3 %collective-permute-done.9 = f32[24,128]{1,0:T(8,128)S(1)} collective-permute-done((f32[24,128]{1,0:T(8,128)S(1)}, f32[24,128]{1,0:T(8,128)S(1)}, u32[]{:S(2)}, u32[]{:S(2)}) %collective-permute-start.9) | collective-permute-done | bytes 12320 | tf_op jit(solution)/shard_map/ppermute | solution.py:234
  30.0 1.4 %collective-permute-done.8 = f32[24,128]{1,0:T(8,128)S(1)} collective-permute-done((f32[24,128]{1,0:T(8,128)S(1)}, f32[24,128]{1,0:T(8,128)S(1)}, u32[]{:S(2)}, u32[]{:S(2)}) %collective-permute-start.8) | collective-permute-done | bytes 12320 | tf_op jit(solution)/shard_map/ppermute | solution.py:234
  31.4 4.3 %collective-permute-start.10 = (f32[96,128]{1,0:T(8,128)S(1)}, f32[96,128]{1,0:T(8,128)S(1)}, u32[]{:S(2)}, u32[]{:S(2)}) collective-permute-start(f32[96,128]{1,0:T(8,128)S(1)} %pad_maximum_fusion.extra_ref), channel_id=1, source_target_pairs={{0,4},{4,0},{8,12},{12,8},{16,20},{20,16},{24,28},{28,24},{1,5},{5... | collective-permute-start | bytes 147464 | tf_op jit(solution)/shard_map/ppermute | solution.py:269
  35.7 1.5 %shard_map.71.d0.refs_0_ = bf16[64,1024]{1,0:T(8,128)(2,1)S(1)} custom-call(s32[4,128]{1,0:T(4,128)S(1)} %fusion.info_ref.table_ref, bf16[16,8,128,128]{3,2,1,0:T(8,128)(2,1)S(1)} %copy-done, bf16[64,2048]{1,0:T(8,128)(2,1)S(1)} %get-tuple-element.15.v_ref.own_ref, bf16[64,2048]{1,0:T(8,128)(2,1)S(1)} %collective-permute-done.11.pair_ref, ...), custom_call_target="tpu_custom_call" | custom-call | flops 4294967296 | tf_op jit(solution)/shard_map/pallas_call | solution.py:214
  37.8 1.3 %collective-permute-start.17 = (bf16[64,1024]{1,0:T(8,128)(2,1)S(1)}, bf16[64,1024]{1,0:T(8,128)(2,1)S(1)}, u32[]{:S(2)}, u32[]{:S(2)}) collective-permute-start(bf16[64,1024]{1,0:T(8,128)(2,1)S(1)} %shard_map.71.d0.refs_0_), channel_id=1, source_target_pairs={{0,2},{1,3},{2,0},{3,1},{4,6},{5,7},{6,4},{7,5},{8,10},{9,11},{10,... | collective-permute-start | bytes 393224 | tf_op jit(solution)/shard_map/ppermute | solution.py:234
  39.1 1.5 %shard_map.72.d1.refs_4_ = bf16[64,1024]{1,0:T(8,128)(2,1)S(1)} custom-call(s32[4,128]{1,0:T(4,128)S(1)} %fusion.info_ref.table_ref, bf16[16,8,128,128]{3,2,1,0:T(8,128)(2,1)S(1)} %copy-done, bf16[64,2048]{1,0:T(8,128)(2,1)S(1)} %get-tuple-element.15.v_ref.own_ref, bf16[64,2048]{1,0:T(8,128)(2,1)S(1)} %collective-permute-done.11.pair_ref, ...), custom_call_target="tpu_custom_call" | custom-call | flops 134217728 | bytes 2097152 | tf_op jit(solution)/shard_map/pallas_call | solution.py:214
  41.4 2.5 %collective-permute-start.14 = (f32[96,128]{1,0:T(8,128)S(1)}, f32[96,128]{1,0:T(8,128)S(1)}, u32[]{:S(2)}, u32[]{:S(2)}) collective-permute-start(f32[96,128]{1,0:T(8,128)S(1)} %fusion.1.extra_ref), channel_id=1, source_target_pairs={{0,16},{4,20},{8,24},{12,28},{16,0},{20,4},{24,8},{28,12},{1,17},{... | collective-permute-start | bytes 147464 | tf_op jit(solution)/shard_map/ppermute | solution.py:269
  43.9 1.4 %collective-permute-start.15 = (f32[96,128]{1,0:T(8,128)S(1)}, f32[96,128]{1,0:T(8,128)S(1)}, u32[]{:S(2)}, u32[]{:S(2)}) collective-permute-start(f32[96,128]{1,0:T(8,128)S(1)} %fusion.1.extra_ref), channel_id=1, source_target_pairs={{0,24},{4,28},{8,16},{12,20},{16,8},{20,12},{24,0},{28,4},{1,25},{... | collective-permute-start | bytes 147464 | tf_op jit(solution)/shard_map/ppermute | solution.py:269
  45.4 1.6 %collective-permute-done.14 = f32[96,128]{1,0:T(8,128)S(1)} collective-permute-done((f32[96,128]{1,0:T(8,128)S(1)}, f32[96,128]{1,0:T(8,128)S(1)}, u32[]{:S(2)}, u32[]{:S(2)}) %collective-permute-start.14) | collective-permute-done | bytes 49184 | tf_op jit(solution)/shard_map/ppermute | solution.py:269
  47.0 2.9 %collective-permute-done.15 = f32[96,128]{1,0:T(8,128)S(1)} collective-permute-done((f32[96,128]{1,0:T(8,128)S(1)}, f32[96,128]{1,0:T(8,128)S(1)}, u32[]{:S(2)}, u32[]{:S(2)}) %collective-permute-start.15) | collective-permute-done | bytes 49184 | tf_op jit(solution)/shard_map/ppermute | solution.py:269
  50.5 3.6 %shard_map.73 = (bf16[96,256]{1,0:T(8,128)(2,1)S(1)}, bf16[64,2048]{1,0:T(8,128)(2,1)}) custom-call(s32[4,128]{1,0:T(4,128)S(1)} %fusion.info_ref.table_ref, f32[96,128]{1,0:T(8,128)S(1)} %add_add_fusion.total_ref, bf16[64,1024]{1,0:T(8,128)(2,1)S(1)} %shard_map.71.d0.refs_0_, bf16[64,1024]{1,0:T(8,128)(2,1)S(1)} %shard_map.72.d1.refs_4_), custom_call_target="tpu_custom_call" | custom-call | flops 16777216 | bytes 524288 | tf_op jit(solution)/shard_map/pallas_call | solution.py:214
  54.1 1.8 %shard_map.74 = f32[48,2048]{1,0:T(8,128)} custom-call(s32[4,128]{1,0:T(4,128)S(1)} %fusion.info_ref.table_ref, bf16[96,256]{1,0:T(8,128)(2,1)S(1)} %get-tuple-element.21.q_ref, bf16[64,1024]{1,0:T(8,128)(2,1)S(1)} %shard_map.71.d0.refs_0_, bf16[64,1024]{1,0:T(8,128)(2,1)S(1)} %collective-permute-done.16.refs_1_, ...), custom_call_target="tpu_custom_call" | custom-call | flops 100663296 | bytes 393216 | tf_op jit(solution)/shard_map/pallas_call | solution.py:214
  (39 shorter events, 6.2 us)
Async XLA Ops:
  0.6 14.9 %collective-permute-start = (bf16[64,2048]{1,0:T(8,128)(2,1)}, bf16[64,2048]{1,0:T(8,128)(2,1)S(1)}, u32[]{:S(2)}, u32[]{:S(2)}) collective-permute-start(bf16[64,2048]{1,0:T(8,128)(2,1)} %v_ref.1), channel_id=1, source_target_pairs={{0,4},{4,0},{8,12},{12,8},{16,20},{20,16},{24,28},{28,24},{1,5},{5... | collective-permute-start | bytes 786440 | tf_op jit(solution)/shard_map/ppermute | solution.py:230
  3.7 11.9 %collective-permute-start.3 = (bf16[64,2048]{1,0:T(8,128)(2,1)}, bf16[64,2048]{1,0:T(8,128)(2,1)S(1)}, u32[]{:S(2)}, u32[]{:S(2)}) collective-permute-start(bf16[64,2048]{1,0:T(8,128)(2,1)} %v_ref.1), channel_id=1, source_target_pairs={{4,8},{12,16},{20,24},{8,4},{16,12},{24,20},{5,9},{13,17},{21,25},... | collective-permute-start | bytes 786440 | tf_op jit(solution)/shard_map/ppermute | solution.py:230
  5.1 10.5 %copy-start = (bf16[16,8,128,128]{3,2,1,0:T(8,128)(2,1)S(1)}, bf16[16,8,128,128]{3,2,1,0:T(8,128)(2,1)}, u32[]{:S(2)}) copy-start(bf16[16,8,128,128]{3,2,1,0:T(8,128)(2,1)} %tiles_ref.7) | copy-start | bytes 12582916
  6.0 1.2 %copy-start.1 = (bf16[64,2048]{1,0:T(8,128)(2,1)S(1)}, bf16[64,2048]{1,0:T(8,128)(2,1)}, u32[]{:S(2)}) copy-start(bf16[64,2048]{1,0:T(8,128)(2,1)} %v_ref.1) | copy-start | bytes 786436
  9.3 11.4 %collective-permute-start.2 = (bf16[48,384]{1,0:T(8,128)(2,1)S(1)}, bf16[48,384]{1,0:T(8,128)(2,1)S(1)}, u32[]{:S(2)}, u32[]{:S(2)}) collective-permute-start(bf16[48,384]{1,0:T(8,128)(2,1)S(1)} %get-tuple-element.13), channel_id=1, source_target_pairs={{4,8},{12,16},{20,24},{8,4},{16,12},{24,20},{5,9},{13,17},{21,25},... | collective-permute-start | bytes 110600 | tf_op jit(solution)/shard_map/ppermute | solution.py:230
  10.0 10.8 %collective-permute-start.1 = (bf16[48,384]{1,0:T(8,128)(2,1)S(1)}, bf16[48,384]{1,0:T(8,128)(2,1)S(1)}, u32[]{:S(2)}, u32[]{:S(2)}) collective-permute-start(bf16[48,384]{1,0:T(8,128)(2,1)S(1)} %get-tuple-element.13), channel_id=1, source_target_pairs={{0,4},{4,0},{8,12},{12,8},{16,20},{20,16},{24,28},{28,24},{1,5},{5... | collective-permute-start | bytes 110600 | tf_op jit(solution)/shard_map/ppermute | solution.py:230
  18.0 17.7 %collective-permute-start.11 = (bf16[64,2048]{1,0:T(8,128)(2,1)S(1)}, bf16[64,2048]{1,0:T(8,128)(2,1)S(1)}, u32[]{:S(2)}, u32[]{:S(2)}) collective-permute-start(bf16[64,2048]{1,0:T(8,128)(2,1)S(1)} %get-tuple-element.15.v_ref.own_ref), channel_id=1, source_target_pairs={{0,4},{4,0},{8,12},{12,8},{16,20},{20,16},{24,28},{28,24},{1,5},{5... | collective-permute-start | bytes 786440 | tf_op jit(solution)/shard_map/ppermute | solution.py:230
  20.0 15.7 %collective-permute-start.12 = (bf16[64,2048]{1,0:T(8,128)(2,1)S(1)}, bf16[64,2048]{1,0:T(8,128)(2,1)S(1)}, u32[]{:S(2)}, u32[]{:S(2)}) collective-permute-start(bf16[64,2048]{1,0:T(8,128)(2,1)S(1)} %get-tuple-element.15.v_ref.own_ref), channel_id=1, source_target_pairs={{4,8},{12,16},{20,24},{8,4},{16,12},{24,20},{5,9},{13,17},{21,25},... | collective-permute-start | bytes 786440 | tf_op jit(solution)/shard_map/ppermute | solution.py:230
  20.8 1.9 %collective-permute-start.4 = (bf16[48,256]{1,0:T(8,128)(2,1)S(1)}, bf16[48,256]{1,0:T(8,128)(2,1)S(1)}, u32[]{:S(2)}, u32[]{:S(2)}) collective-permute-start(bf16[48,256]{1,0:T(8,128)(2,1)S(1)} %slice.2), channel_id=1, source_target_pairs={{0,1},{1,0},{2,3},{3,2},{4,5},{5,4},{6,7},{7,6},{8,9},{9,8},{10,11... | collective-permute-start | bytes 73736 | tf_op jit(solution)/shard_map/ppermute | solution.py:234
  20.8 3.9 %collective-permute-start.5 = (bf16[48,256]{1,0:T(8,128)(2,1)S(1)}, bf16[48,256]{1,0:T(8,128)(2,1)S(1)}, u32[]{:S(2)}, u32[]{:S(2)}) collective-permute-start(bf16[48,256]{1,0:T(8,128)(2,1)S(1)} %slice.2), channel_id=1, source_target_pairs={{0,2},{1,3},{2,0},{3,1},{4,6},{5,7},{6,4},{7,5},{8,10},{9,11},{10,... | collective-permute-start | bytes 73736 | tf_op jit(solution)/shard_map/ppermute | solution.py:234
  22.4 3.3 %collective-permute-start.6 = (bf16[48,256]{1,0:T(8,128)(2,1)S(1)}, bf16[48,256]{1,0:T(8,128)(2,1)S(1)}, u32[]{:S(2)}, u32[]{:S(2)}) collective-permute-start(bf16[48,256]{1,0:T(8,128)(2,1)S(1)} %slice.2), channel_id=1, source_target_pairs={{0,3},{1,2},{2,1},{3,0},{4,7},{5,6},{6,5},{7,4},{8,11},{9,10},{10,... | collective-permute-start | bytes 73736 | tf_op jit(solution)/shard_map/ppermute | solution.py:234
  26.8 3.1 %collective-permute-start.9 = (f32[24,128]{1,0:T(8,128)S(1)}, f32[24,128]{1,0:T(8,128)S(1)}, u32[]{:S(2)}, u32[]{:S(2)}) collective-permute-start(f32[24,128]{1,0:T(8,128)S(1)} %shard_map.70), channel_id=1, source_target_pairs={{0,3},{1,2},{2,1},{3,0},{4,7},{5,6},{6,5},{7,4},{8,11},{9,10},{10,... | collective-permute-start | bytes 36872 | tf_op jit(solution)/shard_map/ppermute | solution.py:234
  27.7 3.7 %collective-permute-start.8 = (f32[24,128]{1,0:T(8,128)S(1)}, f32[24,128]{1,0:T(8,128)S(1)}, u32[]{:S(2)}, u32[]{:S(2)}) collective-permute-start(f32[24,128]{1,0:T(8,128)S(1)} %shard_map.70), channel_id=1, source_target_pairs={{0,2},{1,3},{2,0},{3,1},{4,6},{5,7},{6,4},{7,5},{8,10},{9,11},{10,... | collective-permute-start | bytes 36872 | tf_op jit(solution)/shard_map/ppermute | solution.py:234
  28.7 2.7 %collective-permute-start.7 = (f32[24,128]{1,0:T(8,128)S(1)}, f32[24,128]{1,0:T(8,128)S(1)}, u32[]{:S(2)}, u32[]{:S(2)}) collective-permute-start(f32[24,128]{1,0:T(8,128)S(1)} %shard_map.70), channel_id=1, source_target_pairs={{0,1},{1,0},{2,3},{3,2},{4,5},{5,4},{6,7},{7,6},{8,9},{9,8},{10,11... | collective-permute-start | bytes 36872 | tf_op jit(solution)/shard_map/ppermute | solution.py:234
  31.4 6.4 %collective-permute-start.10 = (f32[96,128]{1,0:T(8,128)S(1)}, f32[96,128]{1,0:T(8,128)S(1)}, u32[]{:S(2)}, u32[]{:S(2)}) collective-permute-start(f32[96,128]{1,0:T(8,128)S(1)} %pad_maximum_fusion.extra_ref), channel_id=1, source_target_pairs={{0,4},{4,0},{8,12},{12,8},{16,20},{20,16},{24,28},{28,24},{1,5},{5... | collective-permute-start | bytes 147464 | tf_op jit(solution)/shard_map/ppermute | solution.py:269
  37.8 12.1 %collective-permute-start.17 = (bf16[64,1024]{1,0:T(8,128)(2,1)S(1)}, bf16[64,1024]{1,0:T(8,128)(2,1)S(1)}, u32[]{:S(2)}, u32[]{:S(2)}) collective-permute-start(bf16[64,1024]{1,0:T(8,128)(2,1)S(1)} %shard_map.71.d0.refs_0_), channel_id=1, source_target_pairs={{0,2},{1,3},{2,0},{3,1},{4,6},{5,7},{6,4},{7,5},{8,10},{9,11},{10,... | collective-permute-start | bytes 393224 | tf_op jit(solution)/shard_map/ppermute | solution.py:234
  40.6 9.8 %collective-permute-start.20 = (bf16[64,1024]{1,0:T(8,128)(2,1)S(1)}, bf16[64,1024]{1,0:T(8,128)(2,1)S(1)}, u32[]{:S(2)}, u32[]{:S(2)}) collective-permute-start(bf16[64,1024]{1,0:T(8,128)(2,1)S(1)} %shard_map.72.d1.refs_4_), channel_id=1, source_target_pairs={{0,2},{1,3},{2,0},{3,1},{4,6},{5,7},{6,4},{7,5},{8,10},{9,11},{10,... | collective-permute-start | bytes 393224 | tf_op jit(solution)/shard_map/ppermute | solution.py:234
  41.4 5.6 %collective-permute-start.14 = (f32[96,128]{1,0:T(8,128)S(1)}, f32[96,128]{1,0:T(8,128)S(1)}, u32[]{:S(2)}, u32[]{:S(2)}) collective-permute-start(f32[96,128]{1,0:T(8,128)S(1)} %fusion.1.extra_ref), channel_id=1, source_target_pairs={{0,16},{4,20},{8,24},{12,28},{16,0},{20,4},{24,8},{28,12},{1,17},{... | collective-permute-start | bytes 147464 | tf_op jit(solution)/shard_map/ppermute | solution.py:269
  43.9 6.0 %collective-permute-start.15 = (f32[96,128]{1,0:T(8,128)S(1)}, f32[96,128]{1,0:T(8,128)S(1)}, u32[]{:S(2)}, u32[]{:S(2)}) collective-permute-start(f32[96,128]{1,0:T(8,128)S(1)} %fusion.1.extra_ref), channel_id=1, source_target_pairs={{0,24},{4,28},{8,16},{12,20},{16,8},{20,12},{24,0},{28,4},{1,25},{... | collective-permute-start | bytes 147464 | tf_op jit(solution)/shard_map/ppermute | solution.py:269
  45.3 5.2 %collective-permute-start.13 = (f32[96,128]{1,0:T(8,128)S(1)}, f32[96,128]{1,0:T(8,128)S(1)}, u32[]{:S(2)}, u32[]{:S(2)}) collective-permute-start(f32[96,128]{1,0:T(8,128)S(1)} %fusion.1.extra_ref), channel_id=1, source_target_pairs={{0,8},{4,12},{8,0},{12,4},{16,24},{20,28},{24,16},{28,20},{1,9},{5... | collective-permute-start | bytes 147464 | tf_op jit(solution)/shard_map/ppermute | solution.py:269
  47.0 7.1 %collective-permute-start.16 = (bf16[64,1024]{1,0:T(8,128)(2,1)S(1)}, bf16[64,1024]{1,0:T(8,128)(2,1)S(1)}, u32[]{:S(2)}, u32[]{:S(2)}) collective-permute-start(bf16[64,1024]{1,0:T(8,128)(2,1)S(1)} %shard_map.71.d0.refs_0_), channel_id=1, source_target_pairs={{0,1},{1,0},{2,3},{3,2},{4,5},{5,4},{6,7},{7,6},{8,9},{9,8},{10,11... | collective-permute-start | bytes 393224 | tf_op jit(solution)/shard_map/ppermute | solution.py:234
  49.9 4.2 %collective-permute-start.19 = (bf16[64,1024]{1,0:T(8,128)(2,1)S(1)}, bf16[64,1024]{1,0:T(8,128)(2,1)S(1)}, u32[]{:S(2)}, u32[]{:S(2)}) collective-permute-start(bf16[64,1024]{1,0:T(8,128)(2,1)S(1)} %shard_map.72.d1.refs_4_), channel_id=1, source_target_pairs={{0,1},{1,0},{2,3},{3,2},{4,5},{5,4},{6,7},{7,6},{8,9},{9,8},{10,11... | collective-permute-start | bytes 393224 | tf_op jit(solution)/shard_map/ppermute | solution.py:234
  49.9 4.2 %collective-permute-start.18 = (bf16[64,1024]{1,0:T(8,128)(2,1)S(1)}, bf16[64,1024]{1,0:T(8,128)(2,1)S(1)}, u32[]{:S(2)}, u32[]{:S(2)}) collective-permute-start(bf16[64,1024]{1,0:T(8,128)(2,1)S(1)} %collective-permute-done.17.refs_2_), channel_id=1, source_target_pairs={{0,1},{1,0},{2,3},{3,2},{4,5},{5,4},{6,7},{7,6},{8,9},{9,8},{10,11... | collective-permute-start | bytes 393224 | tf_op jit(solution)/shard_map/ppermute | solution.py:234
  50.4 3.7 %collective-permute-start.21 = (bf16[64,1024]{1,0:T(8,128)(2,1)S(1)}, bf16[64,1024]{1,0:T(8,128)(2,1)S(1)}, u32[]{:S(2)}, u32[]{:S(2)}) collective-permute-start(bf16[64,1024]{1,0:T(8,128)(2,1)S(1)} %collective-permute-done.20.refs_6_), channel_id=1, source_target_pairs={{0,1},{1,0},{2,3},{3,2},{4,5},{5,4},{6,7},{7,6},{8,9},{9,8},{10,11... | collective-permute-start | bytes 393224 | tf_op jit(solution)/shard_map/ppermute | solution.py:234

commit v4 on v3

--- a/solution.py
+++ b/solution.py
@@ -10,7 +10,7 @@
 TILE = 128
 NBT = 8
 EPS = 1e-05
-COLS, ARCH, COUNTS, META = range(4)
+ARCH, COUNTS, META = range(NBT, NBT + 3)
 
 VMEM = pl.BlockSpec(memory_space=pltpu.VMEM)
 SMEM = pl.BlockSpec(memory_space=pltpu.SMEM)
@@ -59,7 +59,7 @@
     hits = [(local - b * TILE) == at for b in range(blocks)]
     owner = lax.broadcasted_iota(jnp.int32, (narch, blocks), 1) == lax.div(local, TILE)
     owner = jnp.where(jnp.logical_and(owner, local >= 0), 1.0, 0.0).astype(jnp.bfloat16)
-    cols = jnp.concatenate([table_ref[COLS:COLS + 1, j * blocks:(j + 1) * blocks] for j in range(NBT)], axis=0)
+    cols = table_ref[:NBT, :blocks]
     steps = cols - first_block - lax.broadcasted_iota(jnp.int32, cols.shape, 1)
     steps = dot_last(owner, steps.astype(jnp.float32).astype(jnp.bfloat16))
     rows_ref[:, 2 * TILE:] = jnp.zeros((narch, TILE), jnp.bfloat16)
@@ -81,7 +81,7 @@
     first_block, odd = info_ref[META, 0], info_ref[META, 1]
     parts, ones = [], []
     for j in range(NBT):
-        local = info_ref[COLS, j * blocks + b] - first_block
+        local = info_ref[j, b] - first_block
         lower, upper = local < 0, local >= blocks
         at = lanes(jnp.where(lower, local + blocks, jnp.where(upper, local - blocks, local)))
         used = j < info_ref[COUNTS, b]
@@ -100,7 +100,7 @@
     return dot_last(lhs, jnp.concatenate([tiles_ref[b, j] for j in range(NBT)], axis=1))
 
 
-def first_kernel(info_ref, tiles_ref, own_ref, pair_ref, other_ref, out_ref, inv_ref):
+def first_kernel(info_ref, tiles_ref, own_ref, other_ref, pair_ref, out_ref, inv_ref):
     feats = own_ref.shape[0]
     for b in range(tiles_ref.shape[0]):
         out = step_block(info_ref, tiles_ref, own_ref, pair_ref, other_ref, b, True)
@@ -109,11 +109,10 @@
         out_ref[:, b * TILE:(b + 1) * TILE] = (out[:feats] * inv[:1]).astype(jnp.bfloat16)
 
 
-def second_kernel(begin, info_ref, tiles_ref, own_ref, pair_ref, other_ref, inv_ref, extra_ref, out_ref):
-    for i in range(out_ref.shape[1] // TILE):
-        b = begin + i
+def second_kernel(info_ref, tiles_ref, own_ref, other_ref, pair_ref, inv_ref, extra_ref, out_ref):
+    for b in range(tiles_ref.shape[0]):
         out = step_block(info_ref, tiles_ref, own_ref, pair_ref, other_ref, b, False)
-        out_ref[:, i * TILE:(i + 1) * TILE] = (out * inv_ref[b][:1]).astype(jnp.bfloat16)
+        out_ref[:, b * TILE:(b + 1) * TILE] = (out * inv_ref[b][:1]).astype(jnp.bfloat16)
 
 
 def arch_kernel(info_ref, table_ref, r0, r1, r2, r3, v_ref, out_ref):
@@ -148,12 +147,17 @@
     return jnp.broadcast_to(x, shape)
 
 
-def solve_kernel(info_ref, total_ref, d0, d1, q_ref, copy_ref):
+def solve_kernel(info_ref, total_ref, d0, d1, d2, d3, out_ref, copy_ref, whole_ref, scale_ref):
     total = total_ref[...].astype(jnp.bfloat16)
-    feats, half = d0.shape
+    feats, width = d0.shape
     n = total.shape[0] // 2
-    copy_ref[:, :half] = d0[...]
-    copy_ref[:, half:] = d1[...]
+    copy_ref[...] = d0[...]
+    step = 256
+    for c in range(0, width, step):
+        d = jnp.concatenate(in_order(info_ref[META, 2], [d[:, c:c + step] for d in (d0, d1, d2, d3)]), axis=0)
+        whole_ref[:, c:c + step] = d
+        wide = d.astype(jnp.float32)
+        scale_ref[:, c:c + step] = lax.rsqrt(jnp.sum(wide * wide, axis=0, keepdims=True) / F + EPS)
     part = n // 2
     pieces = [total[p * part:(p + 1) * part] for p in range(4)]
     pieces = [jnp.concatenate([p[:, :feats], p[:, feats:]], axis=0) for p in pieces]
@@ -164,25 +168,26 @@
     col = lax.broadcasted_iota(jnp.int32, shape, 1)
     aug = jnp.concatenate([dot_last(arch, arch), jnp.zeros((n, TILE - n), jnp.float32)], axis=1)
     aug = aug + jnp.where(row + n == col, 1.0, 0.0)
-    scale = jnp.zeros(shape, jnp.float32)
-    group = 4
+    diagonal = jnp.zeros(shape, jnp.float32)
+    group = 8
     for start in range(0, n, group):
         columns = [splat(aug[:, start + m:start + m + 1], shape) for m in range(group)]
         for m in range(group):
             k = start + m
             pivot = splat(columns[m][k:k + 1], shape)
-            scale = jnp.where(row == k, pivot, scale)
+            diagonal = jnp.where(row == k, pivot, diagonal)
             factor = jnp.where(row > k, columns[m] * (1.0 / pivot), 0.0)
             for later in range(m + 1, group):
                 columns[later] = columns[later] - factor * splat(columns[later][k:k + 1], shape)
             aug = aug - factor * splat(aug[k:k + 1], shape)
-    inverse = aug[:, n:2 * n] / jnp.sqrt(scale[:, :n])
+    inverse = aug[:, n:2 * n] / jnp.sqrt(diagonal[:, :n])
     high, low = halves(inverse)
     third = (inverse - high.astype(jnp.float32) - low.astype(jnp.float32)).astype(jnp.bfloat16)
     q = dot(jnp.concatenate([high, low, third], axis=0), arch)
-    high, low = halves(q[:n] + q[n:2 * n] + q[2 * n:])
-    q_ref[:n] = high
-    q_ref[n:] = low
+    q = jnp.concatenate(halves(q[:n] + q[n:2 * n] + q[2 * n:]), axis=0)
+    for c in range(0, width, step):
+        z = dot(q, whole_ref[:, c:c + step])
+        out_ref[:, c:c + step] = (z[:n] + z[n:]) * scale_ref[:, c:c + step]
 
 
 def in_order(me, pieces):
@@ -190,22 +195,6 @@
         flip = (me & bit) == bit
         pieces = [jnp.where(flip, pieces[i ^ bit], pieces[i]) for i in range(4)]
     return pieces
-
-
-def finish_kernel(info_ref, q_ref, *refs):
-    pieces, out_ref = refs[:-1], refs[-1]
-    n = out_ref.shape[0]
-    half = pieces[0].shape[1]
-    me = info_ref[META, 2]
-    step = 256
-    for h in range(2):
-        for c in range(0, half, step):
-            d = jnp.concatenate(in_order(me, [d[:, c:c + step] for d in pieces[4 * h:4 * h + 4]]), axis=0)
-            z = dot(q_ref[...], d)
-            wide = d.astype(jnp.float32)
-            sq = jnp.sum(wide * wide, axis=0, keepdims=True)
-            at = h * half + c
-            out_ref[:, at:at + step] = (z[:n] + z[n:]) * lax.rsqrt(sq / F + EPS)
 
 
 def call(kernel, out_shape, kinds, args, flops, nbytes, scratch=(), limit=16):
@@ -242,54 +231,45 @@
     cell, feat = lax.axis_index("cells"), lax.axis_index("feat")
     shape = jax.ShapeDtypeStruct
     bf16, f32 = jnp.bfloat16, jnp.float32
-    line = lambda x: jnp.pad(x.reshape(-1), (0, TILE - x.size))
+    line = lambda x: jnp.pad(x, ((0, 0), (0, TILE - x.shape[1])))
     numbers = jnp.stack([cell * blocks, cell & 1, feat]).astype(jnp.int32)
-    info = jnp.concatenate([line(tile_cols.T), line(archetypes), line(tile_counts), line(numbers)]).reshape(4, TILE)
+    info = jnp.concatenate([line(x) for x in (tile_cols.T, archetypes[None], tile_counts[None], numbers[None])], axis=0)
     flops = 2 * feats * TILE * TILE * NBT * blocks
     nbytes = 2 * TILE * TILE * NBT * blocks
-    half = rows // 2
-    half_shape = shape((feats, half), bf16)
 
     pair, other = exchange(expression)
     arch_rows, own = call(rows_kernel, [shape((narch, 3 * TILE), bf16), shape((feats, rows), bf16)], "svhh",
                      (info, info, tiles, expression), 0, 0,
                      [pltpu.VMEM((blocks, 2, TILE, TILE), bf16), pltpu.SemaphoreType.DMA((3,))], 52)
     first, inv = call(first_kernel, [shape((feats, rows), bf16), shape((blocks, 8, TILE), f32)], "svvvv",
-                      (info, tiles, own, pair, other), flops, nbytes)
+                      (info, tiles, own, other, pair), flops, nbytes)
 
     row_pair, row_other = exchange(arch_rows)
-    own_rows, _ = lax.optimization_barrier((arch_rows, pair))
+    own_rows, _ = lax.optimization_barrier((arch_rows, other))
     near_rows, _ = lax.optimization_barrier((own_rows + row_pair + row_other, first))
     r = [near_rows] + [flip_feat(near_rows[:, :2 * TILE], p) for p in (1, 2, 3)]
     pair, other = exchange(first)
     part = call(arch_kernel, shape((narch // 2, 2 * feats), f32), "svvvvvv", (info, info, *r, first), 0, 0)
-    partial = part
-    part = jnp.concatenate([part] + [flip_feat(part, p) for p in (1, 2, 3)], axis=0)
+    step = (info, tiles, first, other, pair, inv)
+    diffused = call(second_kernel, shape((feats, rows), bf16), "svvvvva", (*step, part), flops * 16, 0)
+    seen, diffused = lax.optimization_barrier(([flip_feat(part, p) for p in (1, 2, 3)], diffused))
+    part = jnp.concatenate([part, *seen], axis=0)
+    flip_cells = lambda x, bits: lax.ppermute(x, "cells", [(i, i ^ bits) for i in range(size)])
     levels = (size - 1).bit_length()
-    flip_cells = lambda x, bits: lax.ppermute(x, "cells", [(i, i ^ bits) for i in range(size)])
     level = levels % 2
-    summed = part
-    seen = flip_cells(part, 1) if level else None
-    step = (info, tiles, first, pair, other, inv)
-    left = call(functools.partial(second_kernel, 0), half_shape, "svvvvva", (*step, summed), flops * 16, 0)
     if level:
-        seen, left = lax.optimization_barrier((seen, left))
-        part = part + seen
-    right = call(functools.partial(second_kernel, blocks // 2), half_shape, "svvvvva", (*step, part),
-                 flops // 2, nbytes // 2)
-
-    pieces = []
-    for d in (left, right):
-        near, far = flip_feat(d, 1), flip_feat(d, 2)
-        pieces += [d, near, far, flip_feat(far, 1)]
+        part = part + flip_cells(part, 1)
+
+    pieces = [diffused, flip_feat(diffused, 1), flip_feat(diffused, 2)]
+    pieces.append(flip_feat(pieces[2], 1))
     while level < levels:
         near, far, both = (flip_cells(part, b << level) for b in (1, 2, 3))
         part = (part + near) + (far + both)
         level += 2
-    q, diffused = call(solve_kernel, [shape((2 * narch, 4 * feats), bf16), shape((feats, rows), bf16)], "svvv",
-                       (info, part, left, right), 1 << 24, 1 << 19)
-    coords = call(finish_kernel, shape((narch, rows), f32), "sv" + "v" * 8, (info, q, *pieces),
-                  4 * narch * F * rows, 4 * narch * rows)
+    coords, diffused = call(
+        solve_kernel, [shape((narch, rows), f32), shape((feats, rows), bf16)], "svvvvv",
+        (info, part, *pieces), 4 * narch * F * rows, 4 * narch * rows,
+        [pltpu.VMEM((4 * feats, rows), bf16), pltpu.VMEM((1, rows), f32)])
     return diffused, coords
 
 

time: 56.2 us -> 50.5 us (0.90)
  Pallas kernels: 14.2 us -> 12 us
  starting transfers between devices: 27.4 us -> 25.8 us
  waiting for transfers between devices: 10.7 us -> 9.49 us
  local copies, waits for them, and re-layouts: 1.93 us -> 1.19 us
    ppermute x3, waiting for transfers between devices: 0.01 us -> 2.47 us  [exchange(): lax.ppermute(matrix, 'cells', pairs)]
    pallas_call x7 -> x5, Pallas kernels: 14.2 us -> 12 us  [call(): pl.pallas_call(kernel, out_shape=out_shape, in_specs=[spec[k] for k in ki...]
    ppermute x12 -> x9, waiting for transfers between devices: 5.57 us -> 3.62 us  [flip_feat(): lax.ppermute(x, 'feat', [(i, i ^ bits) for i in range(lax.axis_size('feat...]
    ppermute x4, waiting for transfers between devices: 5.1 us -> 3.39 us  [on_device(): lax.ppermute(x, 'cells', [(i, i ^ bits) for i in range(size)])]
    ppermute x12 -> x9, starting transfers between devices: 6.5 us -> 5.15 us  [flip_feat(): lax.ppermute(x, 'feat', [(i, i ^ bits) for i in range(lax.axis_size('feat...]
    concatenate x1 -> x2, other arithmetic: 0.01 us -> 0.89 us  [the longest x1 0.88 us: on_device(): jnp.concatenate([line(x) for x in (tile_cols.T, archetypes[None], tile_co...]
    reshape x1 -> x0, other arithmetic: 0.83 us -> none  [on_device(): jnp.concatenate([line(tile_cols.T), line(archetypes), line(tile_counts),...]
    reshape x1 -> x0, local copies, waits for them, and re-layouts: 0.77 us -> none  [on_device(): line = lambda x: jnp.pad(x.reshape(-1), (0, TILE - x.size))]
  transfers between devices with their start and end apart: 22 -> 19, of which waited for: 7 -> 8; matrix products, arithmetic and copies ran while one was open for 3% -> 2% of each run, Pallas kernels for 22% -> 17%
where the time goes in v4:
time: 50.5 us; the launch traced here: 50.3 us
  starting transfers between devices  25.8 us (51%)
  Pallas kernels  12 us (24%)
  waiting for transfers between devices  9.49 us (19%)
  local copies, waits for them, and re-layouts  1.19 us (2%)
  other arithmetic  1 us (2%)
  between operations  0.8 us (2%)
    pallas_call x5, Pallas kernels, call(): pl.pallas_call(kernel, out_shape=out_shape, in_specs=[spec[k] for k in ki...  12 us
    ppermute x3, starting transfers between devices, exchange(): lax.ppermute(matrix, 'cells', pairs)  11 us
    ppermute x4, starting transfers between devices, on_device(): lax.ppermute(x, 'cells', [(i, i ^ bits) for i in range(size)])  7.63 us
    ppermute x9, starting transfers between devices, flip_feat(): lax.ppermute(x, 'feat', [(i, i ^ bits) for i in range(lax.axis_size('feat...  5.15 us
    ppermute x9, waiting for transfers between devices, flip_feat(): lax.ppermute(x, 'feat', [(i, i ^ bits) for i in range(lax.axis_size('feat...  3.62 us
    ppermute x4, waiting for transfers between devices, on_device(): lax.ppermute(x, 'cells', [(i, i ^ bits) for i in range(size)])  3.39 us
    ppermute x3, waiting for transfers between devices, exchange(): lax.ppermute(matrix, 'cells', pairs)  2.47 us
    ppermute x3, starting transfers between devices, exchange(): lax.ppermute(matrix, 'cells', others)  1.99 us
  transfers between devices with their start and end apart: 19, of which 8 were waited for; matrix products, arithmetic and copies ran while one was open for 2% of the time, Pallas kernels for 17%

profile of v4, /device:TPU:0, one launch (start us, length us, event | category | flops | bytes accessed | tf_op | source)
XLA Modules:
  0.0 50.3 jit_solution(3708761758576372709)
XLA Ops:
  0.6 3.0 %collective-permute-start.3 = (bf16[64,2048]{1,0:T(8,128)(2,1)}, bf16[64,2048]{1,0:T(8,128)(2,1)S(1)}, u32[]{:S(2)}, u32[]{:S(2)}) collective-permute-start(bf16[64,2048]{1,0:T(8,128)(2,1)} %v_ref.1), channel_id=1, source_target_pairs={{0,4},{4,0},{8,12},{12,8},{16,20},{20,16},{24,28},{28,24},{1,5},{5... | collective-permute-start | bytes 786440 | tf_op jit(solution)/shard_map/ppermute | solution.py:219
  4.4 0.9 %pad_add_fusion.info_ref.table_ref = s32[11,128]{1,0:T(8,128)S(1)} fusion(s32[1,3]{1,0:T(1,128)S(1)} %add_bitcast_fusion, s32[1,16]{1,0:T(1,128)} %bitcast.9, s32[1,48]{1,0:T(1,128)} %bitcast.10, s32[8,16]{1,0:T(8,128)} %bitcast.8), kind=kLoop, calls=%fused_computation.3 | loop fusion | flops 4224 | bytes 6412 | tf_op jit(solution)/shard_map/concatenate | solution.py:236
  5.3 1.2 %copy-done.1 = bf16[64,2048]{1,0:T(8,128)(2,1)S(1)} copy-done((bf16[64,2048]{1,0:T(8,128)(2,1)S(1)}, bf16[64,2048]{1,0:T(8,128)(2,1)}, u32[]{:S(2)}) %copy-start.1) | copy-done | bytes 262168
  6.5 2.2 %shard_map.68 = (bf16[48,384]{1,0:T(8,128)(2,1)S(1)}, bf16[64,2048]{1,0:T(8,128)(2,1)S(1)}) custom-call(s32[11,128]{1,0:T(8,128)S(1)} %pad_add_fusion.info_ref.table_ref, s32[11,128]{1,0:T(8,128)S(1)} %pad_add_fusion.info_ref.table_ref, bf16[16,8,128,128]{3,2,1,0:T(8,128)(2,1)} %tiles_ref.5, bf16[64,2048]{1,0:T(8,128)(2,1)S(1)} %copy-done.1), custom_call_target="tpu_custom_call" | custom-call | tf_op jit(solution)/shard_map/pallas_call | solution.py:203
  9.4 5.6 %collective-permute-start.1 = (bf16[48,384]{1,0:T(8,128)(2,1)S(1)}, bf16[48,384]{1,0:T(8,128)(2,1)S(1)}, u32[]{:S(2)}, u32[]{:S(2)}) collective-permute-start(bf16[48,384]{1,0:T(8,128)(2,1)S(1)} %get-tuple-element.15), channel_id=1, source_target_pairs={{0,4},{4,0},{8,12},{12,8},{16,20},{20,16},{24,28},{28,24},{1,5},{5... | collective-permute-start | bytes 110600 | tf_op jit(solution)/shard_map/ppermute | solution.py:219
  15.0 1.0 %collective-permute-done.3.pair_ref = bf16[64,2048]{1,0:T(8,128)(2,1)S(1)} collective-permute-done((bf16[64,2048]{1,0:T(8,128)(2,1)}, bf16[64,2048]{1,0:T(8,128)(2,1)S(1)}, u32[]{:S(2)}, u32[]{:S(2)}) %collective-permute-start.3) | collective-permute-done | bytes 262176 | tf_op jit(solution)/shard_map/ppermute | solution.py:219
  16.0 2.5 %shard_map.69 = (bf16[64,2048]{1,0:T(8,128)(2,1)S(1)}, f32[16,8,128]{2,1,0:T(8,128)S(1)}) custom-call(s32[11,128]{1,0:T(8,128)S(1)} %pad_add_fusion.info_ref.table_ref, bf16[16,8,128,128]{3,2,1,0:T(8,128)(2,1)S(1)} %copy-done, bf16[64,2048]{1,0:T(8,128)(2,1)S(1)} %get-tuple-element.16.own_ref, bf16[64,2048]{1,0:T(8,128)(2,1)S(1)} %collective-permute-done.other_ref, ...), custom_call_target="tpu_custom_call" | custom-call | flops 268435456 | bytes 4194304 | tf_op jit(solution)/shard_map/pallas_call | solution.py:203
  18.5 2.4 %collective-permute-start.11 = (bf16[64,2048]{1,0:T(8,128)(2,1)S(1)}, bf16[64,2048]{1,0:T(8,128)(2,1)S(1)}, u32[]{:S(2)}, u32[]{:S(2)}) collective-permute-start(bf16[64,2048]{1,0:T(8,128)(2,1)S(1)} %get-tuple-element.17.v_ref.own_ref), channel_id=1, source_target_pairs={{0,4},{4,0},{8,12},{12,8},{16,20},{20,16},{24,28},{28,24},{1,5},{5... | collective-permute-start | bytes 786440 | tf_op jit(solution)/shard_map/ppermute | solution.py:219
  20.9 0.7 %collective-permute-start.10 = (bf16[64,2048]{1,0:T(8,128)(2,1)S(1)}, bf16[64,2048]{1,0:T(8,128)(2,1)S(1)}, u32[]{:S(2)}, u32[]{:S(2)}) collective-permute-start(bf16[64,2048]{1,0:T(8,128)(2,1)S(1)} %get-tuple-element.17.v_ref.own_ref), channel_id=1, source_target_pairs={{4,8},{12,16},{20,24},{8,4},{16,12},{24,20},{5,9},{13,17},{21,25},... | collective-permute-start | bytes 786440 | tf_op jit(solution)/shard_map/ppermute | solution.py:219
  21.7 1.6 %collective-permute-start.5 = (bf16[48,256]{1,0:T(8,128)(2,1)S(1)}, bf16[48,256]{1,0:T(8,128)(2,1)S(1)}, u32[]{:S(2)}, u32[]{:S(2)}) collective-permute-start(bf16[48,256]{1,0:T(8,128)(2,1)S(1)} %slice.2), channel_id=1, source_target_pairs={{0,2},{1,3},{2,0},{3,1},{4,6},{5,7},{6,4},{7,5},{8,10},{9,11},{10,... | collective-permute-start | bytes 73736 | tf_op jit(solution)/shard_map/ppermute | solution.py:223
  23.5 1.6 %collective-permute-done.6.r3 = bf16[48,256]{1,0:T(8,128)(2,1)S(1)} collective-permute-done((bf16[48,256]{1,0:T(8,128)(2,1)S(1)}, bf16[48,256]{1,0:T(8,128)(2,1)S(1)}, u32[]{:S(2)}, u32[]{:S(2)}) %collective-permute-start.6) | collective-permute-done | bytes 24608 | tf_op jit(solution)/shard_map/ppermute | solution.py:223
  25.6 1.3 %shard_map.70.extra_ref = f32[24,128]{1,0:T(8,128)S(1)} custom-call(s32[11,128]{1,0:T(8,128)S(1)} %pad_add_fusion.info_ref.table_ref, s32[11,128]{1,0:T(8,128)S(1)} %pad_add_fusion.info_ref.table_ref, bf16[48,384]{1,0:T(8,128)(2,1)S(1)} %add_add_fusion.1.r0, bf16[48,256]{1,0:T(8,128)(2,1)S(1)} %collective-permute-done.4.r1, ...), custom_call_target="tpu_custom_call" | custom-call | tf_op jit(solution)/shard_map/pallas_call | solution.py:203
  26.9 0.9 %collective-permute-start.9 = (f32[24,128]{1,0:T(8,128)S(1)}, f32[24,128]{1,0:T(8,128)S(1)}, u32[]{:S(2)}, u32[]{:S(2)}) collective-permute-start(f32[24,128]{1,0:T(8,128)S(1)} %shard_map.70.extra_ref), channel_id=1, source_target_pairs={{0,3},{1,2},{2,1},{3,0},{4,7},{5,6},{6,5},{7,4},{8,11},{9,10},{10,... | collective-permute-start | bytes 36872 | tf_op jit(solution)/shard_map/ppermute | solution.py:223
  27.8 1.2 %collective-permute-start.8 = (f32[24,128]{1,0:T(8,128)S(1)}, f32[24,128]{1,0:T(8,128)S(1)}, u32[]{:S(2)}, u32[]{:S(2)}) collective-permute-start(f32[24,128]{1,0:T(8,128)S(1)} %shard_map.70.extra_ref), channel_id=1, source_target_pairs={{0,2},{1,3},{2,0},{3,1},{4,6},{5,7},{6,4},{7,5},{8,10},{9,11},{10,... | collective-permute-start | bytes 36872 | tf_op jit(solution)/shard_map/ppermute | solution.py:223
  29.0 1.4 %collective-permute-done.11.pair_ref = bf16[64,2048]{1,0:T(8,128)(2,1)S(1)} collective-permute-done((bf16[64,2048]{1,0:T(8,128)(2,1)S(1)}, bf16[64,2048]{1,0:T(8,128)(2,1)S(1)}, u32[]{:S(2)}, u32[]{:S(2)}) %collective-permute-start.11) | collective-permute-done | bytes 262176 | tf_op jit(solution)/shard_map/ppermute | solution.py:219
  30.4 2.5 %shard_map.71.d0 = bf16[64,2048]{1,0:T(8,128)(2,1)S(1)} custom-call(s32[11,128]{1,0:T(8,128)S(1)} %pad_add_fusion.info_ref.table_ref, bf16[16,8,128,128]{3,2,1,0:T(8,128)(2,1)S(1)} %copy-done, bf16[64,2048]{1,0:T(8,128)(2,1)S(1)} %get-tuple-element.17.v_ref.own_ref, bf16[64,2048]{1,0:T(8,128)(2,1)S(1)} %collective-permute-done.10.other_ref, ...), custom_call_target="tpu_custom_call" | custom-call | flops 4294967296 | tf_op jit(solution)/shard_map/pallas_call | solution.py:203
  32.9 3.2 %collective-permute-start.12 = (f32[96,128]{1,0:T(8,128)S(1)}, f32[96,128]{1,0:T(8,128)S(1)}, u32[]{:S(2)}, u32[]{:S(2)}) collective-permute-start(f32[96,128]{1,0:T(8,128)S(1)} %pad_maximum_fusion), channel_id=1, source_target_pairs={{0,4},{4,0},{8,12},{12,8},{16,20},{20,16},{24,28},{28,24},{1,5},{5... | collective-permute-start | bytes 147464 | tf_op jit(solution)/shard_map/ppermute | solution.py:257
  36.1 1.2 %collective-permute-start.17 = (bf16[64,2048]{1,0:T(8,128)(2,1)S(1)}, bf16[64,2048]{1,0:T(8,128)(2,1)S(1)}, u32[]{:S(2)}, u32[]{:S(2)}) collective-permute-start(bf16[64,2048]{1,0:T(8,128)(2,1)S(1)} %shard_map.71.d0), channel_id=1, source_target_pairs={{0,2},{1,3},{2,0},{3,1},{4,6},{5,7},{6,4},{7,5},{8,10},{9,11},{10,... | collective-permute-start | bytes 786440 | tf_op jit(solution)/shard_map/ppermute | solution.py:223
  37.3 1.2 %collective-permute-done.12 = f32[96,128]{1,0:T(8,128)S(1)} collective-permute-done((f32[96,128]{1,0:T(8,128)S(1)}, f32[96,128]{1,0:T(8,128)S(1)}, u32[]{:S(2)}, u32[]{:S(2)}) %collective-permute-start.12) | collective-permute-done | bytes 49184 | tf_op jit(solution)/shard_map/ppermute | solution.py:257
  38.5 3.2 %collective-permute-start.15 = (f32[96,128]{1,0:T(8,128)S(1)}, f32[96,128]{1,0:T(8,128)S(1)}, u32[]{:S(2)}, u32[]{:S(2)}) collective-permute-start(f32[96,128]{1,0:T(8,128)S(1)} %fusion), channel_id=1, source_target_pairs={{0,24},{4,28},{8,16},{12,20},{16,8},{20,12},{24,0},{28,4},{1,25},{... | collective-permute-start | bytes 147464 | tf_op jit(solution)/shard_map/ppermute | solution.py:257
  41.7 1.3 %collective-permute-start.13 = (f32[96,128]{1,0:T(8,128)S(1)}, f32[96,128]{1,0:T(8,128)S(1)}, u32[]{:S(2)}, u32[]{:S(2)}) collective-permute-start(f32[96,128]{1,0:T(8,128)S(1)} %fusion), channel_id=1, source_target_pairs={{0,8},{4,12},{8,0},{12,4},{16,24},{20,28},{24,16},{28,20},{1,9},{5... | collective-permute-start | bytes 147464 | tf_op jit(solution)/shard_map/ppermute | solution.py:257
  43.0 1.6 %collective-permute-done.17.d2 = bf16[64,2048]{1,0:T(8,128)(2,1)S(1)} collective-permute-done((bf16[64,2048]{1,0:T(8,128)(2,1)S(1)}, bf16[64,2048]{1,0:T(8,128)(2,1)S(1)}, u32[]{:S(2)}, u32[]{:S(2)}) %collective-permute-start.17) | collective-permute-done | bytes 262176 | tf_op jit(solution)/shard_map/ppermute | solution.py:223
  44.7 2.0 %collective-permute-done.14 = f32[96,128]{1,0:T(8,128)S(1)} collective-permute-done((f32[96,128]{1,0:T(8,128)S(1)}, f32[96,128]{1,0:T(8,128)S(1)}, u32[]{:S(2)}, u32[]{:S(2)}) %collective-permute-start.14) | collective-permute-done | bytes 49184 | tf_op jit(solution)/shard_map/ppermute | solution.py:257
  46.8 3.5 %shard_map.72 = (f32[48,2048]{1,0:T(8,128)}, bf16[64,2048]{1,0:T(8,128)(2,1)}) custom-call(s32[11,128]{1,0:T(8,128)S(1)} %pad_add_fusion.info_ref.table_ref, f32[96,128]{1,0:T(8,128)S(1)} %add_add_fusion.total_ref, bf16[64,2048]{1,0:T(8,128)(2,1)S(1)} %shard_map.71.d0, bf16[64,2048]{1,0:T(8,128)(2,1)S(1)} %collective-permute-done.16.d1, ...), custom_call_target="tpu_custom_call" | custom-call | flops 100663296 | bytes 393216 | tf_op jit(solution)/shard_map/pallas_call | solution.py:203
  (30 shorter events, 2.4 us)
Async XLA Ops:
  0.6 15.4 %collective-permute-start.3 = (bf16[64,2048]{1,0:T(8,128)(2,1)}, bf16[64,2048]{1,0:T(8,128)(2,1)S(1)}, u32[]{:S(2)}, u32[]{:S(2)}) collective-permute-start(bf16[64,2048]{1,0:T(8,128)(2,1)} %v_ref.1), channel_id=1, source_target_pairs={{0,4},{4,0},{8,12},{12,8},{16,20},{20,16},{24,28},{28,24},{1,5},{5... | collective-permute-start | bytes 786440 | tf_op jit(solution)/shard_map/ppermute | solution.py:219
  3.7 12.3 %collective-permute-start = (bf16[64,2048]{1,0:T(8,128)(2,1)}, bf16[64,2048]{1,0:T(8,128)(2,1)S(1)}, u32[]{:S(2)}, u32[]{:S(2)}) collective-permute-start(bf16[64,2048]{1,0:T(8,128)(2,1)} %v_ref.1), channel_id=1, source_target_pairs={{4,8},{12,16},{20,24},{8,4},{16,12},{24,20},{5,9},{13,17},{21,25},... | collective-permute-start | bytes 786440 | tf_op jit(solution)/shard_map/ppermute | solution.py:219
  4.3 11.6 %copy-start = (bf16[16,8,128,128]{3,2,1,0:T(8,128)(2,1)S(1)}, bf16[16,8,128,128]{3,2,1,0:T(8,128)(2,1)}, u32[]{:S(2)}) copy-start(bf16[16,8,128,128]{3,2,1,0:T(8,128)(2,1)} %tiles_ref.5) | copy-start | bytes 12582916
  5.3 1.2 %copy-start.1 = (bf16[64,2048]{1,0:T(8,128)(2,1)S(1)}, bf16[64,2048]{1,0:T(8,128)(2,1)}, u32[]{:S(2)}) copy-start(bf16[64,2048]{1,0:T(8,128)(2,1)} %v_ref.1) | copy-start | bytes 786436
  8.7 12.9 %collective-permute-start.2 = (bf16[48,384]{1,0:T(8,128)(2,1)S(1)}, bf16[48,384]{1,0:T(8,128)(2,1)S(1)}, u32[]{:S(2)}, u32[]{:S(2)}) collective-permute-start(bf16[48,384]{1,0:T(8,128)(2,1)S(1)} %get-tuple-element.15), channel_id=1, source_target_pairs={{4,8},{12,16},{20,24},{8,4},{16,12},{24,20},{5,9},{13,17},{21,25},... | collective-permute-start | bytes 110600 | tf_op jit(solution)/shard_map/ppermute | solution.py:219
  9.4 12.2 %collective-permute-start.1 = (bf16[48,384]{1,0:T(8,128)(2,1)S(1)}, bf16[48,384]{1,0:T(8,128)(2,1)S(1)}, u32[]{:S(2)}, u32[]{:S(2)}) collective-permute-start(bf16[48,384]{1,0:T(8,128)(2,1)S(1)} %get-tuple-element.15), channel_id=1, source_target_pairs={{0,4},{4,0},{8,12},{12,8},{16,20},{20,16},{24,28},{28,24},{1,5},{5... | collective-permute-start | bytes 110600 | tf_op jit(solution)/shard_map/ppermute | solution.py:219
  18.5 11.9 %collective-permute-start.11 = (bf16[64,2048]{1,0:T(8,128)(2,1)S(1)}, bf16[64,2048]{1,0:T(8,128)(2,1)S(1)}, u32[]{:S(2)}, u32[]{:S(2)}) collective-permute-start(bf16[64,2048]{1,0:T(8,128)(2,1)S(1)} %get-tuple-element.17.v_ref.own_ref), channel_id=1, source_target_pairs={{0,4},{4,0},{8,12},{12,8},{16,20},{20,16},{24,28},{28,24},{1,5},{5... | collective-permute-start | bytes 786440 | tf_op jit(solution)/shard_map/ppermute | solution.py:219
  20.9 9.5 %collective-permute-start.10 = (bf16[64,2048]{1,0:T(8,128)(2,1)S(1)}, bf16[64,2048]{1,0:T(8,128)(2,1)S(1)}, u32[]{:S(2)}, u32[]{:S(2)}) collective-permute-start(bf16[64,2048]{1,0:T(8,128)(2,1)S(1)} %get-tuple-element.17.v_ref.own_ref), channel_id=1, source_target_pairs={{4,8},{12,16},{20,24},{8,4},{16,12},{24,20},{5,9},{13,17},{21,25},... | collective-permute-start | bytes 786440 | tf_op jit(solution)/shard_map/ppermute | solution.py:219
  21.6 3.5 %collective-permute-start.6 = (bf16[48,256]{1,0:T(8,128)(2,1)S(1)}, bf16[48,256]{1,0:T(8,128)(2,1)S(1)}, u32[]{:S(2)}, u32[]{:S(2)}) collective-permute-start(bf16[48,256]{1,0:T(8,128)(2,1)S(1)} %slice.2), channel_id=1, source_target_pairs={{0,3},{1,2},{2,1},{3,0},{4,7},{5,6},{6,5},{7,4},{8,11},{9,10},{10,... | collective-permute-start | bytes 73736 | tf_op jit(solution)/shard_map/ppermute | solution.py:223
  21.7 3.9 %collective-permute-start.5 = (bf16[48,256]{1,0:T(8,128)(2,1)S(1)}, bf16[48,256]{1,0:T(8,128)(2,1)S(1)}, u32[]{:S(2)}, u32[]{:S(2)}) collective-permute-start(bf16[48,256]{1,0:T(8,128)(2,1)S(1)} %slice.2), channel_id=1, source_target_pairs={{0,2},{1,3},{2,0},{3,1},{4,6},{5,7},{6,4},{7,5},{8,10},{9,11},{10,... | collective-permute-start | bytes 73736 | tf_op jit(solution)/shard_map/ppermute | solution.py:223
  23.3 2.3 %collective-permute-start.4 = (bf16[48,256]{1,0:T(8,128)(2,1)S(1)}, bf16[48,256]{1,0:T(8,128)(2,1)S(1)}, u32[]{:S(2)}, u32[]{:S(2)}) collective-permute-start(bf16[48,256]{1,0:T(8,128)(2,1)S(1)} %slice.2), channel_id=1, source_target_pairs={{0,1},{1,0},{2,3},{3,2},{4,5},{5,4},{6,7},{7,6},{8,9},{9,8},{10,11... | collective-permute-start | bytes 73736 | tf_op jit(solution)/shard_map/ppermute | solution.py:223
  26.9 6.0 %collective-permute-start.9 = (f32[24,128]{1,0:T(8,128)S(1)}, f32[24,128]{1,0:T(8,128)S(1)}, u32[]{:S(2)}, u32[]{:S(2)}) collective-permute-start(f32[24,128]{1,0:T(8,128)S(1)} %shard_map.70.extra_ref), channel_id=1, source_target_pairs={{0,3},{1,2},{2,1},{3,0},{4,7},{5,6},{6,5},{7,4},{8,11},{9,10},{10,... | collective-permute-start | bytes 36872 | tf_op jit(solution)/shard_map/ppermute | solution.py:223
  27.8 5.1 %collective-permute-start.8 = (f32[24,128]{1,0:T(8,128)S(1)}, f32[24,128]{1,0:T(8,128)S(1)}, u32[]{:S(2)}, u32[]{:S(2)}) collective-permute-start(f32[24,128]{1,0:T(8,128)S(1)} %shard_map.70.extra_ref), channel_id=1, source_target_pairs={{0,2},{1,3},{2,0},{3,1},{4,6},{5,7},{6,4},{7,5},{8,10},{9,11},{10,... | collective-permute-start | bytes 36872 | tf_op jit(solution)/shard_map/ppermute | solution.py:223
  29.0 3.9 %collective-permute-start.7 = (f32[24,128]{1,0:T(8,128)S(1)}, f32[24,128]{1,0:T(8,128)S(1)}, u32[]{:S(2)}, u32[]{:S(2)}) collective-permute-start(f32[24,128]{1,0:T(8,128)S(1)} %shard_map.70.extra_ref), channel_id=1, source_target_pairs={{0,1},{1,0},{2,3},{3,2},{4,5},{5,4},{6,7},{7,6},{8,9},{9,8},{10,11... | collective-permute-start | bytes 36872 | tf_op jit(solution)/shard_map/ppermute | solution.py:223
  32.9 5.6 %collective-permute-start.12 = (f32[96,128]{1,0:T(8,128)S(1)}, f32[96,128]{1,0:T(8,128)S(1)}, u32[]{:S(2)}, u32[]{:S(2)}) collective-permute-start(f32[96,128]{1,0:T(8,128)S(1)} %pad_maximum_fusion), channel_id=1, source_target_pairs={{0,4},{4,0},{8,12},{12,8},{16,20},{20,16},{24,28},{28,24},{1,5},{5... | collective-permute-start | bytes 147464 | tf_op jit(solution)/shard_map/ppermute | solution.py:257
  36.1 8.4 %collective-permute-start.17 = (bf16[64,2048]{1,0:T(8,128)(2,1)S(1)}, bf16[64,2048]{1,0:T(8,128)(2,1)S(1)}, u32[]{:S(2)}, u32[]{:S(2)}) collective-permute-start(bf16[64,2048]{1,0:T(8,128)(2,1)S(1)} %shard_map.71.d0), channel_id=1, source_target_pairs={{0,2},{1,3},{2,0},{3,1},{4,6},{5,7},{6,4},{7,5},{8,10},{9,11},{10,... | collective-permute-start | bytes 786440 | tf_op jit(solution)/shard_map/ppermute | solution.py:223
  38.5 6.1 %collective-permute-start.15 = (f32[96,128]{1,0:T(8,128)S(1)}, f32[96,128]{1,0:T(8,128)S(1)}, u32[]{:S(2)}, u32[]{:S(2)}) collective-permute-start(f32[96,128]{1,0:T(8,128)S(1)} %fusion), channel_id=1, source_target_pairs={{0,24},{4,28},{8,16},{12,20},{16,8},{20,12},{24,0},{28,4},{1,25},{... | collective-permute-start | bytes 147464 | tf_op jit(solution)/shard_map/ppermute | solution.py:257
  41.7 5.0 %collective-permute-start.14 = (f32[96,128]{1,0:T(8,128)S(1)}, f32[96,128]{1,0:T(8,128)S(1)}, u32[]{:S(2)}, u32[]{:S(2)}) collective-permute-start(f32[96,128]{1,0:T(8,128)S(1)} %fusion), channel_id=1, source_target_pairs={{0,16},{4,20},{8,24},{12,28},{16,0},{20,4},{24,8},{28,12},{1,17},{... | collective-permute-start | bytes 147464 | tf_op jit(solution)/shard_map/ppermute | solution.py:257
  41.7 5.0 %collective-permute-start.13 = (f32[96,128]{1,0:T(8,128)S(1)}, f32[96,128]{1,0:T(8,128)S(1)}, u32[]{:S(2)}, u32[]{:S(2)}) collective-permute-start(f32[96,128]{1,0:T(8,128)S(1)} %fusion), channel_id=1, source_target_pairs={{0,8},{4,12},{8,0},{12,4},{16,24},{20,28},{24,16},{28,20},{1,9},{5... | collective-permute-start | bytes 147464 | tf_op jit(solution)/shard_map/ppermute | solution.py:257
  43.0 3.7 %collective-permute-start.16 = (bf16[64,2048]{1,0:T(8,128)(2,1)S(1)}, bf16[64,2048]{1,0:T(8,128)(2,1)S(1)}, u32[]{:S(2)}, u32[]{:S(2)}) collective-permute-start(bf16[64,2048]{1,0:T(8,128)(2,1)S(1)} %shard_map.71.d0), channel_id=1, source_target_pairs={{0,1},{1,0},{2,3},{3,2},{4,5},{5,4},{6,7},{7,6},{8,9},{9,8},{10,11... | collective-permute-start | bytes 786440 | tf_op jit(solution)/shard_map/ppermute | solution.py:223
  44.6 2.2 %collective-permute-start.18 = (bf16[64,2048]{1,0:T(8,128)(2,1)S(1)}, bf16[64,2048]{1,0:T(8,128)(2,1)S(1)}, u32[]{:S(2)}, u32[]{:S(2)}) collective-permute-start(bf16[64,2048]{1,0:T(8,128)(2,1)S(1)} %collective-permute-done.17.d2), channel_id=1, source_target_pairs={{0,1},{1,0},{2,3},{3,2},{4,5},{5,4},{6,7},{7,6},{8,9},{9,8},{10,11... | collective-permute-start | bytes 786440 | tf_op jit(solution)/shard_map/ppermute | solution.py:223

commit v5 on v4

--- a/solution.py
+++ b/solution.py
@@ -11,9 +11,9 @@
 NBT = 8
 EPS = 1e-05
 ARCH, COUNTS, META = range(NBT, NBT + 3)
+OWN, PAIR, OTHER = range(1, 4)
 
 VMEM = pl.BlockSpec(memory_space=pltpu.VMEM)
-SMEM = pl.BlockSpec(memory_space=pltpu.SMEM)
 ANY = pl.BlockSpec(memory_space=pl.ANY)
 HBM = pl.BlockSpec(memory_space=pltpu.HBM)
 
@@ -47,7 +47,8 @@
 def rows_kernel(info_ref, table_ref, tiles_ref, v_ref, rows_ref, own_ref, held_ref, sem):
     blocks = tiles_ref.shape[0]
     narch = rows_ref.shape[0]
-    first_block, first_slot = info_ref[META, 0], 2 * info_ref[META, 2]
+    info = info_ref[...]
+    first_block, first_slot = info[META, 0], 2 * info[META, 2]
     whole = pltpu.make_async_copy(v_ref, own_ref, sem.at[2])
     whole.start()
     copies = []
@@ -66,7 +67,7 @@
     rows_ref[:, 2 * TILE:2 * TILE + NBT] = steps.astype(jnp.bfloat16)
     for i in range(2):
         sel = [
-            jnp.where(hit, jnp.where(first_slot + i < info_ref[COUNTS, b], 1.0, 0.0), 0.0).astype(jnp.bfloat16)
+            jnp.where(hit, jnp.where(first_slot + i < info[COUNTS, b], 1.0, 0.0), 0.0).astype(jnp.bfloat16)
             for b, hit in enumerate(hits)
         ]
         copies[i].wait()
@@ -76,24 +77,32 @@
     whole.wait()
 
 
-def step_block(info_ref, tiles_ref, own_ref, pair_ref, other_ref, b, with_degree):
-    blocks = own_ref.shape[1] // TILE
-    first_block, odd = info_ref[META, 0], info_ref[META, 1]
+def slot_codes(info_ref, blocks):
+    shape = (NBT, TILE)
+    local = info_ref[:NBT] - info_ref[META:META + 1, :1]
+    odd = jnp.broadcast_to(info_ref[META:META + 1, 1:2], shape)
+    counts = jnp.broadcast_to(info_ref[COUNTS:COUNTS + 1], shape)
+    below = jnp.where(odd == 1, PAIR, OTHER)
+    side = jnp.where(local < 0, below, jnp.where(local >= blocks, PAIR + OTHER - below, OWN))
+    at = jnp.where(local < 0, local + blocks, jnp.where(local >= blocks, local - blocks, local))
+    used = lax.broadcasted_iota(jnp.int32, shape, 0) < counts
+    return jnp.where(used, side, 0) * blocks + at
+
+
+def step_block(codes, tiles_ref, own_ref, pair_ref, other_ref, b, with_degree):
+    blocks = tiles_ref.shape[0]
     parts, ones = [], []
     for j in range(NBT):
-        local = info_ref[j, b] - first_block
-        lower, upper = local < 0, local >= blocks
-        at = lanes(jnp.where(lower, local + blocks, jnp.where(upper, local - blocks, local)))
-        used = j < info_ref[COUNTS, b]
+        code = codes[j, b]
+        side, at = lax.div(code, blocks), lanes(lax.rem(code, blocks))
         x = own_ref[:, at]
         if j > 0:
-            near = jnp.logical_or(jnp.logical_and(lower, odd == 1), jnp.logical_and(upper, odd == 0))
-            beside = jnp.where(near, pair_ref[:, at], other_ref[:, at])
-            x = beside if j < 3 else jnp.where(jnp.logical_or(lower, upper), beside, x)
+            beside = jnp.where(side == PAIR, pair_ref[:, at], other_ref[:, at])
+            x = beside if j < 3 else jnp.where(side == OWN, x, beside)
         if j >= 3:
-            x = jnp.where(used, x, jnp.zeros_like(x))
+            x = jnp.where(side > 0, x, jnp.zeros_like(x))
         parts.append(x)
-        ones.append(jnp.full((16, TILE), jnp.where(used, 1.0, 0.0), jnp.float32).astype(jnp.bfloat16))
+        ones.append(jnp.full((16, TILE), jnp.where(side > 0, 1.0, 0.0), jnp.float32).astype(jnp.bfloat16))
     lhs = jnp.concatenate(parts, axis=1)
     if with_degree:
         lhs = jnp.concatenate([lhs, jnp.concatenate(ones, axis=1)], axis=0)
@@ -102,24 +111,27 @@
 
 def first_kernel(info_ref, tiles_ref, own_ref, other_ref, pair_ref, out_ref, inv_ref):
     feats = own_ref.shape[0]
+    codes = slot_codes(info_ref, tiles_ref.shape[0])
     for b in range(tiles_ref.shape[0]):
-        out = step_block(info_ref, tiles_ref, own_ref, pair_ref, other_ref, b, True)
+        out = step_block(codes, tiles_ref, own_ref, pair_ref, other_ref, b, True)
         inv = 1.0 / out[feats:feats + 8]
         inv_ref[b] = inv
         out_ref[:, b * TILE:(b + 1) * TILE] = (out[:feats] * inv[:1]).astype(jnp.bfloat16)
 
 
 def second_kernel(info_ref, tiles_ref, own_ref, other_ref, pair_ref, inv_ref, extra_ref, out_ref):
+    codes = slot_codes(info_ref, tiles_ref.shape[0])
     for b in range(tiles_ref.shape[0]):
-        out = step_block(info_ref, tiles_ref, own_ref, pair_ref, other_ref, b, False)
+        out = step_block(codes, tiles_ref, own_ref, pair_ref, other_ref, b, False)
         out_ref[:, b * TILE:(b + 1) * TILE] = (out * inv_ref[b][:1]).astype(jnp.bfloat16)
 
 
 def arch_kernel(info_ref, table_ref, r0, r1, r2, r3, v_ref, out_ref):
     blocks = v_ref.shape[1] // TILE
     narch = r0.shape[0]
-    me = info_ref[META, 2]
-    block = lax.div(column(table_ref[ARCH:ARCH + 1, :narch], narch), TILE) - info_ref[META, 0]
+    info = info_ref[...]
+    me = info[META, 2]
+    block = lax.div(column(table_ref[ARCH:ARCH + 1, :narch], narch), TILE) - info[META, 0]
     offsets = r0[:, 2 * TILE:].astype(jnp.float32)
     lane = lax.broadcasted_iota(jnp.int32, offsets.shape, 1)
     rows, places = [], []
@@ -147,21 +159,23 @@
     return jnp.broadcast_to(x, shape)
 
 
-def solve_kernel(info_ref, total_ref, d0, d1, d2, d3, out_ref, copy_ref, whole_ref, scale_ref):
+def solve_kernel(info_ref, total_ref, d0, d1, d2, d3, out_ref, copy_ref, whole_ref, scale_ref, made_ref, sem):
     total = total_ref[...].astype(jnp.bfloat16)
     feats, width = d0.shape
     n = total.shape[0] // 2
-    copy_ref[...] = d0[...]
+    same = pltpu.make_async_copy(d0, copy_ref, sem.at[0])
+    same.start()
+    me = info_ref[...][META, 2]
     step = 256
     for c in range(0, width, step):
-        d = jnp.concatenate(in_order(info_ref[META, 2], [d[:, c:c + step] for d in (d0, d1, d2, d3)]), axis=0)
+        d = jnp.concatenate(in_order(me, [d[:, c:c + step] for d in (d0, d1, d2, d3)]), axis=0)
         whole_ref[:, c:c + step] = d
         wide = d.astype(jnp.float32)
         scale_ref[:, c:c + step] = lax.rsqrt(jnp.sum(wide * wide, axis=0, keepdims=True) / F + EPS)
     part = n // 2
     pieces = [total[p * part:(p + 1) * part] for p in range(4)]
     pieces = [jnp.concatenate([p[:, :feats], p[:, feats:]], axis=0) for p in pieces]
-    pieces = in_order(info_ref[META, 2], pieces)
+    pieces = in_order(me, pieces)
     arch = jnp.concatenate(pieces, axis=1)
     shape = (n, TILE)
     row = lax.broadcasted_iota(jnp.int32, shape, 0)
@@ -185,9 +199,14 @@
     third = (inverse - high.astype(jnp.float32) - low.astype(jnp.float32)).astype(jnp.bfloat16)
     q = dot(jnp.concatenate([high, low, third], axis=0), arch)
     q = jnp.concatenate(halves(q[:n] + q[n:2 * n] + q[2 * n:]), axis=0)
-    for c in range(0, width, step):
+    copies = [same]
+    for i, c in enumerate(range(0, width, step)):
         z = dot(q, whole_ref[:, c:c + step])
-        out_ref[:, c:c + step] = (z[:n] + z[n:]) * scale_ref[:, c:c + step]
+        made_ref[:, c:c + step] = (z[:n] + z[n:]) * scale_ref[:, c:c + step]
+        copies.append(pltpu.make_async_copy(made_ref.at[:, c:c + step], out_ref.at[:, c:c + step], sem.at[1 + i]))
+        copies[-1].start()
+    for copy in copies:
+        copy.wait()
 
 
 def in_order(me, pieces):
@@ -197,14 +216,14 @@
     return pieces
 
 
-def call(kernel, out_shape, kinds, args, flops, nbytes, scratch=(), limit=16):
+def call(kernel, out_shape, kinds, args, flops, nbytes, scratch=(), limit=16, place=VMEM):
     single = not isinstance(out_shape, (list, tuple))
-    spec = {"s": SMEM, "v": VMEM, "a": ANY, "h": HBM}
+    spec = {"v": VMEM, "a": ANY, "h": HBM}
     return pl.pallas_call(
         kernel,
         out_shape=out_shape,
         in_specs=[spec[k] for k in kinds],
-        out_specs=VMEM if single else [VMEM] * len(out_shape),
+        out_specs=place if single else [place] * len(out_shape),
         scratch_shapes=scratch,
         compiler_params=pltpu.CompilerParams(vmem_limit_bytes=limit << 20),
         cost_estimate=pl.CostEstimate(flops=flops, bytes_accessed=nbytes, transcendentals=0),
@@ -238,10 +257,10 @@
     nbytes = 2 * TILE * TILE * NBT * blocks
 
     pair, other = exchange(expression)
-    arch_rows, own = call(rows_kernel, [shape((narch, 3 * TILE), bf16), shape((feats, rows), bf16)], "svhh",
+    arch_rows, own = call(rows_kernel, [shape((narch, 3 * TILE), bf16), shape((feats, rows), bf16)], "vvhh",
                      (info, info, tiles, expression), 0, 0,
                      [pltpu.VMEM((blocks, 2, TILE, TILE), bf16), pltpu.SemaphoreType.DMA((3,))], 52)
-    first, inv = call(first_kernel, [shape((feats, rows), bf16), shape((blocks, 8, TILE), f32)], "svvvv",
+    first, inv = call(first_kernel, [shape((feats, rows), bf16), shape((blocks, 8, TILE), f32)], "vvvvv",
                       (info, tiles, own, other, pair), flops, nbytes)
 
     row_pair, row_other = exchange(arch_rows)
@@ -249,9 +268,9 @@
     near_rows, _ = lax.optimization_barrier((own_rows + row_pair + row_other, first))
     r = [near_rows] + [flip_feat(near_rows[:, :2 * TILE], p) for p in (1, 2, 3)]
     pair, other = exchange(first)
-    part = call(arch_kernel, shape((narch // 2, 2 * feats), f32), "svvvvvv", (info, info, *r, first), 0, 0)
+    part = call(arch_kernel, shape((narch // 2, 2 * feats), f32), "vvvvvvv", (info, info, *r, first), 0, 0)
     step = (info, tiles, first, other, pair, inv)
-    diffused = call(second_kernel, shape((feats, rows), bf16), "svvvvva", (*step, part), flops * 16, 0)
+    diffused = call(second_kernel, shape((feats, rows), bf16), "vvvvvva", (*step, part), flops * 16, 0)
     seen, diffused = lax.optimization_barrier(([flip_feat(part, p) for p in (1, 2, 3)], diffused))
     part = jnp.concatenate([part, *seen], axis=0)
     flip_cells = lambda x, bits: lax.ppermute(x, "cells", [(i, i ^ bits) for i in range(size)])
@@ -267,9 +286,10 @@
         part = (part + near) + (far + both)
         level += 2
     coords, diffused = call(
-        solve_kernel, [shape((narch, rows), f32), shape((feats, rows), bf16)], "svvvvv",
+        solve_kernel, [shape((narch, rows), f32), shape((feats, rows), bf16)], "vvvvvv",
         (info, part, *pieces), 4 * narch * F * rows, 4 * narch * rows,
-        [pltpu.VMEM((4 * feats, rows), bf16), pltpu.VMEM((1, rows), f32)])
+        [pltpu.VMEM((4 * feats, rows), bf16), pltpu.VMEM((1, rows), f32), pltpu.VMEM((narch, rows), f32),
+         pltpu.SemaphoreType.DMA((1 + rows // 256,))], place=HBM)
     return diffused, coords
 
 

time: 50.5 us -> 49.2 us (0.974)
  Pallas kernels: 12 us -> 9.3 us
  waiting for transfers between devices: 9.49 us -> 10.6 us
    pallas_call x5, Pallas kernels: 12 us -> 9.3 us  [call(): pl.pallas_call(kernel, out_shape=out_shape, in_specs=[spec[k] for k in ki...]
    ppermute x3, waiting for transfers between devices: 2.47 us -> 3.45 us  [exchange(): lax.ppermute(matrix, 'cells', pairs)]
    ppermute x4, waiting for transfers between devices: 3.39 us -> 3.89 us  [on_device(): lax.ppermute(x, 'cells', [(i, i ^ bits) for i in range(size)])]
  transfers between devices with their start and end apart: 19 -> 19, of which waited for: 8 -> 8; matrix products, arithmetic and copies ran while one was open for 2% -> 2% of each run, Pallas kernels for 17% -> 13%
where the time goes in v5:
time: 49.2 us; the launch traced here: 49 us
  starting transfers between devices  26.1 us (53%)
  waiting for transfers between devices  10.6 us (22%)
  Pallas kernels  9.3 us (19%)
  local copies, waits for them, and re-layouts  1.19 us (2%)
  other arithmetic  1 us (2%)
  between operations  0.8 us (2%)
    ppermute x3, starting transfers between devices, exchange(): lax.ppermute(matrix, 'cells', pairs)  11 us
    pallas_call x5, Pallas kernels, call(): pl.pallas_call(kernel, out_shape=out_shape, in_specs=[spec[k] for k in ki...  9.3 us
    ppermute x4, starting transfers between devices, on_device(): lax.ppermute(x, 'cells', [(i, i ^ bits) for i in range(size)])  7.59 us
    ppermute x9, starting transfers between devices, flip_feat(): lax.ppermute(x, 'feat', [(i, i ^ bits) for i in range(lax.axis_size('feat...  5.44 us
    ppermute x4, waiting for transfers between devices, on_device(): lax.ppermute(x, 'cells', [(i, i ^ bits) for i in range(size)])  3.89 us
    ppermute x3, waiting for transfers between devices, exchange(): lax.ppermute(matrix, 'cells', pairs)  3.45 us
    ppermute x9, waiting for transfers between devices, flip_feat(): lax.ppermute(x, 'feat', [(i, i ^ bits) for i in range(lax.axis_size('feat...  3.26 us
    ppermute x3, starting transfers between devices, exchange(): lax.ppermute(matrix, 'cells', others)  1.99 us
  transfers between devices with their start and end apart: 19, of which 8 were waited for; matrix products, arithmetic and copies ran while one was open for 2% of the time, Pallas kernels for 13%

profile of v5, /device:TPU:0, one launch (start us, length us, event | category | flops | bytes accessed | tf_op | source)
XLA Modules:
  0.0 49.0 jit_solution(6733660863516666250)
XLA Ops:
  0.6 3.0 %collective-permute-start.3 = (bf16[64,2048]{1,0:T(8,128)(2,1)}, bf16[64,2048]{1,0:T(8,128)(2,1)S(1)}, u32[]{:S(2)}, u32[]{:S(2)}) collective-permute-start(bf16[64,2048]{1,0:T(8,128)(2,1)} %v_ref.1), channel_id=1, source_target_pairs={{0,4},{4,0},{8,12},{12,8},{16,20},{20,16},{24,28},{28,24},{1,5},{5... | collective-permute-start | bytes 786440 | tf_op jit(solution)/shard_map/ppermute | solution.py:238
  3.7 0.7 %collective-permute-start = (bf16[64,2048]{1,0:T(8,128)(2,1)}, bf16[64,2048]{1,0:T(8,128)(2,1)S(1)}, u32[]{:S(2)}, u32[]{:S(2)}) collective-permute-start(bf16[64,2048]{1,0:T(8,128)(2,1)} %v_ref.1), channel_id=1, source_target_pairs={{4,8},{12,16},{20,24},{8,4},{16,12},{24,20},{5,9},{13,17},{21,25},... | collective-permute-start | bytes 786440 | tf_op jit(solution)/shard_map/ppermute | solution.py:238
  4.4 0.9 %pad_add_fusion.info_ref.table_ref = s32[11,128]{1,0:T(8,128)S(1)} fusion(s32[1,3]{1,0:T(1,128)S(1)} %add_bitcast_fusion, s32[1,16]{1,0:T(1,128)} %bitcast.9, s32[1,48]{1,0:T(1,128)} %bitcast.10, s32[8,16]{1,0:T(8,128)} %bitcast.8), kind=kLoop, calls=%fused_computation.3 | loop fusion | flops 4224 | bytes 6412 | tf_op jit(solution)/shard_map/concatenate | solution.py:255
  5.3 1.2 %copy-done.1 = bf16[64,2048]{1,0:T(8,128)(2,1)S(1)} copy-done((bf16[64,2048]{1,0:T(8,128)(2,1)S(1)}, bf16[64,2048]{1,0:T(8,128)(2,1)}, u32[]{:S(2)}) %copy-start.1) | copy-done | bytes 262168
  6.5 1.8 %shard_map.68 = (bf16[48,384]{1,0:T(8,128)(2,1)S(1)}, bf16[64,2048]{1,0:T(8,128)(2,1)S(1)}) custom-call(s32[11,128]{1,0:T(8,128)S(1)} %pad_add_fusion.info_ref.table_ref, s32[11,128]{1,0:T(8,128)S(1)} %pad_add_fusion.info_ref.table_ref, bf16[16,8,128,128]{3,2,1,0:T(8,128)(2,1)} %tiles_ref.5, bf16[64,2048]{1,0:T(8,128)(2,1)S(1)} %copy-done.1), custom_call_target="tpu_custom_call" | custom-call | tf_op jit(solution)/shard_map/pallas_call | solution.py:222
  9.0 5.6 %collective-permute-start.1 = (bf16[48,384]{1,0:T(8,128)(2,1)S(1)}, bf16[48,384]{1,0:T(8,128)(2,1)S(1)}, u32[]{:S(2)}, u32[]{:S(2)}) collective-permute-start(bf16[48,384]{1,0:T(8,128)(2,1)S(1)} %get-tuple-element.15), channel_id=1, source_target_pairs={{0,4},{4,0},{8,12},{12,8},{16,20},{20,16},{24,28},{28,24},{1,5},{5... | collective-permute-start | bytes 110600 | tf_op jit(solution)/shard_map/ppermute | solution.py:238
  14.6 1.4 %collective-permute-done.3.pair_ref = bf16[64,2048]{1,0:T(8,128)(2,1)S(1)} collective-permute-done((bf16[64,2048]{1,0:T(8,128)(2,1)}, bf16[64,2048]{1,0:T(8,128)(2,1)S(1)}, u32[]{:S(2)}, u32[]{:S(2)}) %collective-permute-start.3) | collective-permute-done | bytes 262176 | tf_op jit(solution)/shard_map/ppermute | solution.py:238
  16.0 2.0 %shard_map.69 = (bf16[64,2048]{1,0:T(8,128)(2,1)S(1)}, f32[16,8,128]{2,1,0:T(8,128)S(1)}) custom-call(s32[11,128]{1,0:T(8,128)S(1)} %pad_add_fusion.info_ref.table_ref, bf16[16,8,128,128]{3,2,1,0:T(8,128)(2,1)S(1)} %copy-done, bf16[64,2048]{1,0:T(8,128)(2,1)S(1)} %get-tuple-element.16.own_ref, bf16[64,2048]{1,0:T(8,128)(2,1)S(1)} %collective-permute-done.other_ref, ...), custom_call_target="tpu_custom_call" | custom-call | flops 268435456 | bytes 4194304 | tf_op jit(solution)/shard_map/pallas_call | solution.py:222
  18.0 2.4 %collective-permute-start.11 = (bf16[64,2048]{1,0:T(8,128)(2,1)S(1)}, bf16[64,2048]{1,0:T(8,128)(2,1)S(1)}, u32[]{:S(2)}, u32[]{:S(2)}) collective-permute-start(bf16[64,2048]{1,0:T(8,128)(2,1)S(1)} %get-tuple-element.17.v_ref.own_ref), channel_id=1, source_target_pairs={{0,4},{4,0},{8,12},{12,8},{16,20},{20,16},{24,28},{28,24},{1,5},{5... | collective-permute-start | bytes 786440 | tf_op jit(solution)/shard_map/ppermute | solution.py:238
  20.4 0.7 %collective-permute-start.10 = (bf16[64,2048]{1,0:T(8,128)(2,1)S(1)}, bf16[64,2048]{1,0:T(8,128)(2,1)S(1)}, u32[]{:S(2)}, u32[]{:S(2)}) collective-permute-start(bf16[64,2048]{1,0:T(8,128)(2,1)S(1)} %get-tuple-element.17.v_ref.own_ref), channel_id=1, source_target_pairs={{4,8},{12,16},{20,24},{8,4},{16,12},{24,20},{5,9},{13,17},{21,25},... | collective-permute-start | bytes 786440 | tf_op jit(solution)/shard_map/ppermute | solution.py:238
  21.2 1.6 %collective-permute-start.5 = (bf16[48,256]{1,0:T(8,128)(2,1)S(1)}, bf16[48,256]{1,0:T(8,128)(2,1)S(1)}, u32[]{:S(2)}, u32[]{:S(2)}) collective-permute-start(bf16[48,256]{1,0:T(8,128)(2,1)S(1)} %slice.2), channel_id=1, source_target_pairs={{0,2},{1,3},{2,0},{3,1},{4,6},{5,7},{6,4},{7,5},{8,10},{9,11},{10,... | collective-permute-start | bytes 73736 | tf_op jit(solution)/shard_map/ppermute | solution.py:242
  23.1 1.6 %collective-permute-done.6.r3 = bf16[48,256]{1,0:T(8,128)(2,1)S(1)} collective-permute-done((bf16[48,256]{1,0:T(8,128)(2,1)S(1)}, bf16[48,256]{1,0:T(8,128)(2,1)S(1)}, u32[]{:S(2)}, u32[]{:S(2)}) %collective-permute-start.6) | collective-permute-done | bytes 24608 | tf_op jit(solution)/shard_map/ppermute | solution.py:242
  25.1 0.8 %shard_map.70.extra_ref = f32[24,128]{1,0:T(8,128)S(1)} custom-call(s32[11,128]{1,0:T(8,128)S(1)} %pad_add_fusion.info_ref.table_ref, s32[11,128]{1,0:T(8,128)S(1)} %pad_add_fusion.info_ref.table_ref, bf16[48,384]{1,0:T(8,128)(2,1)S(1)} %add_add_fusion.1.r0, bf16[48,256]{1,0:T(8,128)(2,1)S(1)} %collective-permute-done.4.r1, ...), custom_call_target="tpu_custom_call" | custom-call | tf_op jit(solution)/shard_map/pallas_call | solution.py:222
  25.9 0.8 %collective-permute-start.9 = (f32[24,128]{1,0:T(8,128)S(1)}, f32[24,128]{1,0:T(8,128)S(1)}, u32[]{:S(2)}, u32[]{:S(2)}) collective-permute-start(f32[24,128]{1,0:T(8,128)S(1)} %shard_map.70.extra_ref), channel_id=1, source_target_pairs={{0,3},{1,2},{2,1},{3,0},{4,7},{5,6},{6,5},{7,4},{8,11},{9,10},{10,... | collective-permute-start | bytes 36872 | tf_op jit(solution)/shard_map/ppermute | solution.py:242
  26.7 1.2 %collective-permute-start.8 = (f32[24,128]{1,0:T(8,128)S(1)}, f32[24,128]{1,0:T(8,128)S(1)}, u32[]{:S(2)}, u32[]{:S(2)}) collective-permute-start(f32[24,128]{1,0:T(8,128)S(1)} %shard_map.70.extra_ref), channel_id=1, source_target_pairs={{0,2},{1,3},{2,0},{3,1},{4,6},{5,7},{6,4},{7,5},{8,10},{9,11},{10,... | collective-permute-start | bytes 36872 | tf_op jit(solution)/shard_map/ppermute | solution.py:242
  27.9 2.0 %collective-permute-done.11.pair_ref = bf16[64,2048]{1,0:T(8,128)(2,1)S(1)} collective-permute-done((bf16[64,2048]{1,0:T(8,128)(2,1)S(1)}, bf16[64,2048]{1,0:T(8,128)(2,1)S(1)}, u32[]{:S(2)}, u32[]{:S(2)}) %collective-permute-start.11) | collective-permute-done | bytes 262176 | tf_op jit(solution)/shard_map/ppermute | solution.py:238
  29.9 2.0 %shard_map.71.d0 = bf16[64,2048]{1,0:T(8,128)(2,1)S(1)} custom-call(s32[11,128]{1,0:T(8,128)S(1)} %pad_add_fusion.info_ref.table_ref, bf16[16,8,128,128]{3,2,1,0:T(8,128)(2,1)S(1)} %copy-done, bf16[64,2048]{1,0:T(8,128)(2,1)S(1)} %get-tuple-element.17.v_ref.own_ref, bf16[64,2048]{1,0:T(8,128)(2,1)S(1)} %collective-permute-done.10.other_ref, ...), custom_call_target="tpu_custom_call" | custom-call | flops 4294967296 | tf_op jit(solution)/shard_map/pallas_call | solution.py:222
  32.0 2.8 %collective-permute-start.12 = (f32[96,128]{1,0:T(8,128)S(1)}, f32[96,128]{1,0:T(8,128)S(1)}, u32[]{:S(2)}, u32[]{:S(2)}) collective-permute-start(f32[96,128]{1,0:T(8,128)S(1)} %pad_maximum_fusion), channel_id=1, source_target_pairs={{0,4},{4,0},{8,12},{12,8},{16,20},{20,16},{24,28},{28,24},{1,5},{5... | collective-permute-start | bytes 147464 | tf_op jit(solution)/shard_map/ppermute | solution.py:276
  34.7 1.5 %collective-permute-start.17 = (bf16[64,2048]{1,0:T(8,128)(2,1)S(1)}, bf16[64,2048]{1,0:T(8,128)(2,1)S(1)}, u32[]{:S(2)}, u32[]{:S(2)}) collective-permute-start(bf16[64,2048]{1,0:T(8,128)(2,1)S(1)} %shard_map.71.d0), channel_id=1, source_target_pairs={{0,2},{1,3},{2,0},{3,1},{4,6},{5,7},{6,4},{7,5},{8,10},{9,11},{10,... | collective-permute-start | bytes 786440 | tf_op jit(solution)/shard_map/ppermute | solution.py:242
  36.2 0.7 %collective-permute-done.12 = f32[96,128]{1,0:T(8,128)S(1)} collective-permute-done((f32[96,128]{1,0:T(8,128)S(1)}, f32[96,128]{1,0:T(8,128)S(1)}, u32[]{:S(2)}, u32[]{:S(2)}) %collective-permute-start.12) | collective-permute-done | bytes 49184 | tf_op jit(solution)/shard_map/ppermute | solution.py:276
  37.0 4.2 %collective-permute-start.15 = (f32[96,128]{1,0:T(8,128)S(1)}, f32[96,128]{1,0:T(8,128)S(1)}, u32[]{:S(2)}, u32[]{:S(2)}) collective-permute-start(f32[96,128]{1,0:T(8,128)S(1)} %fusion), channel_id=1, source_target_pairs={{0,24},{4,28},{8,16},{12,20},{16,8},{20,12},{24,0},{28,4},{1,25},{... | collective-permute-start | bytes 147464 | tf_op jit(solution)/shard_map/ppermute | solution.py:276
  41.8 1.2 %collective-permute-done.17.d2 = bf16[64,2048]{1,0:T(8,128)(2,1)S(1)} collective-permute-done((bf16[64,2048]{1,0:T(8,128)(2,1)S(1)}, bf16[64,2048]{1,0:T(8,128)(2,1)S(1)}, u32[]{:S(2)}, u32[]{:S(2)}) %collective-permute-start.17) | collective-permute-done | bytes 262176 | tf_op jit(solution)/shard_map/ppermute | solution.py:242
  43.2 2.9 %collective-permute-done.14 = f32[96,128]{1,0:T(8,128)S(1)} collective-permute-done((f32[96,128]{1,0:T(8,128)S(1)}, f32[96,128]{1,0:T(8,128)S(1)}, u32[]{:S(2)}, u32[]{:S(2)}) %collective-permute-start.14) | collective-permute-done | bytes 49184 | tf_op jit(solution)/shard_map/ppermute | solution.py:276
  46.2 2.8 %shard_map.72 = (f32[48,2048]{1,0:T(8,128)}, bf16[64,2048]{1,0:T(8,128)(2,1)}) custom-call(s32[11,128]{1,0:T(8,128)S(1)} %pad_add_fusion.info_ref.table_ref, f32[96,128]{1,0:T(8,128)S(1)} %add_add_fusion.total_ref, bf16[64,2048]{1,0:T(8,128)(2,1)S(1)} %shard_map.71.d0, bf16[64,2048]{1,0:T(8,128)(2,1)S(1)} %collective-permute-done.16.d1, ...), custom_call_target="tpu_custom_call" | custom-call | flops 100663296 | bytes 393216 | tf_op jit(solution)/shard_map/pallas_call | solution.py:222
  (30 shorter events, 2.5 us)
Async XLA Ops:
  0.6 15.4 %collective-permute-start.3 = (bf16[64,2048]{1,0:T(8,128)(2,1)}, bf16[64,2048]{1,0:T(8,128)(2,1)S(1)}, u32[]{:S(2)}, u32[]{:S(2)}) collective-permute-start(bf16[64,2048]{1,0:T(8,128)(2,1)} %v_ref.1), channel_id=1, source_target_pairs={{0,4},{4,0},{8,12},{12,8},{16,20},{20,16},{24,28},{28,24},{1,5},{5... | collective-permute-start | bytes 786440 | tf_op jit(solution)/shard_map/ppermute | solution.py:238
  3.7 12.3 %collective-permute-start = (bf16[64,2048]{1,0:T(8,128)(2,1)}, bf16[64,2048]{1,0:T(8,128)(2,1)S(1)}, u32[]{:S(2)}, u32[]{:S(2)}) collective-permute-start(bf16[64,2048]{1,0:T(8,128)(2,1)} %v_ref.1), channel_id=1, source_target_pairs={{4,8},{12,16},{20,24},{8,4},{16,12},{24,20},{5,9},{13,17},{21,25},... | collective-permute-start | bytes 786440 | tf_op jit(solution)/shard_map/ppermute | solution.py:238
  4.3 11.6 %copy-start = (bf16[16,8,128,128]{3,2,1,0:T(8,128)(2,1)S(1)}, bf16[16,8,128,128]{3,2,1,0:T(8,128)(2,1)}, u32[]{:S(2)}) copy-start(bf16[16,8,128,128]{3,2,1,0:T(8,128)(2,1)} %tiles_ref.5) | copy-start | bytes 12582916
  5.3 1.2 %copy-start.1 = (bf16[64,2048]{1,0:T(8,128)(2,1)S(1)}, bf16[64,2048]{1,0:T(8,128)(2,1)}, u32[]{:S(2)}) copy-start(bf16[64,2048]{1,0:T(8,128)(2,1)} %v_ref.1) | copy-start | bytes 786436
  8.3 12.8 %collective-permute-start.2 = (bf16[48,384]{1,0:T(8,128)(2,1)S(1)}, bf16[48,384]{1,0:T(8,128)(2,1)S(1)}, u32[]{:S(2)}, u32[]{:S(2)}) collective-permute-start(bf16[48,384]{1,0:T(8,128)(2,1)S(1)} %get-tuple-element.15), channel_id=1, source_target_pairs={{4,8},{12,16},{20,24},{8,4},{16,12},{24,20},{5,9},{13,17},{21,25},... | collective-permute-start | bytes 110600 | tf_op jit(solution)/shard_map/ppermute | solution.py:238
  9.0 12.1 %collective-permute-start.1 = (bf16[48,384]{1,0:T(8,128)(2,1)S(1)}, bf16[48,384]{1,0:T(8,128)(2,1)S(1)}, u32[]{:S(2)}, u32[]{:S(2)}) collective-permute-start(bf16[48,384]{1,0:T(8,128)(2,1)S(1)} %get-tuple-element.15), channel_id=1, source_target_pairs={{0,4},{4,0},{8,12},{12,8},{16,20},{20,16},{24,28},{28,24},{1,5},{5... | collective-permute-start | bytes 110600 | tf_op jit(solution)/shard_map/ppermute | solution.py:238
  18.0 11.9 %collective-permute-start.11 = (bf16[64,2048]{1,0:T(8,128)(2,1)S(1)}, bf16[64,2048]{1,0:T(8,128)(2,1)S(1)}, u32[]{:S(2)}, u32[]{:S(2)}) collective-permute-start(bf16[64,2048]{1,0:T(8,128)(2,1)S(1)} %get-tuple-element.17.v_ref.own_ref), channel_id=1, source_target_pairs={{0,4},{4,0},{8,12},{12,8},{16,20},{20,16},{24,28},{28,24},{1,5},{5... | collective-permute-start | bytes 786440 | tf_op jit(solution)/shard_map/ppermute | solution.py:238
  20.4 9.5 %collective-permute-start.10 = (bf16[64,2048]{1,0:T(8,128)(2,1)S(1)}, bf16[64,2048]{1,0:T(8,128)(2,1)S(1)}, u32[]{:S(2)}, u32[]{:S(2)}) collective-permute-start(bf16[64,2048]{1,0:T(8,128)(2,1)S(1)} %get-tuple-element.17.v_ref.own_ref), channel_id=1, source_target_pairs={{4,8},{12,16},{20,24},{8,4},{16,12},{24,20},{5,9},{13,17},{21,25},... | collective-permute-start | bytes 786440 | tf_op jit(solution)/shard_map/ppermute | solution.py:238
  21.1 3.5 %collective-permute-start.6 = (bf16[48,256]{1,0:T(8,128)(2,1)S(1)}, bf16[48,256]{1,0:T(8,128)(2,1)S(1)}, u32[]{:S(2)}, u32[]{:S(2)}) collective-permute-start(bf16[48,256]{1,0:T(8,128)(2,1)S(1)} %slice.2), channel_id=1, source_target_pairs={{0,3},{1,2},{2,1},{3,0},{4,7},{5,6},{6,5},{7,4},{8,11},{9,10},{10,... | collective-permute-start | bytes 73736 | tf_op jit(solution)/shard_map/ppermute | solution.py:242
  21.2 3.9 %collective-permute-start.5 = (bf16[48,256]{1,0:T(8,128)(2,1)S(1)}, bf16[48,256]{1,0:T(8,128)(2,1)S(1)}, u32[]{:S(2)}, u32[]{:S(2)}) collective-permute-start(bf16[48,256]{1,0:T(8,128)(2,1)S(1)} %slice.2), channel_id=1, source_target_pairs={{0,2},{1,3},{2,0},{3,1},{4,6},{5,7},{6,4},{7,5},{8,10},{9,11},{10,... | collective-permute-start | bytes 73736 | tf_op jit(solution)/shard_map/ppermute | solution.py:242
  22.8 2.3 %collective-permute-start.4 = (bf16[48,256]{1,0:T(8,128)(2,1)S(1)}, bf16[48,256]{1,0:T(8,128)(2,1)S(1)}, u32[]{:S(2)}, u32[]{:S(2)}) collective-permute-start(bf16[48,256]{1,0:T(8,128)(2,1)S(1)} %slice.2), channel_id=1, source_target_pairs={{0,1},{1,0},{2,3},{3,2},{4,5},{5,4},{6,7},{7,6},{8,9},{9,8},{10,11... | collective-permute-start | bytes 73736 | tf_op jit(solution)/shard_map/ppermute | solution.py:242
  25.9 6.1 %collective-permute-start.9 = (f32[24,128]{1,0:T(8,128)S(1)}, f32[24,128]{1,0:T(8,128)S(1)}, u32[]{:S(2)}, u32[]{:S(2)}) collective-permute-start(f32[24,128]{1,0:T(8,128)S(1)} %shard_map.70.extra_ref), channel_id=1, source_target_pairs={{0,3},{1,2},{2,1},{3,0},{4,7},{5,6},{6,5},{7,4},{8,11},{9,10},{10,... | collective-permute-start | bytes 36872 | tf_op jit(solution)/shard_map/ppermute | solution.py:242
  26.7 5.2 %collective-permute-start.8 = (f32[24,128]{1,0:T(8,128)S(1)}, f32[24,128]{1,0:T(8,128)S(1)}, u32[]{:S(2)}, u32[]{:S(2)}) collective-permute-start(f32[24,128]{1,0:T(8,128)S(1)} %shard_map.70.extra_ref), channel_id=1, source_target_pairs={{0,2},{1,3},{2,0},{3,1},{4,6},{5,7},{6,4},{7,5},{8,10},{9,11},{10,... | collective-permute-start | bytes 36872 | tf_op jit(solution)/shard_map/ppermute | solution.py:242
  27.9 4.0 %collective-permute-start.7 = (f32[24,128]{1,0:T(8,128)S(1)}, f32[24,128]{1,0:T(8,128)S(1)}, u32[]{:S(2)}, u32[]{:S(2)}) collective-permute-start(f32[24,128]{1,0:T(8,128)S(1)} %shard_map.70.extra_ref), channel_id=1, source_target_pairs={{0,1},{1,0},{2,3},{3,2},{4,5},{5,4},{6,7},{7,6},{8,9},{9,8},{10,11... | collective-permute-start | bytes 36872 | tf_op jit(solution)/shard_map/ppermute | solution.py:242
  32.0 5.0 %collective-permute-start.12 = (f32[96,128]{1,0:T(8,128)S(1)}, f32[96,128]{1,0:T(8,128)S(1)}, u32[]{:S(2)}, u32[]{:S(2)}) collective-permute-start(f32[96,128]{1,0:T(8,128)S(1)} %pad_maximum_fusion), channel_id=1, source_target_pairs={{0,4},{4,0},{8,12},{12,8},{16,20},{20,16},{24,28},{28,24},{1,5},{5... | collective-permute-start | bytes 147464 | tf_op jit(solution)/shard_map/ppermute | solution.py:276
  34.7 8.3 %collective-permute-start.17 = (bf16[64,2048]{1,0:T(8,128)(2,1)S(1)}, bf16[64,2048]{1,0:T(8,128)(2,1)S(1)}, u32[]{:S(2)}, u32[]{:S(2)}) collective-permute-start(bf16[64,2048]{1,0:T(8,128)(2,1)S(1)} %shard_map.71.d0), channel_id=1, source_target_pairs={{0,2},{1,3},{2,0},{3,1},{4,6},{5,7},{6,4},{7,5},{8,10},{9,11},{10,... | collective-permute-start | bytes 786440 | tf_op jit(solution)/shard_map/ppermute | solution.py:242
  37.0 6.2 %collective-permute-start.15 = (f32[96,128]{1,0:T(8,128)S(1)}, f32[96,128]{1,0:T(8,128)S(1)}, u32[]{:S(2)}, u32[]{:S(2)}) collective-permute-start(f32[96,128]{1,0:T(8,128)S(1)} %fusion), channel_id=1, source_target_pairs={{0,24},{4,28},{8,16},{12,20},{16,8},{20,12},{24,0},{28,4},{1,25},{... | collective-permute-start | bytes 147464 | tf_op jit(solution)/shard_map/ppermute | solution.py:276
  41.2 5.0 %collective-permute-start.14 = (f32[96,128]{1,0:T(8,128)S(1)}, f32[96,128]{1,0:T(8,128)S(1)}, u32[]{:S(2)}, u32[]{:S(2)}) collective-permute-start(f32[96,128]{1,0:T(8,128)S(1)} %fusion), channel_id=1, source_target_pairs={{0,16},{4,20},{8,24},{12,28},{16,0},{20,4},{24,8},{28,12},{1,17},{... | collective-permute-start | bytes 147464 | tf_op jit(solution)/shard_map/ppermute | solution.py:276
  41.2 5.0 %collective-permute-start.13 = (f32[96,128]{1,0:T(8,128)S(1)}, f32[96,128]{1,0:T(8,128)S(1)}, u32[]{:S(2)}, u32[]{:S(2)}) collective-permute-start(f32[96,128]{1,0:T(8,128)S(1)} %fusion), channel_id=1, source_target_pairs={{0,8},{4,12},{8,0},{12,4},{16,24},{20,28},{24,16},{28,20},{1,9},{5... | collective-permute-start | bytes 147464 | tf_op jit(solution)/shard_map/ppermute | solution.py:276
  41.8 4.4 %collective-permute-start.16 = (bf16[64,2048]{1,0:T(8,128)(2,1)S(1)}, bf16[64,2048]{1,0:T(8,128)(2,1)S(1)}, u32[]{:S(2)}, u32[]{:S(2)}) collective-permute-start(bf16[64,2048]{1,0:T(8,128)(2,1)S(1)} %shard_map.71.d0), channel_id=1, source_target_pairs={{0,1},{1,0},{2,3},{3,2},{4,5},{5,4},{6,7},{7,6},{8,9},{9,8},{10,11... | collective-permute-start | bytes 786440 | tf_op jit(solution)/shard_map/ppermute | solution.py:242
  43.0 3.2 %collective-permute-start.18 = (bf16[64,2048]{1,0:T(8,128)(2,1)S(1)}, bf16[64,2048]{1,0:T(8,128)(2,1)S(1)}, u32[]{:S(2)}, u32[]{:S(2)}) collective-permute-start(bf16[64,2048]{1,0:T(8,128)(2,1)S(1)} %collective-permute-done.17.d2), channel_id=1, source_target_pairs={{0,1},{1,0},{2,3},{3,2},{4,5},{5,4},{6,7},{7,6},{8,9},{9,8},{10,11... | collective-permute-start | bytes 786440 | tf_op jit(solution)/shard_map/ppermute | solution.py:242

commit v6 on v5

--- a/solution.py
+++ b/solution.py
@@ -183,7 +183,7 @@
     aug = jnp.concatenate([dot_last(arch, arch), jnp.zeros((n, TILE - n), jnp.float32)], axis=1)
     aug = aug + jnp.where(row + n == col, 1.0, 0.0)
     diagonal = jnp.zeros(shape, jnp.float32)
-    group = 8
+    group = 16
     for start in range(0, n, group):
         columns = [splat(aug[:, start + m:start + m + 1], shape) for m in range(group)]
         for m in range(group):

time: 49.2 us -> 48.9 us (level)
  no operation moved by 1% of the time
where the time goes in v6:
time: 48.9 us; the launch traced here: 48.7 us
  starting transfers between devices  26.1 us (53%)
  waiting for transfers between devices  10.6 us (22%)
  Pallas kernels  9.06 us (19%)
  local copies, waits for them, and re-layouts  1.19 us (2%)
  other arithmetic  1 us (2%)
  between operations  0.8 us (2%)
    ppermute x3, starting transfers between devices, exchange(): lax.ppermute(matrix, 'cells', pairs)  11 us
    pallas_call x5, Pallas kernels, call(): pl.pallas_call(kernel, out_shape=out_shape, in_specs=[spec[k] for k in ki...  9.06 us
    ppermute x4, starting transfers between devices, on_device(): lax.ppermute(x, 'cells', [(i, i ^ bits) for i in range(size)])  7.59 us
    ppermute x9, starting transfers between devices, flip_feat(): lax.ppermute(x, 'feat', [(i, i ^ bits) for i in range(lax.axis_size('feat...  5.44 us
    ppermute x4, waiting for transfers between devices, on_device(): lax.ppermute(x, 'cells', [(i, i ^ bits) for i in range(size)])  3.88 us
    ppermute x3, waiting for transfers between devices, exchange(): lax.ppermute(matrix, 'cells', pairs)  3.44 us
    ppermute x9, waiting for transfers between devices, flip_feat(): lax.ppermute(x, 'feat', [(i, i ^ bits) for i in range(lax.axis_size('feat...  3.27 us
    ppermute x3, starting transfers between devices, exchange(): lax.ppermute(matrix, 'cells', others)  1.99 us
  transfers between devices with their start and end apart: 19, of which 8 were waited for; matrix products, arithmetic and copies ran while one was open for 2% of the time, Pallas kernels for 13%

profile of v6, /device:TPU:0, one launch (start us, length us, event | category | flops | bytes accessed | tf_op | source)
XLA Modules:
  0.0 48.7 jit_solution(6111588794638206034)
XLA Ops:
  0.6 3.0 %collective-permute-start.3 = (bf16[64,2048]{1,0:T(8,128)(2,1)}, bf16[64,2048]{1,0:T(8,128)(2,1)S(1)}, u32[]{:S(2)}, u32[]{:S(2)}) collective-permute-start(bf16[64,2048]{1,0:T(8,128)(2,1)} %v_ref.1), channel_id=1, source_target_pairs={{0,4},{4,0},{8,12},{12,8},{16,20},{20,16},{24,28},{28,24},{1,5},{5... | collective-permute-start | bytes 786440 | tf_op jit(solution)/shard_map/ppermute | solution.py:238
  3.7 0.7 %collective-permute-start = (bf16[64,2048]{1,0:T(8,128)(2,1)}, bf16[64,2048]{1,0:T(8,128)(2,1)S(1)}, u32[]{:S(2)}, u32[]{:S(2)}) collective-permute-start(bf16[64,2048]{1,0:T(8,128)(2,1)} %v_ref.1), channel_id=1, source_target_pairs={{4,8},{12,16},{20,24},{8,4},{16,12},{24,20},{5,9},{13,17},{21,25},... | collective-permute-start | bytes 786440 | tf_op jit(solution)/shard_map/ppermute | solution.py:238
  4.4 0.9 %pad_add_fusion.info_ref.table_ref = s32[11,128]{1,0:T(8,128)S(1)} fusion(s32[1,3]{1,0:T(1,128)S(1)} %add_bitcast_fusion, s32[1,16]{1,0:T(1,128)} %bitcast.9, s32[1,48]{1,0:T(1,128)} %bitcast.10, s32[8,16]{1,0:T(8,128)} %bitcast.8), kind=kLoop, calls=%fused_computation.3 | loop fusion | flops 4224 | bytes 6412 | tf_op jit(solution)/shard_map/concatenate | solution.py:255
  5.3 1.2 %copy-done.1 = bf16[64,2048]{1,0:T(8,128)(2,1)S(1)} copy-done((bf16[64,2048]{1,0:T(8,128)(2,1)S(1)}, bf16[64,2048]{1,0:T(8,128)(2,1)}, u32[]{:S(2)}) %copy-start.1) | copy-done | bytes 262168
  6.5 1.8 %shard_map.68 = (bf16[48,384]{1,0:T(8,128)(2,1)S(1)}, bf16[64,2048]{1,0:T(8,128)(2,1)S(1)}) custom-call(s32[11,128]{1,0:T(8,128)S(1)} %pad_add_fusion.info_ref.table_ref, s32[11,128]{1,0:T(8,128)S(1)} %pad_add_fusion.info_ref.table_ref, bf16[16,8,128,128]{3,2,1,0:T(8,128)(2,1)} %tiles_ref.5, bf16[64,2048]{1,0:T(8,128)(2,1)S(1)} %copy-done.1), custom_call_target="tpu_custom_call" | custom-call | tf_op jit(solution)/shard_map/pallas_call | solution.py:222
  9.0 5.6 %collective-permute-start.1 = (bf16[48,384]{1,0:T(8,128)(2,1)S(1)}, bf16[48,384]{1,0:T(8,128)(2,1)S(1)}, u32[]{:S(2)}, u32[]{:S(2)}) collective-permute-start(bf16[48,384]{1,0:T(8,128)(2,1)S(1)} %get-tuple-element.15), channel_id=1, source_target_pairs={{0,4},{4,0},{8,12},{12,8},{16,20},{20,16},{24,28},{28,24},{1,5},{5... | collective-permute-start | bytes 110600 | tf_op jit(solution)/shard_map/ppermute | solution.py:238
  14.6 1.4 %collective-permute-done.3.pair_ref = bf16[64,2048]{1,0:T(8,128)(2,1)S(1)} collective-permute-done((bf16[64,2048]{1,0:T(8,128)(2,1)}, bf16[64,2048]{1,0:T(8,128)(2,1)S(1)}, u32[]{:S(2)}, u32[]{:S(2)}) %collective-permute-start.3) | collective-permute-done | bytes 262176 | tf_op jit(solution)/shard_map/ppermute | solution.py:238
  16.0 2.0 %shard_map.69 = (bf16[64,2048]{1,0:T(8,128)(2,1)S(1)}, f32[16,8,128]{2,1,0:T(8,128)S(1)}) custom-call(s32[11,128]{1,0:T(8,128)S(1)} %pad_add_fusion.info_ref.table_ref, bf16[16,8,128,128]{3,2,1,0:T(8,128)(2,1)S(1)} %copy-done, bf16[64,2048]{1,0:T(8,128)(2,1)S(1)} %get-tuple-element.16.own_ref, bf16[64,2048]{1,0:T(8,128)(2,1)S(1)} %collective-permute-done.other_ref, ...), custom_call_target="tpu_custom_call" | custom-call | flops 268435456 | bytes 4194304 | tf_op jit(solution)/shard_map/pallas_call | solution.py:222
  18.0 2.4 %collective-permute-start.11 = (bf16[64,2048]{1,0:T(8,128)(2,1)S(1)}, bf16[64,2048]{1,0:T(8,128)(2,1)S(1)}, u32[]{:S(2)}, u32[]{:S(2)}) collective-permute-start(bf16[64,2048]{1,0:T(8,128)(2,1)S(1)} %get-tuple-element.17.v_ref.own_ref), channel_id=1, source_target_pairs={{0,4},{4,0},{8,12},{12,8},{16,20},{20,16},{24,28},{28,24},{1,5},{5... | collective-permute-start | bytes 786440 | tf_op jit(solution)/shard_map/ppermute | solution.py:238
  20.4 0.7 %collective-permute-start.10 = (bf16[64,2048]{1,0:T(8,128)(2,1)S(1)}, bf16[64,2048]{1,0:T(8,128)(2,1)S(1)}, u32[]{:S(2)}, u32[]{:S(2)}) collective-permute-start(bf16[64,2048]{1,0:T(8,128)(2,1)S(1)} %get-tuple-element.17.v_ref.own_ref), channel_id=1, source_target_pairs={{4,8},{12,16},{20,24},{8,4},{16,12},{24,20},{5,9},{13,17},{21,25},... | collective-permute-start | bytes 786440 | tf_op jit(solution)/shard_map/ppermute | solution.py:238
  21.2 1.6 %collective-permute-start.5 = (bf16[48,256]{1,0:T(8,128)(2,1)S(1)}, bf16[48,256]{1,0:T(8,128)(2,1)S(1)}, u32[]{:S(2)}, u32[]{:S(2)}) collective-permute-start(bf16[48,256]{1,0:T(8,128)(2,1)S(1)} %slice.2), channel_id=1, source_target_pairs={{0,2},{1,3},{2,0},{3,1},{4,6},{5,7},{6,4},{7,5},{8,10},{9,11},{10,... | collective-permute-start | bytes 73736 | tf_op jit(solution)/shard_map/ppermute | solution.py:242
  23.1 1.6 %collective-permute-done.6.r3 = bf16[48,256]{1,0:T(8,128)(2,1)S(1)} collective-permute-done((bf16[48,256]{1,0:T(8,128)(2,1)S(1)}, bf16[48,256]{1,0:T(8,128)(2,1)S(1)}, u32[]{:S(2)}, u32[]{:S(2)}) %collective-permute-start.6) | collective-permute-done | bytes 24608 | tf_op jit(solution)/shard_map/ppermute | solution.py:242
  25.1 0.8 %shard_map.70.extra_ref = f32[24,128]{1,0:T(8,128)S(1)} custom-call(s32[11,128]{1,0:T(8,128)S(1)} %pad_add_fusion.info_ref.table_ref, s32[11,128]{1,0:T(8,128)S(1)} %pad_add_fusion.info_ref.table_ref, bf16[48,384]{1,0:T(8,128)(2,1)S(1)} %add_add_fusion.1.r0, bf16[48,256]{1,0:T(8,128)(2,1)S(1)} %collective-permute-done.4.r1, ...), custom_call_target="tpu_custom_call" | custom-call | tf_op jit(solution)/shard_map/pallas_call | solution.py:222
  25.9 0.8 %collective-permute-start.9 = (f32[24,128]{1,0:T(8,128)S(1)}, f32[24,128]{1,0:T(8,128)S(1)}, u32[]{:S(2)}, u32[]{:S(2)}) collective-permute-start(f32[24,128]{1,0:T(8,128)S(1)} %shard_map.70.extra_ref), channel_id=1, source_target_pairs={{0,3},{1,2},{2,1},{3,0},{4,7},{5,6},{6,5},{7,4},{8,11},{9,10},{10,... | collective-permute-start | bytes 36872 | tf_op jit(solution)/shard_map/ppermute | solution.py:242
  26.7 1.2 %collective-permute-start.8 = (f32[24,128]{1,0:T(8,128)S(1)}, f32[24,128]{1,0:T(8,128)S(1)}, u32[]{:S(2)}, u32[]{:S(2)}) collective-permute-start(f32[24,128]{1,0:T(8,128)S(1)} %shard_map.70.extra_ref), channel_id=1, source_target_pairs={{0,2},{1,3},{2,0},{3,1},{4,6},{5,7},{6,4},{7,5},{8,10},{9,11},{10,... | collective-permute-start | bytes 36872 | tf_op jit(solution)/shard_map/ppermute | solution.py:242
  27.9 2.0 %collective-permute-done.11.pair_ref = bf16[64,2048]{1,0:T(8,128)(2,1)S(1)} collective-permute-done((bf16[64,2048]{1,0:T(8,128)(2,1)S(1)}, bf16[64,2048]{1,0:T(8,128)(2,1)S(1)}, u32[]{:S(2)}, u32[]{:S(2)}) %collective-permute-start.11) | collective-permute-done | bytes 262176 | tf_op jit(solution)/shard_map/ppermute | solution.py:238
  29.9 2.0 %shard_map.71.d0 = bf16[64,2048]{1,0:T(8,128)(2,1)S(1)} custom-call(s32[11,128]{1,0:T(8,128)S(1)} %pad_add_fusion.info_ref.table_ref, bf16[16,8,128,128]{3,2,1,0:T(8,128)(2,1)S(1)} %copy-done, bf16[64,2048]{1,0:T(8,128)(2,1)S(1)} %get-tuple-element.17.v_ref.own_ref, bf16[64,2048]{1,0:T(8,128)(2,1)S(1)} %collective-permute-done.10.other_ref, ...), custom_call_target="tpu_custom_call" | custom-call | flops 4294967296 | tf_op jit(solution)/shard_map/pallas_call | solution.py:222
  32.0 2.8 %collective-permute-start.12 = (f32[96,128]{1,0:T(8,128)S(1)}, f32[96,128]{1,0:T(8,128)S(1)}, u32[]{:S(2)}, u32[]{:S(2)}) collective-permute-start(f32[96,128]{1,0:T(8,128)S(1)} %pad_maximum_fusion), channel_id=1, source_target_pairs={{0,4},{4,0},{8,12},{12,8},{16,20},{20,16},{24,28},{28,24},{1,5},{5... | collective-permute-start | bytes 147464 | tf_op jit(solution)/shard_map/ppermute | solution.py:276
  34.7 1.5 %collective-permute-start.17 = (bf16[64,2048]{1,0:T(8,128)(2,1)S(1)}, bf16[64,2048]{1,0:T(8,128)(2,1)S(1)}, u32[]{:S(2)}, u32[]{:S(2)}) collective-permute-start(bf16[64,2048]{1,0:T(8,128)(2,1)S(1)} %shard_map.71.d0), channel_id=1, source_target_pairs={{0,2},{1,3},{2,0},{3,1},{4,6},{5,7},{6,4},{7,5},{8,10},{9,11},{10,... | collective-permute-start | bytes 786440 | tf_op jit(solution)/shard_map/ppermute | solution.py:242
  36.2 0.7 %collective-permute-done.12 = f32[96,128]{1,0:T(8,128)S(1)} collective-permute-done((f32[96,128]{1,0:T(8,128)S(1)}, f32[96,128]{1,0:T(8,128)S(1)}, u32[]{:S(2)}, u32[]{:S(2)}) %collective-permute-start.12) | collective-permute-done | bytes 49184 | tf_op jit(solution)/shard_map/ppermute | solution.py:276
  37.0 4.2 %collective-permute-start.15 = (f32[96,128]{1,0:T(8,128)S(1)}, f32[96,128]{1,0:T(8,128)S(1)}, u32[]{:S(2)}, u32[]{:S(2)}) collective-permute-start(f32[96,128]{1,0:T(8,128)S(1)} %fusion), channel_id=1, source_target_pairs={{0,24},{4,28},{8,16},{12,20},{16,8},{20,12},{24,0},{28,4},{1,25},{... | collective-permute-start | bytes 147464 | tf_op jit(solution)/shard_map/ppermute | solution.py:276
  41.8 1.2 %collective-permute-done.17.d2 = bf16[64,2048]{1,0:T(8,128)(2,1)S(1)} collective-permute-done((bf16[64,2048]{1,0:T(8,128)(2,1)S(1)}, bf16[64,2048]{1,0:T(8,128)(2,1)S(1)}, u32[]{:S(2)}, u32[]{:S(2)}) %collective-permute-start.17) | collective-permute-done | bytes 262176 | tf_op jit(solution)/shard_map/ppermute | solution.py:242
  43.2 2.9 %collective-permute-done.14 = f32[96,128]{1,0:T(8,128)S(1)} collective-permute-done((f32[96,128]{1,0:T(8,128)S(1)}, f32[96,128]{1,0:T(8,128)S(1)}, u32[]{:S(2)}, u32[]{:S(2)}) %collective-permute-start.14) | collective-permute-done | bytes 49184 | tf_op jit(solution)/shard_map/ppermute | solution.py:276
  46.2 2.5 %shard_map.72 = (f32[48,2048]{1,0:T(8,128)}, bf16[64,2048]{1,0:T(8,128)(2,1)}) custom-call(s32[11,128]{1,0:T(8,128)S(1)} %pad_add_fusion.info_ref.table_ref, f32[96,128]{1,0:T(8,128)S(1)} %add_add_fusion.total_ref, bf16[64,2048]{1,0:T(8,128)(2,1)S(1)} %shard_map.71.d0, bf16[64,2048]{1,0:T(8,128)(2,1)S(1)} %collective-permute-done.16.d1, ...), custom_call_target="tpu_custom_call" | custom-call | flops 100663296 | bytes 393216 | tf_op jit(solution)/shard_map/pallas_call | solution.py:222
  (30 shorter events, 2.5 us)
Async XLA Ops:
  0.6 15.4 %collective-permute-start.3 = (bf16[64,2048]{1,0:T(8,128)(2,1)}, bf16[64,2048]{1,0:T(8,128)(2,1)S(1)}, u32[]{:S(2)}, u32[]{:S(2)}) collective-permute-start(bf16[64,2048]{1,0:T(8,128)(2,1)} %v_ref.1), channel_id=1, source_target_pairs={{0,4},{4,0},{8,12},{12,8},{16,20},{20,16},{24,28},{28,24},{1,5},{5... | collective-permute-start | bytes 786440 | tf_op jit(solution)/shard_map/ppermute | solution.py:238
  3.7 12.3 %collective-permute-start = (bf16[64,2048]{1,0:T(8,128)(2,1)}, bf16[64,2048]{1,0:T(8,128)(2,1)S(1)}, u32[]{:S(2)}, u32[]{:S(2)}) collective-permute-start(bf16[64,2048]{1,0:T(8,128)(2,1)} %v_ref.1), channel_id=1, source_target_pairs={{4,8},{12,16},{20,24},{8,4},{16,12},{24,20},{5,9},{13,17},{21,25},... | collective-permute-start | bytes 786440 | tf_op jit(solution)/shard_map/ppermute | solution.py:238
  4.3 11.6 %copy-start = (bf16[16,8,128,128]{3,2,1,0:T(8,128)(2,1)S(1)}, bf16[16,8,128,128]{3,2,1,0:T(8,128)(2,1)}, u32[]{:S(2)}) copy-start(bf16[16,8,128,128]{3,2,1,0:T(8,128)(2,1)} %tiles_ref.5) | copy-start | bytes 12582916
  5.3 1.2 %copy-start.1 = (bf16[64,2048]{1,0:T(8,128)(2,1)S(1)}, bf16[64,2048]{1,0:T(8,128)(2,1)}, u32[]{:S(2)}) copy-start(bf16[64,2048]{1,0:T(8,128)(2,1)} %v_ref.1) | copy-start | bytes 786436
  8.3 12.8 %collective-permute-start.2 = (bf16[48,384]{1,0:T(8,128)(2,1)S(1)}, bf16[48,384]{1,0:T(8,128)(2,1)S(1)}, u32[]{:S(2)}, u32[]{:S(2)}) collective-permute-start(bf16[48,384]{1,0:T(8,128)(2,1)S(1)} %get-tuple-element.15), channel_id=1, source_target_pairs={{4,8},{12,16},{20,24},{8,4},{16,12},{24,20},{5,9},{13,17},{21,25},... | collective-permute-start | bytes 110600 | tf_op jit(solution)/shard_map/ppermute | solution.py:238
  9.0 12.1 %collective-permute-start.1 = (bf16[48,384]{1,0:T(8,128)(2,1)S(1)}, bf16[48,384]{1,0:T(8,128)(2,1)S(1)}, u32[]{:S(2)}, u32[]{:S(2)}) collective-permute-start(bf16[48,384]{1,0:T(8,128)(2,1)S(1)} %get-tuple-element.15), channel_id=1, source_target_pairs={{0,4},{4,0},{8,12},{12,8},{16,20},{20,16},{24,28},{28,24},{1,5},{5... | collective-permute-start | bytes 110600 | tf_op jit(solution)/shard_map/ppermute | solution.py:238
  18.0 11.9 %collective-permute-start.11 = (bf16[64,2048]{1,0:T(8,128)(2,1)S(1)}, bf16[64,2048]{1,0:T(8,128)(2,1)S(1)}, u32[]{:S(2)}, u32[]{:S(2)}) collective-permute-start(bf16[64,2048]{1,0:T(8,128)(2,1)S(1)} %get-tuple-element.17.v_ref.own_ref), channel_id=1, source_target_pairs={{0,4},{4,0},{8,12},{12,8},{16,20},{20,16},{24,28},{28,24},{1,5},{5... | collective-permute-start | bytes 786440 | tf_op jit(solution)/shard_map/ppermute | solution.py:238
  20.4 9.5 %collective-permute-start.10 = (bf16[64,2048]{1,0:T(8,128)(2,1)S(1)}, bf16[64,2048]{1,0:T(8,128)(2,1)S(1)}, u32[]{:S(2)}, u32[]{:S(2)}) collective-permute-start(bf16[64,2048]{1,0:T(8,128)(2,1)S(1)} %get-tuple-element.17.v_ref.own_ref), channel_id=1, source_target_pairs={{4,8},{12,16},{20,24},{8,4},{16,12},{24,20},{5,9},{13,17},{21,25},... | collective-permute-start | bytes 786440 | tf_op jit(solution)/shard_map/ppermute | solution.py:238
  21.1 3.5 %collective-permute-start.6 = (bf16[48,256]{1,0:T(8,128)(2,1)S(1)}, bf16[48,256]{1,0:T(8,128)(2,1)S(1)}, u32[]{:S(2)}, u32[]{:S(2)}) collective-permute-start(bf16[48,256]{1,0:T(8,128)(2,1)S(1)} %slice.2), channel_id=1, source_target_pairs={{0,3},{1,2},{2,1},{3,0},{4,7},{5,6},{6,5},{7,4},{8,11},{9,10},{10,... | collective-permute-start | bytes 73736 | tf_op jit(solution)/shard_map/ppermute | solution.py:242
  21.2 3.9 %collective-permute-start.5 = (bf16[48,256]{1,0:T(8,128)(2,1)S(1)}, bf16[48,256]{1,0:T(8,128)(2,1)S(1)}, u32[]{:S(2)}, u32[]{:S(2)}) collective-permute-start(bf16[48,256]{1,0:T(8,128)(2,1)S(1)} %slice.2), channel_id=1, source_target_pairs={{0,2},{1,3},{2,0},{3,1},{4,6},{5,7},{6,4},{7,5},{8,10},{9,11},{10,... | collective-permute-start | bytes 73736 | tf_op jit(solution)/shard_map/ppermute | solution.py:242
  22.8 2.3 %collective-permute-start.4 = (bf16[48,256]{1,0:T(8,128)(2,1)S(1)}, bf16[48,256]{1,0:T(8,128)(2,1)S(1)}, u32[]{:S(2)}, u32[]{:S(2)}) collective-permute-start(bf16[48,256]{1,0:T(8,128)(2,1)S(1)} %slice.2), channel_id=1, source_target_pairs={{0,1},{1,0},{2,3},{3,2},{4,5},{5,4},{6,7},{7,6},{8,9},{9,8},{10,11... | collective-permute-start | bytes 73736 | tf_op jit(solution)/shard_map/ppermute | solution.py:242
  25.9 6.1 %collective-permute-start.9 = (f32[24,128]{1,0:T(8,128)S(1)}, f32[24,128]{1,0:T(8,128)S(1)}, u32[]{:S(2)}, u32[]{:S(2)}) collective-permute-start(f32[24,128]{1,0:T(8,128)S(1)} %shard_map.70.extra_ref), channel_id=1, source_target_pairs={{0,3},{1,2},{2,1},{3,0},{4,7},{5,6},{6,5},{7,4},{8,11},{9,10},{10,... | collective-permute-start | bytes 36872 | tf_op jit(solution)/shard_map/ppermute | solution.py:242
  26.7 5.2 %collective-permute-start.8 = (f32[24,128]{1,0:T(8,128)S(1)}, f32[24,128]{1,0:T(8,128)S(1)}, u32[]{:S(2)}, u32[]{:S(2)}) collective-permute-start(f32[24,128]{1,0:T(8,128)S(1)} %shard_map.70.extra_ref), channel_id=1, source_target_pairs={{0,2},{1,3},{2,0},{3,1},{4,6},{5,7},{6,4},{7,5},{8,10},{9,11},{10,... | collective-permute-start | bytes 36872 | tf_op jit(solution)/shard_map/ppermute | solution.py:242
  27.9 4.0 %collective-permute-start.7 = (f32[24,128]{1,0:T(8,128)S(1)}, f32[24,128]{1,0:T(8,128)S(1)}, u32[]{:S(2)}, u32[]{:S(2)}) collective-permute-start(f32[24,128]{1,0:T(8,128)S(1)} %shard_map.70.extra_ref), channel_id=1, source_target_pairs={{0,1},{1,0},{2,3},{3,2},{4,5},{5,4},{6,7},{7,6},{8,9},{9,8},{10,11... | collective-permute-start | bytes 36872 | tf_op jit(solution)/shard_map/ppermute | solution.py:242
  32.0 5.0 %collective-permute-start.12 = (f32[96,128]{1,0:T(8,128)S(1)}, f32[96,128]{1,0:T(8,128)S(1)}, u32[]{:S(2)}, u32[]{:S(2)}) collective-permute-start(f32[96,128]{1,0:T(8,128)S(1)} %pad_maximum_fusion), channel_id=1, source_target_pairs={{0,4},{4,0},{8,12},{12,8},{16,20},{20,16},{24,28},{28,24},{1,5},{5... | collective-permute-start | bytes 147464 | tf_op jit(solution)/shard_map/ppermute | solution.py:276
  34.7 8.2 %collective-permute-start.17 = (bf16[64,2048]{1,0:T(8,128)(2,1)S(1)}, bf16[64,2048]{1,0:T(8,128)(2,1)S(1)}, u32[]{:S(2)}, u32[]{:S(2)}) collective-permute-start(bf16[64,2048]{1,0:T(8,128)(2,1)S(1)} %shard_map.71.d0), channel_id=1, source_target_pairs={{0,2},{1,3},{2,0},{3,1},{4,6},{5,7},{6,4},{7,5},{8,10},{9,11},{10,... | collective-permute-start | bytes 786440 | tf_op jit(solution)/shard_map/ppermute | solution.py:242
  37.0 6.2 %collective-permute-start.15 = (f32[96,128]{1,0:T(8,128)S(1)}, f32[96,128]{1,0:T(8,128)S(1)}, u32[]{:S(2)}, u32[]{:S(2)}) collective-permute-start(f32[96,128]{1,0:T(8,128)S(1)} %fusion), channel_id=1, source_target_pairs={{0,24},{4,28},{8,16},{12,20},{16,8},{20,12},{24,0},{28,4},{1,25},{... | collective-permute-start | bytes 147464 | tf_op jit(solution)/shard_map/ppermute | solution.py:276
  41.1 5.0 %collective-permute-start.14 = (f32[96,128]{1,0:T(8,128)S(1)}, f32[96,128]{1,0:T(8,128)S(1)}, u32[]{:S(2)}, u32[]{:S(2)}) collective-permute-start(f32[96,128]{1,0:T(8,128)S(1)} %fusion), channel_id=1, source_target_pairs={{0,16},{4,20},{8,24},{12,28},{16,0},{20,4},{24,8},{28,12},{1,17},{... | collective-permute-start | bytes 147464 | tf_op jit(solution)/shard_map/ppermute | solution.py:276
  41.1 5.0 %collective-permute-start.13 = (f32[96,128]{1,0:T(8,128)S(1)}, f32[96,128]{1,0:T(8,128)S(1)}, u32[]{:S(2)}, u32[]{:S(2)}) collective-permute-start(f32[96,128]{1,0:T(8,128)S(1)} %fusion), channel_id=1, source_target_pairs={{0,8},{4,12},{8,0},{12,4},{16,24},{20,28},{24,16},{28,20},{1,9},{5... | collective-permute-start | bytes 147464 | tf_op jit(solution)/shard_map/ppermute | solution.py:276
  41.8 4.4 %collective-permute-start.16 = (bf16[64,2048]{1,0:T(8,128)(2,1)S(1)}, bf16[64,2048]{1,0:T(8,128)(2,1)S(1)}, u32[]{:S(2)}, u32[]{:S(2)}) collective-permute-start(bf16[64,2048]{1,0:T(8,128)(2,1)S(1)} %shard_map.71.d0), channel_id=1, source_target_pairs={{0,1},{1,0},{2,3},{3,2},{4,5},{5,4},{6,7},{7,6},{8,9},{9,8},{10,11... | collective-permute-start | bytes 786440 | tf_op jit(solution)/shard_map/ppermute | solution.py:242
  43.0 3.2 %collective-permute-start.18 = (bf16[64,2048]{1,0:T(8,128)(2,1)S(1)}, bf16[64,2048]{1,0:T(8,128)(2,1)S(1)}, u32[]{:S(2)}, u32[]{:S(2)}) collective-permute-start(bf16[64,2048]{1,0:T(8,128)(2,1)S(1)} %collective-permute-done.17.d2), channel_id=1, source_target_pairs={{0,1},{1,0},{2,3},{3,2},{4,5},{5,4},{6,7},{7,6},{8,9},{9,8},{10,11... | collective-permute-start | bytes 786440 | tf_op jit(solution)/shard_map/ppermute | solution.py:242

commit v7 on v6

--- a/solution.py
+++ b/solution.py
@@ -11,7 +11,6 @@
 NBT = 8
 EPS = 1e-05
 ARCH, COUNTS, META = range(NBT, NBT + 3)
-OWN, PAIR, OTHER = range(1, 4)
 
 VMEM = pl.BlockSpec(memory_space=pltpu.VMEM)
 ANY = pl.BlockSpec(memory_space=pl.ANY)
@@ -77,52 +76,56 @@
     whole.wait()
 
 
-def slot_codes(info_ref, blocks):
+def slot_places(info_ref, blocks):
     shape = (NBT, TILE)
     local = info_ref[:NBT] - info_ref[META:META + 1, :1]
     odd = jnp.broadcast_to(info_ref[META:META + 1, 1:2], shape)
     counts = jnp.broadcast_to(info_ref[COUNTS:COUNTS + 1], shape)
-    below = jnp.where(odd == 1, PAIR, OTHER)
-    side = jnp.where(local < 0, below, jnp.where(local >= blocks, PAIR + OTHER - below, OWN))
-    at = jnp.where(local < 0, local + blocks, jnp.where(local >= blocks, local - blocks, local))
+    below = jnp.where(odd == 1, 1, 2)
+    lower, upper = local + (below + 1) * blocks, local - blocks + (3 - below) * blocks
+    at = jnp.where(local < 0, lower, jnp.where(local >= blocks, upper, local))
     used = lax.broadcasted_iota(jnp.int32, shape, 0) < counts
-    return jnp.where(used, side, 0) * blocks + at
-
-
-def step_block(codes, tiles_ref, own_ref, pair_ref, other_ref, b, with_degree):
+    return jnp.where(used, at, 3 * blocks)
+
+
+def side_by_side(all_ref, own_ref, pair_ref, other_ref):
+    width = own_ref.shape[1]
+    for i, ref in enumerate((own_ref, pair_ref, other_ref)):
+        all_ref[:, i * width:(i + 1) * width] = ref[...]
+    all_ref[:, 3 * width:] = jnp.zeros_like(all_ref[:, 3 * width:])
+
+
+def step_block(places, tiles_ref, own_ref, all_ref, b, with_degree):
     blocks = tiles_ref.shape[0]
     parts, ones = [], []
     for j in range(NBT):
-        code = codes[j, b]
-        side, at = lax.div(code, blocks), lanes(lax.rem(code, blocks))
-        x = own_ref[:, at]
-        if j > 0:
-            beside = jnp.where(side == PAIR, pair_ref[:, at], other_ref[:, at])
-            x = beside if j < 3 else jnp.where(side == OWN, x, beside)
-        if j >= 3:
-            x = jnp.where(side > 0, x, jnp.zeros_like(x))
-        parts.append(x)
-        ones.append(jnp.full((16, TILE), jnp.where(side > 0, 1.0, 0.0), jnp.float32).astype(jnp.bfloat16))
+        at = places[j, b]
+        parts.append(all_ref[:, lanes(at)] if j else own_ref[:, b * TILE:(b + 1) * TILE])
+        if with_degree:
+            used = jnp.where(at < 3 * blocks, 1.0, 0.0)
+            ones.append(jnp.full((16, TILE), used, jnp.float32).astype(jnp.bfloat16))
     lhs = jnp.concatenate(parts, axis=1)
     if with_degree:
         lhs = jnp.concatenate([lhs, jnp.concatenate(ones, axis=1)], axis=0)
-    return dot_last(lhs, jnp.concatenate([tiles_ref[b, j] for j in range(NBT)], axis=1))
-
-
-def first_kernel(info_ref, tiles_ref, own_ref, other_ref, pair_ref, out_ref, inv_ref):
+    return dot_last(lhs, wide_tile(tiles_ref, b, range(NBT)))
+
+
+def first_kernel(info_ref, tiles_ref, own_ref, other_ref, pair_ref, out_ref, inv_ref, all_ref):
     feats = own_ref.shape[0]
-    codes = slot_codes(info_ref, tiles_ref.shape[0])
+    places = slot_places(info_ref, tiles_ref.shape[0])
+    side_by_side(all_ref, own_ref, pair_ref, other_ref)
     for b in range(tiles_ref.shape[0]):
-        out = step_block(codes, tiles_ref, own_ref, pair_ref, other_ref, b, True)
+        out = step_block(places, tiles_ref, own_ref, all_ref, b, True)
         inv = 1.0 / out[feats:feats + 8]
         inv_ref[b] = inv
         out_ref[:, b * TILE:(b + 1) * TILE] = (out[:feats] * inv[:1]).astype(jnp.bfloat16)
 
 
-def second_kernel(info_ref, tiles_ref, own_ref, other_ref, pair_ref, inv_ref, extra_ref, out_ref):
-    codes = slot_codes(info_ref, tiles_ref.shape[0])
+def second_kernel(info_ref, tiles_ref, own_ref, other_ref, pair_ref, inv_ref, extra_ref, out_ref, all_ref):
+    places = slot_places(info_ref, tiles_ref.shape[0])
+    side_by_side(all_ref, own_ref, pair_ref, other_ref)
     for b in range(tiles_ref.shape[0]):
-        out = step_block(codes, tiles_ref, own_ref, pair_ref, other_ref, b, False)
+        out = step_block(places, tiles_ref, own_ref, all_ref, b, False)
         out_ref[:, b * TILE:(b + 1) * TILE] = (out * inv_ref[b][:1]).astype(jnp.bfloat16)
 
 
@@ -260,8 +263,9 @@
     arch_rows, own = call(rows_kernel, [shape((narch, 3 * TILE), bf16), shape((feats, rows), bf16)], "vvhh",
                      (info, info, tiles, expression), 0, 0,
                      [pltpu.VMEM((blocks, 2, TILE, TILE), bf16), pltpu.SemaphoreType.DMA((3,))], 52)
+    every = [pltpu.VMEM((feats, 3 * rows + TILE), bf16)]
     first, inv = call(first_kernel, [shape((feats, rows), bf16), shape((blocks, 8, TILE), f32)], "vvvvv",
-                      (info, tiles, own, other, pair), flops, nbytes)
+                      (info, tiles, own, other, pair), flops, nbytes, every)
 
     row_pair, row_other = exchange(arch_rows)
     own_rows, _ = lax.optimization_barrier((arch_rows, other))
@@ -270,7 +274,7 @@
     pair, other = exchange(first)
     part = call(arch_kernel, shape((narch // 2, 2 * feats), f32), "vvvvvvv", (info, info, *r, first), 0, 0)
     step = (info, tiles, first, other, pair, inv)
-    diffused = call(second_kernel, shape((feats, rows), bf16), "vvvvvva", (*step, part), flops * 16, 0)
+    diffused = call(second_kernel, shape((feats, rows), bf16), "vvvvvva", (*step, part), flops * 16, 0, every)
     seen, diffused = lax.optimization_barrier(([flip_feat(part, p) for p in (1, 2, 3)], diffused))
     part = jnp.concatenate([part, *seen], axis=0)
     flip_cells = lambda x, bits: lax.ppermute(x, "cells", [(i, i ^ bits) for i in range(size)])
@@ -281,6 +285,7 @@
 
     pieces = [diffused, flip_feat(diffused, 1), flip_feat(diffused, 2)]
     pieces.append(flip_feat(pieces[2], 1))
+    part, pieces[1] = lax.optimization_barrier((part, pieces[1]))
     while level < levels:
         near, far, both = (flip_cells(part, b << level) for b in (1, 2, 3))
         part = (part + near) + (far + both)

time: 48.9 us -> 48.4 us (0.990)
    ppermute x4, waiting for transfers between devices: 3.88 us -> 3.04 us  [on_device(): lax.ppermute(x, 'cells', [(i, i ^ bits) for i in range(size)])]
    ppermute x9, waiting for transfers between devices: 3.27 us -> 3.95 us  [flip_feat(): lax.ppermute(x, 'feat', [(i, i ^ bits) for i in range(lax.axis_size('feat...]
  transfers between devices with their start and end apart: 19 -> 19, of which waited for: 8 -> 7; matrix products, arithmetic and copies ran while one was open for 2% -> 2% of each run, Pallas kernels for 13% -> 13%
where the time goes in v7:
time: 48.4 us; the launch traced here: 48.2 us
  starting transfers between devices  26.2 us (54%)
  waiting for transfers between devices  10.4 us (21%)
  Pallas kernels  8.6 us (18%)
  local copies, waits for them, and re-layouts  1.19 us (2%)
  other arithmetic  1 us (2%)
  between operations  0.79 us (2%)
    ppermute x3, starting transfers between devices, exchange(): lax.ppermute(matrix, 'cells', pairs)  11 us
    pallas_call x5, Pallas kernels, call(): pl.pallas_call(kernel, out_shape=out_shape, in_specs=[spec[k] for k in ki...  8.6 us
    ppermute x4, starting transfers between devices, on_device(): lax.ppermute(x, 'cells', [(i, i ^ bits) for i in range(size)])  7.76 us
    ppermute x9, starting transfers between devices, flip_feat(): lax.ppermute(x, 'feat', [(i, i ^ bits) for i in range(lax.axis_size('feat...  5.43 us
    ppermute x9, waiting for transfers between devices, flip_feat(): lax.ppermute(x, 'feat', [(i, i ^ bits) for i in range(lax.axis_size('feat...  3.95 us
    ppermute x3, waiting for transfers between devices, exchange(): lax.ppermute(matrix, 'cells', pairs)  3.45 us
    ppermute x4, waiting for transfers between devices, on_device(): lax.ppermute(x, 'cells', [(i, i ^ bits) for i in range(size)])  3.04 us
    ppermute x3, starting transfers between devices, exchange(): lax.ppermute(matrix, 'cells', others)  1.99 us
  transfers between devices with their start and end apart: 19, of which 7 were waited for; matrix products, arithmetic and copies ran while one was open for 2% of the time, Pallas kernels for 13%

profile of v7, /device:TPU:0, one launch (start us, length us, event | category | flops | bytes accessed | tf_op | source)
XLA Modules:
  0.0 48.2 jit_solution(7104563220607773524)
XLA Ops:
  0.6 3.0 %collective-permute-start.3 = (bf16[64,2048]{1,0:T(8,128)(2,1)}, bf16[64,2048]{1,0:T(8,128)(2,1)S(1)}, u32[]{:S(2)}, u32[]{:S(2)}) collective-permute-start(bf16[64,2048]{1,0:T(8,128)(2,1)} %v_ref.1), channel_id=1, source_target_pairs={{0,4},{4,0},{8,12},{12,8},{16,20},{20,16},{24,28},{28,24},{1,5},{5... | collective-permute-start | bytes 786440 | tf_op jit(solution)/shard_map/ppermute | solution.py:241
  3.7 0.7 %collective-permute-start = (bf16[64,2048]{1,0:T(8,128)(2,1)}, bf16[64,2048]{1,0:T(8,128)(2,1)S(1)}, u32[]{:S(2)}, u32[]{:S(2)}) collective-permute-start(bf16[64,2048]{1,0:T(8,128)(2,1)} %v_ref.1), channel_id=1, source_target_pairs={{4,8},{12,16},{20,24},{8,4},{16,12},{24,20},{5,9},{13,17},{21,25},... | collective-permute-start | bytes 786440 | tf_op jit(solution)/shard_map/ppermute | solution.py:241
  4.4 0.9 %pad_add_fusion.info_ref.table_ref = s32[11,128]{1,0:T(8,128)S(1)} fusion(s32[1,3]{1,0:T(1,128)S(1)} %add_bitcast_fusion, s32[1,16]{1,0:T(1,128)} %bitcast.9, s32[1,48]{1,0:T(1,128)} %bitcast.10, s32[8,16]{1,0:T(8,128)} %bitcast.8), kind=kLoop, calls=%fused_computation.3 | loop fusion | flops 4224 | bytes 6412 | tf_op jit(solution)/shard_map/concatenate | solution.py:258
  5.3 1.2 %copy-done.1 = bf16[64,2048]{1,0:T(8,128)(2,1)S(1)} copy-done((bf16[64,2048]{1,0:T(8,128)(2,1)S(1)}, bf16[64,2048]{1,0:T(8,128)(2,1)}, u32[]{:S(2)}) %copy-start.1) | copy-done | bytes 262168
  6.5 1.8 %shard_map.68 = (bf16[48,384]{1,0:T(8,128)(2,1)S(1)}, bf16[64,2048]{1,0:T(8,128)(2,1)S(1)}) custom-call(s32[11,128]{1,0:T(8,128)S(1)} %pad_add_fusion.info_ref.table_ref, s32[11,128]{1,0:T(8,128)S(1)} %pad_add_fusion.info_ref.table_ref, bf16[16,8,128,128]{3,2,1,0:T(8,128)(2,1)} %tiles_ref.5, bf16[64,2048]{1,0:T(8,128)(2,1)S(1)} %copy-done.1), custom_call_target="tpu_custom_call" | custom-call | tf_op jit(solution)/shard_map/pallas_call | solution.py:225
  8.3 0.7 %collective-permute-start.2 = (bf16[48,384]{1,0:T(8,128)(2,1)S(1)}, bf16[48,384]{1,0:T(8,128)(2,1)S(1)}, u32[]{:S(2)}, u32[]{:S(2)}) collective-permute-start(bf16[48,384]{1,0:T(8,128)(2,1)S(1)} %get-tuple-element.17), channel_id=1, source_target_pairs={{4,8},{12,16},{20,24},{8,4},{16,12},{24,20},{5,9},{13,17},{21,25},... | collective-permute-start | bytes 110600 | tf_op jit(solution)/shard_map/ppermute | solution.py:241
  9.0 5.6 %collective-permute-start.1 = (bf16[48,384]{1,0:T(8,128)(2,1)S(1)}, bf16[48,384]{1,0:T(8,128)(2,1)S(1)}, u32[]{:S(2)}, u32[]{:S(2)}) collective-permute-start(bf16[48,384]{1,0:T(8,128)(2,1)S(1)} %get-tuple-element.17), channel_id=1, source_target_pairs={{0,4},{4,0},{8,12},{12,8},{16,20},{20,16},{24,28},{28,24},{1,5},{5... | collective-permute-start | bytes 110600 | tf_op jit(solution)/shard_map/ppermute | solution.py:241
  14.6 1.4 %collective-permute-done.3.pair_ref = bf16[64,2048]{1,0:T(8,128)(2,1)S(1)} collective-permute-done((bf16[64,2048]{1,0:T(8,128)(2,1)}, bf16[64,2048]{1,0:T(8,128)(2,1)S(1)}, u32[]{:S(2)}, u32[]{:S(2)}) %collective-permute-start.3) | collective-permute-done | bytes 262176 | tf_op jit(solution)/shard_map/ppermute | solution.py:241
  16.0 1.8 %shard_map.69 = (bf16[64,2048]{1,0:T(8,128)(2,1)S(1)}, f32[16,8,128]{2,1,0:T(8,128)S(1)}) custom-call(s32[11,128]{1,0:T(8,128)S(1)} %pad_add_fusion.info_ref.table_ref, bf16[16,8,128,128]{3,2,1,0:T(8,128)(2,1)S(1)} %copy-done, bf16[64,2048]{1,0:T(8,128)(2,1)S(1)} %get-tuple-element.18.own_ref, bf16[64,2048]{1,0:T(8,128)(2,1)S(1)} %collective-permute-done.other_ref, ...), custom_call_target="tpu_custom_call" | custom-call | flops 268435456 | bytes 4194304 | tf_op jit(solution)/shard_map/pallas_call | solution.py:225
  17.8 2.4 %collective-permute-start.11 = (bf16[64,2048]{1,0:T(8,128)(2,1)S(1)}, bf16[64,2048]{1,0:T(8,128)(2,1)S(1)}, u32[]{:S(2)}, u32[]{:S(2)}) collective-permute-start(bf16[64,2048]{1,0:T(8,128)(2,1)S(1)} %get-tuple-element.19.v_ref.own_ref), channel_id=1, source_target_pairs={{0,4},{4,0},{8,12},{12,8},{16,20},{20,16},{24,28},{28,24},{1,5},{5... | collective-permute-start | bytes 786440 | tf_op jit(solution)/shard_map/ppermute | solution.py:241
  20.2 0.7 %collective-permute-start.10 = (bf16[64,2048]{1,0:T(8,128)(2,1)S(1)}, bf16[64,2048]{1,0:T(8,128)(2,1)S(1)}, u32[]{:S(2)}, u32[]{:S(2)}) collective-permute-start(bf16[64,2048]{1,0:T(8,128)(2,1)S(1)} %get-tuple-element.19.v_ref.own_ref), channel_id=1, source_target_pairs={{4,8},{12,16},{20,24},{8,4},{16,12},{24,20},{5,9},{13,17},{21,25},... | collective-permute-start | bytes 786440 | tf_op jit(solution)/shard_map/ppermute | solution.py:241
  21.0 1.6 %collective-permute-start.5 = (bf16[48,256]{1,0:T(8,128)(2,1)S(1)}, bf16[48,256]{1,0:T(8,128)(2,1)S(1)}, u32[]{:S(2)}, u32[]{:S(2)}) collective-permute-start(bf16[48,256]{1,0:T(8,128)(2,1)S(1)} %slice.2), channel_id=1, source_target_pairs={{0,2},{1,3},{2,0},{3,1},{4,6},{5,7},{6,4},{7,5},{8,10},{9,11},{10,... | collective-permute-start | bytes 73736 | tf_op jit(solution)/shard_map/ppermute | solution.py:245
  22.8 1.6 %collective-permute-done.6.r3 = bf16[48,256]{1,0:T(8,128)(2,1)S(1)} collective-permute-done((bf16[48,256]{1,0:T(8,128)(2,1)S(1)}, bf16[48,256]{1,0:T(8,128)(2,1)S(1)}, u32[]{:S(2)}, u32[]{:S(2)}) %collective-permute-start.6) | collective-permute-done | bytes 24608 | tf_op jit(solution)/shard_map/ppermute | solution.py:245
  24.9 0.8 %shard_map.70.extra_ref = f32[24,128]{1,0:T(8,128)S(1)} custom-call(s32[11,128]{1,0:T(8,128)S(1)} %pad_add_fusion.info_ref.table_ref, s32[11,128]{1,0:T(8,128)S(1)} %pad_add_fusion.info_ref.table_ref, bf16[48,384]{1,0:T(8,128)(2,1)S(1)} %add_add_fusion.1.r0, bf16[48,256]{1,0:T(8,128)(2,1)S(1)} %collective-permute-done.4.r1, ...), custom_call_target="tpu_custom_call" | custom-call | tf_op jit(solution)/shard_map/pallas_call | solution.py:225
  25.6 0.8 %collective-permute-start.9 = (f32[24,128]{1,0:T(8,128)S(1)}, f32[24,128]{1,0:T(8,128)S(1)}, u32[]{:S(2)}, u32[]{:S(2)}) collective-permute-start(f32[24,128]{1,0:T(8,128)S(1)} %shard_map.70.extra_ref), channel_id=1, source_target_pairs={{0,3},{1,2},{2,1},{3,0},{4,7},{5,6},{6,5},{7,4},{8,11},{9,10},{10,... | collective-permute-start | bytes 36872 | tf_op jit(solution)/shard_map/ppermute | solution.py:245
  26.5 1.2 %collective-permute-start.8 = (f32[24,128]{1,0:T(8,128)S(1)}, f32[24,128]{1,0:T(8,128)S(1)}, u32[]{:S(2)}, u32[]{:S(2)}) collective-permute-start(f32[24,128]{1,0:T(8,128)S(1)} %shard_map.70.extra_ref), channel_id=1, source_target_pairs={{0,2},{1,3},{2,0},{3,1},{4,6},{5,7},{6,4},{7,5},{8,10},{9,11},{10,... | collective-permute-start | bytes 36872 | tf_op jit(solution)/shard_map/ppermute | solution.py:245
  27.6 2.0 %collective-permute-done.11.pair_ref = bf16[64,2048]{1,0:T(8,128)(2,1)S(1)} collective-permute-done((bf16[64,2048]{1,0:T(8,128)(2,1)S(1)}, bf16[64,2048]{1,0:T(8,128)(2,1)S(1)}, u32[]{:S(2)}, u32[]{:S(2)}) %collective-permute-start.11) | collective-permute-done | bytes 262176 | tf_op jit(solution)/shard_map/ppermute | solution.py:241
  29.7 1.7 %shard_map.71.d0 = bf16[64,2048]{1,0:T(8,128)(2,1)S(1)} custom-call(s32[11,128]{1,0:T(8,128)S(1)} %pad_add_fusion.info_ref.table_ref, bf16[16,8,128,128]{3,2,1,0:T(8,128)(2,1)S(1)} %copy-done, bf16[64,2048]{1,0:T(8,128)(2,1)S(1)} %get-tuple-element.19.v_ref.own_ref, bf16[64,2048]{1,0:T(8,128)(2,1)S(1)} %collective-permute-done.10.other_ref, ...), custom_call_target="tpu_custom_call" | custom-call | flops 4294967296 | tf_op jit(solution)/shard_map/pallas_call | solution.py:225
  31.5 3.0 %collective-permute-start.12 = (f32[96,128]{1,0:T(8,128)S(1)}, f32[96,128]{1,0:T(8,128)S(1)}, u32[]{:S(2)}, u32[]{:S(2)}) collective-permute-start(f32[96,128]{1,0:T(8,128)S(1)} %pad_maximum_fusion), channel_id=1, source_target_pairs={{0,4},{4,0},{8,12},{12,8},{16,20},{20,16},{24,28},{28,24},{1,5},{5... | collective-permute-start | bytes 147464 | tf_op jit(solution)/shard_map/ppermute | solution.py:280
  34.5 1.5 %collective-permute-start.17 = (bf16[64,2048]{1,0:T(8,128)(2,1)S(1)}, bf16[64,2048]{1,0:T(8,128)(2,1)S(1)}, u32[]{:S(2)}, u32[]{:S(2)}) collective-permute-start(bf16[64,2048]{1,0:T(8,128)(2,1)S(1)} %shard_map.71.d0), channel_id=1, source_target_pairs={{0,2},{1,3},{2,0},{3,1},{4,6},{5,7},{6,4},{7,5},{8,10},{9,11},{10,... | collective-permute-start | bytes 786440 | tf_op jit(solution)/shard_map/ppermute | solution.py:245
  36.6 4.1 %collective-permute-start.16 = (f32[96,128]{1,0:T(8,128)S(1)}, f32[96,128]{1,0:T(8,128)S(1)}, u32[]{:S(2)}, u32[]{:S(2)}) collective-permute-start(f32[96,128]{1,0:T(8,128)S(1)} %fusion), channel_id=1, source_target_pairs={{0,24},{4,28},{8,16},{12,20},{16,8},{20,12},{24,0},{28,4},{1,25},{... | collective-permute-start | bytes 147464 | tf_op jit(solution)/shard_map/ppermute | solution.py:280
  41.3 1.9 %collective-permute-done.17.d2 = bf16[64,2048]{1,0:T(8,128)(2,1)S(1)} collective-permute-done((bf16[64,2048]{1,0:T(8,128)(2,1)S(1)}, bf16[64,2048]{1,0:T(8,128)(2,1)S(1)}, u32[]{:S(2)}, u32[]{:S(2)}) %collective-permute-start.17) | collective-permute-done | bytes 262176 | tf_op jit(solution)/shard_map/ppermute | solution.py:245
  43.2 2.5 %collective-permute-done.15 = f32[96,128]{1,0:T(8,128)S(1)} collective-permute-done((f32[96,128]{1,0:T(8,128)S(1)}, f32[96,128]{1,0:T(8,128)S(1)}, u32[]{:S(2)}, u32[]{:S(2)}) %collective-permute-start.15) | collective-permute-done | bytes 49184 | tf_op jit(solution)/shard_map/ppermute | solution.py:280
  45.7 2.5 %shard_map.72 = (f32[48,2048]{1,0:T(8,128)}, bf16[64,2048]{1,0:T(8,128)(2,1)}) custom-call(s32[11,128]{1,0:T(8,128)S(1)} %pad_add_fusion.info_ref.table_ref, f32[96,128]{1,0:T(8,128)S(1)} %add_add_fusion.total_ref, bf16[64,2048]{1,0:T(8,128)(2,1)S(1)} %shard_map.71.d0, bf16[64,2048]{1,0:T(8,128)(2,1)S(1)} %collective-permute-done.13.d1, ...), custom_call_target="tpu_custom_call" | custom-call | flops 100663296 | bytes 393216 | tf_op jit(solution)/shard_map/pallas_call | solution.py:225
  (30 shorter events, 2.2 us)
Async XLA Ops:
  0.6 15.4 %collective-permute-start.3 = (bf16[64,2048]{1,0:T(8,128)(2,1)}, bf16[64,2048]{1,0:T(8,128)(2,1)S(1)}, u32[]{:S(2)}, u32[]{:S(2)}) collective-permute-start(bf16[64,2048]{1,0:T(8,128)(2,1)} %v_ref.1), channel_id=1, source_target_pairs={{0,4},{4,0},{8,12},{12,8},{16,20},{20,16},{24,28},{28,24},{1,5},{5... | collective-permute-start | bytes 786440 | tf_op jit(solution)/shard_map/ppermute | solution.py:241
  3.7 12.3 %collective-permute-start = (bf16[64,2048]{1,0:T(8,128)(2,1)}, bf16[64,2048]{1,0:T(8,128)(2,1)S(1)}, u32[]{:S(2)}, u32[]{:S(2)}) collective-permute-start(bf16[64,2048]{1,0:T(8,128)(2,1)} %v_ref.1), channel_id=1, source_target_pairs={{4,8},{12,16},{20,24},{8,4},{16,12},{24,20},{5,9},{13,17},{21,25},... | collective-permute-start | bytes 786440 | tf_op jit(solution)/shard_map/ppermute | solution.py:241
  4.3 11.6 %copy-start = (bf16[16,8,128,128]{3,2,1,0:T(8,128)(2,1)S(1)}, bf16[16,8,128,128]{3,2,1,0:T(8,128)(2,1)}, u32[]{:S(2)}) copy-start(bf16[16,8,128,128]{3,2,1,0:T(8,128)(2,1)} %tiles_ref.5) | copy-start | bytes 12582916
  5.3 1.2 %copy-start.1 = (bf16[64,2048]{1,0:T(8,128)(2,1)S(1)}, bf16[64,2048]{1,0:T(8,128)(2,1)}, u32[]{:S(2)}) copy-start(bf16[64,2048]{1,0:T(8,128)(2,1)} %v_ref.1) | copy-start | bytes 786436
  8.3 12.5 %collective-permute-start.2 = (bf16[48,384]{1,0:T(8,128)(2,1)S(1)}, bf16[48,384]{1,0:T(8,128)(2,1)S(1)}, u32[]{:S(2)}, u32[]{:S(2)}) collective-permute-start(bf16[48,384]{1,0:T(8,128)(2,1)S(1)} %get-tuple-element.17), channel_id=1, source_target_pairs={{4,8},{12,16},{20,24},{8,4},{16,12},{24,20},{5,9},{13,17},{21,25},... | collective-permute-start | bytes 110600 | tf_op jit(solution)/shard_map/ppermute | solution.py:241
  9.0 11.9 %collective-permute-start.1 = (bf16[48,384]{1,0:T(8,128)(2,1)S(1)}, bf16[48,384]{1,0:T(8,128)(2,1)S(1)}, u32[]{:S(2)}, u32[]{:S(2)}) collective-permute-start(bf16[48,384]{1,0:T(8,128)(2,1)S(1)} %get-tuple-element.17), channel_id=1, source_target_pairs={{0,4},{4,0},{8,12},{12,8},{16,20},{20,16},{24,28},{28,24},{1,5},{5... | collective-permute-start | bytes 110600 | tf_op jit(solution)/shard_map/ppermute | solution.py:241
  17.8 11.9 %collective-permute-start.11 = (bf16[64,2048]{1,0:T(8,128)(2,1)S(1)}, bf16[64,2048]{1,0:T(8,128)(2,1)S(1)}, u32[]{:S(2)}, u32[]{:S(2)}) collective-permute-start(bf16[64,2048]{1,0:T(8,128)(2,1)S(1)} %get-tuple-element.19.v_ref.own_ref), channel_id=1, source_target_pairs={{0,4},{4,0},{8,12},{12,8},{16,20},{20,16},{24,28},{28,24},{1,5},{5... | collective-permute-start | bytes 786440 | tf_op jit(solution)/shard_map/ppermute | solution.py:241
  20.2 9.5 %collective-permute-start.10 = (bf16[64,2048]{1,0:T(8,128)(2,1)S(1)}, bf16[64,2048]{1,0:T(8,128)(2,1)S(1)}, u32[]{:S(2)}, u32[]{:S(2)}) collective-permute-start(bf16[64,2048]{1,0:T(8,128)(2,1)S(1)} %get-tuple-element.19.v_ref.own_ref), channel_id=1, source_target_pairs={{4,8},{12,16},{20,24},{8,4},{16,12},{24,20},{5,9},{13,17},{21,25},... | collective-permute-start | bytes 786440 | tf_op jit(solution)/shard_map/ppermute | solution.py:241
  20.9 3.5 %collective-permute-start.6 = (bf16[48,256]{1,0:T(8,128)(2,1)S(1)}, bf16[48,256]{1,0:T(8,128)(2,1)S(1)}, u32[]{:S(2)}, u32[]{:S(2)}) collective-permute-start(bf16[48,256]{1,0:T(8,128)(2,1)S(1)} %slice.2), channel_id=1, source_target_pairs={{0,3},{1,2},{2,1},{3,0},{4,7},{5,6},{6,5},{7,4},{8,11},{9,10},{10,... | collective-permute-start | bytes 73736 | tf_op jit(solution)/shard_map/ppermute | solution.py:245
  21.0 3.9 %collective-permute-start.5 = (bf16[48,256]{1,0:T(8,128)(2,1)S(1)}, bf16[48,256]{1,0:T(8,128)(2,1)S(1)}, u32[]{:S(2)}, u32[]{:S(2)}) collective-permute-start(bf16[48,256]{1,0:T(8,128)(2,1)S(1)} %slice.2), channel_id=1, source_target_pairs={{0,2},{1,3},{2,0},{3,1},{4,6},{5,7},{6,4},{7,5},{8,10},{9,11},{10,... | collective-permute-start | bytes 73736 | tf_op jit(solution)/shard_map/ppermute | solution.py:245
  22.5 2.3 %collective-permute-start.4 = (bf16[48,256]{1,0:T(8,128)(2,1)S(1)}, bf16[48,256]{1,0:T(8,128)(2,1)S(1)}, u32[]{:S(2)}, u32[]{:S(2)}) collective-permute-start(bf16[48,256]{1,0:T(8,128)(2,1)S(1)} %slice.2), channel_id=1, source_target_pairs={{0,1},{1,0},{2,3},{3,2},{4,5},{5,4},{6,7},{7,6},{8,9},{9,8},{10,11... | collective-permute-start | bytes 73736 | tf_op jit(solution)/shard_map/ppermute | solution.py:245
  25.6 5.8 %collective-permute-start.9 = (f32[24,128]{1,0:T(8,128)S(1)}, f32[24,128]{1,0:T(8,128)S(1)}, u32[]{:S(2)}, u32[]{:S(2)}) collective-permute-start(f32[24,128]{1,0:T(8,128)S(1)} %shard_map.70.extra_ref), channel_id=1, source_target_pairs={{0,3},{1,2},{2,1},{3,0},{4,7},{5,6},{6,5},{7,4},{8,11},{9,10},{10,... | collective-permute-start | bytes 36872 | tf_op jit(solution)/shard_map/ppermute | solution.py:245
  26.5 5.0 %collective-permute-start.8 = (f32[24,128]{1,0:T(8,128)S(1)}, f32[24,128]{1,0:T(8,128)S(1)}, u32[]{:S(2)}, u32[]{:S(2)}) collective-permute-start(f32[24,128]{1,0:T(8,128)S(1)} %shard_map.70.extra_ref), channel_id=1, source_target_pairs={{0,2},{1,3},{2,0},{3,1},{4,6},{5,7},{6,4},{7,5},{8,10},{9,11},{10,... | collective-permute-start | bytes 36872 | tf_op jit(solution)/shard_map/ppermute | solution.py:245
  27.6 3.8 %collective-permute-start.7 = (f32[24,128]{1,0:T(8,128)S(1)}, f32[24,128]{1,0:T(8,128)S(1)}, u32[]{:S(2)}, u32[]{:S(2)}) collective-permute-start(f32[24,128]{1,0:T(8,128)S(1)} %shard_map.70.extra_ref), channel_id=1, source_target_pairs={{0,1},{1,0},{2,3},{3,2},{4,5},{5,4},{6,7},{7,6},{8,9},{9,8},{10,11... | collective-permute-start | bytes 36872 | tf_op jit(solution)/shard_map/ppermute | solution.py:245
  31.5 5.1 %collective-permute-start.12 = (f32[96,128]{1,0:T(8,128)S(1)}, f32[96,128]{1,0:T(8,128)S(1)}, u32[]{:S(2)}, u32[]{:S(2)}) collective-permute-start(f32[96,128]{1,0:T(8,128)S(1)} %pad_maximum_fusion), channel_id=1, source_target_pairs={{0,4},{4,0},{8,12},{12,8},{16,20},{20,16},{24,28},{28,24},{1,5},{5... | collective-permute-start | bytes 147464 | tf_op jit(solution)/shard_map/ppermute | solution.py:280
  34.5 2.1 %collective-permute-start.13 = (bf16[64,2048]{1,0:T(8,128)(2,1)S(1)}, bf16[64,2048]{1,0:T(8,128)(2,1)S(1)}, u32[]{:S(2)}, u32[]{:S(2)}) collective-permute-start(bf16[64,2048]{1,0:T(8,128)(2,1)S(1)} %shard_map.71.d0), channel_id=1, source_target_pairs={{0,1},{1,0},{2,3},{3,2},{4,5},{5,4},{6,7},{7,6},{8,9},{9,8},{10,11... | collective-permute-start | bytes 786440 | tf_op jit(solution)/shard_map/ppermute | solution.py:245
  34.5 8.7 %collective-permute-start.17 = (bf16[64,2048]{1,0:T(8,128)(2,1)S(1)}, bf16[64,2048]{1,0:T(8,128)(2,1)S(1)}, u32[]{:S(2)}, u32[]{:S(2)}) collective-permute-start(bf16[64,2048]{1,0:T(8,128)(2,1)S(1)} %shard_map.71.d0), channel_id=1, source_target_pairs={{0,2},{1,3},{2,0},{3,1},{4,6},{5,7},{6,4},{7,5},{8,10},{9,11},{10,... | collective-permute-start | bytes 786440 | tf_op jit(solution)/shard_map/ppermute | solution.py:245
  36.6 6.6 %collective-permute-start.16 = (f32[96,128]{1,0:T(8,128)S(1)}, f32[96,128]{1,0:T(8,128)S(1)}, u32[]{:S(2)}, u32[]{:S(2)}) collective-permute-start(f32[96,128]{1,0:T(8,128)S(1)} %fusion), channel_id=1, source_target_pairs={{0,24},{4,28},{8,16},{12,20},{16,8},{20,12},{24,0},{28,4},{1,25},{... | collective-permute-start | bytes 147464 | tf_op jit(solution)/shard_map/ppermute | solution.py:280
  40.7 5.0 %collective-permute-start.15 = (f32[96,128]{1,0:T(8,128)S(1)}, f32[96,128]{1,0:T(8,128)S(1)}, u32[]{:S(2)}, u32[]{:S(2)}) collective-permute-start(f32[96,128]{1,0:T(8,128)S(1)} %fusion), channel_id=1, source_target_pairs={{0,16},{4,20},{8,24},{12,28},{16,0},{20,4},{24,8},{28,12},{1,17},{... | collective-permute-start | bytes 147464 | tf_op jit(solution)/shard_map/ppermute | solution.py:280
  40.7 5.0 %collective-permute-start.14 = (f32[96,128]{1,0:T(8,128)S(1)}, f32[96,128]{1,0:T(8,128)S(1)}, u32[]{:S(2)}, u32[]{:S(2)}) collective-permute-start(f32[96,128]{1,0:T(8,128)S(1)} %fusion), channel_id=1, source_target_pairs={{0,8},{4,12},{8,0},{12,4},{16,24},{20,28},{24,16},{28,20},{1,9},{5... | collective-permute-start | bytes 147464 | tf_op jit(solution)/shard_map/ppermute | solution.py:280
  43.2 2.5 %collective-permute-start.18 = (bf16[64,2048]{1,0:T(8,128)(2,1)S(1)}, bf16[64,2048]{1,0:T(8,128)(2,1)S(1)}, u32[]{:S(2)}, u32[]{:S(2)}) collective-permute-start(bf16[64,2048]{1,0:T(8,128)(2,1)S(1)} %collective-permute-done.17.d2), channel_id=1, source_target_pairs={{0,1},{1,0},{2,3},{3,2},{4,5},{5,4},{6,7},{7,6},{8,9},{9,8},{10,11... | collective-permute-start | bytes 786440 | tf_op jit(solution)/shard_map/ppermute | solution.py:245

commit v8 on v7

--- a/solution.py
+++ b/solution.py
@@ -169,7 +169,7 @@
     same = pltpu.make_async_copy(d0, copy_ref, sem.at[0])
     same.start()
     me = info_ref[...][META, 2]
-    step = 256
+    step = 512
     for c in range(0, width, step):
         d = jnp.concatenate(in_order(me, [d[:, c:c + step] for d in (d0, d1, d2, d3)]), axis=0)
         whole_ref[:, c:c + step] = d

time: 48.4 us -> 48.5 us (level)
  no operation moved by 1% of the time
where the time goes in v8:
time: 48.5 us; the launch traced here: 48.3 us
  starting transfers between devices  26.2 us (54%)
  waiting for transfers between devices  10.4 us (21%)
  Pallas kernels  8.67 us (18%)
  local copies, waits for them, and re-layouts  1.19 us (2%)
  other arithmetic  1 us (2%)
  between operations  0.79 us (2%)
    ppermute x3, starting transfers between devices, exchange(): lax.ppermute(matrix, 'cells', pairs)  11 us
    pallas_call x5, Pallas kernels, call(): pl.pallas_call(kernel, out_shape=out_shape, in_specs=[spec[k] for k in ki...  8.67 us
    ppermute x4, starting transfers between devices, on_device(): lax.ppermute(x, 'cells', [(i, i ^ bits) for i in range(size)])  7.75 us
    ppermute x9, starting transfers between devices, flip_feat(): lax.ppermute(x, 'feat', [(i, i ^ bits) for i in range(lax.axis_size('feat...  5.43 us
    ppermute x9, waiting for transfers between devices, flip_feat(): lax.ppermute(x, 'feat', [(i, i ^ bits) for i in range(lax.axis_size('feat...  3.95 us
    ppermute x3, waiting for transfers between devices, exchange(): lax.ppermute(matrix, 'cells', pairs)  3.45 us
    ppermute x4, waiting for transfers between devices, on_device(): lax.ppermute(x, 'cells', [(i, i ^ bits) for i in range(size)])  3.04 us
    ppermute x3, starting transfers between devices, exchange(): lax.ppermute(matrix, 'cells', others)  1.99 us
  transfers between devices with their start and end apart: 19, of which 7 were waited for; matrix products, arithmetic and copies ran while one was open for 2% of the time, Pallas kernels for 13%

profile of v8, /device:TPU:0, one launch (start us, length us, event | category | flops | bytes accessed | tf_op | source)
XLA Modules:
  0.0 48.3 jit_solution(5544334968719223380)
XLA Ops:
  0.6 3.0 %collective-permute-start.3 = (bf16[64,2048]{1,0:T(8,128)(2,1)}, bf16[64,2048]{1,0:T(8,128)(2,1)S(1)}, u32[]{:S(2)}, u32[]{:S(2)}) collective-permute-start(bf16[64,2048]{1,0:T(8,128)(2,1)} %v_ref.1), channel_id=1, source_target_pairs={{0,4},{4,0},{8,12},{12,8},{16,20},{20,16},{24,28},{28,24},{1,5},{5... | collective-permute-start | bytes 786440 | tf_op jit(solution)/shard_map/ppermute | solution.py:241
  3.7 0.7 %collective-permute-start = (bf16[64,2048]{1,0:T(8,128)(2,1)}, bf16[64,2048]{1,0:T(8,128)(2,1)S(1)}, u32[]{:S(2)}, u32[]{:S(2)}) collective-permute-start(bf16[64,2048]{1,0:T(8,128)(2,1)} %v_ref.1), channel_id=1, source_target_pairs={{4,8},{12,16},{20,24},{8,4},{16,12},{24,20},{5,9},{13,17},{21,25},... | collective-permute-start | bytes 786440 | tf_op jit(solution)/shard_map/ppermute | solution.py:241
  4.4 0.9 %pad_add_fusion.info_ref.table_ref = s32[11,128]{1,0:T(8,128)S(1)} fusion(s32[1,3]{1,0:T(1,128)S(1)} %add_bitcast_fusion, s32[1,16]{1,0:T(1,128)} %bitcast.9, s32[1,48]{1,0:T(1,128)} %bitcast.10, s32[8,16]{1,0:T(8,128)} %bitcast.8), kind=kLoop, calls=%fused_computation.3 | loop fusion | flops 4224 | bytes 6412 | tf_op jit(solution)/shard_map/concatenate | solution.py:258
  5.3 1.2 %copy-done.1 = bf16[64,2048]{1,0:T(8,128)(2,1)S(1)} copy-done((bf16[64,2048]{1,0:T(8,128)(2,1)S(1)}, bf16[64,2048]{1,0:T(8,128)(2,1)}, u32[]{:S(2)}) %copy-start.1) | copy-done | bytes 262168
  6.5 1.8 %shard_map.68 = (bf16[48,384]{1,0:T(8,128)(2,1)S(1)}, bf16[64,2048]{1,0:T(8,128)(2,1)S(1)}) custom-call(s32[11,128]{1,0:T(8,128)S(1)} %pad_add_fusion.info_ref.table_ref, s32[11,128]{1,0:T(8,128)S(1)} %pad_add_fusion.info_ref.table_ref, bf16[16,8,128,128]{3,2,1,0:T(8,128)(2,1)} %tiles_ref.5, bf16[64,2048]{1,0:T(8,128)(2,1)S(1)} %copy-done.1), custom_call_target="tpu_custom_call" | custom-call | tf_op jit(solution)/shard_map/pallas_call | solution.py:225
  8.3 0.7 %collective-permute-start.2 = (bf16[48,384]{1,0:T(8,128)(2,1)S(1)}, bf16[48,384]{1,0:T(8,128)(2,1)S(1)}, u32[]{:S(2)}, u32[]{:S(2)}) collective-permute-start(bf16[48,384]{1,0:T(8,128)(2,1)S(1)} %get-tuple-element.17), channel_id=1, source_target_pairs={{4,8},{12,16},{20,24},{8,4},{16,12},{24,20},{5,9},{13,17},{21,25},... | collective-permute-start | bytes 110600 | tf_op jit(solution)/shard_map/ppermute | solution.py:241
  9.0 5.6 %collective-permute-start.1 = (bf16[48,384]{1,0:T(8,128)(2,1)S(1)}, bf16[48,384]{1,0:T(8,128)(2,1)S(1)}, u32[]{:S(2)}, u32[]{:S(2)}) collective-permute-start(bf16[48,384]{1,0:T(8,128)(2,1)S(1)} %get-tuple-element.17), channel_id=1, source_target_pairs={{0,4},{4,0},{8,12},{12,8},{16,20},{20,16},{24,28},{28,24},{1,5},{5... | collective-permute-start | bytes 110600 | tf_op jit(solution)/shard_map/ppermute | solution.py:241
  14.6 1.4 %collective-permute-done.3.pair_ref = bf16[64,2048]{1,0:T(8,128)(2,1)S(1)} collective-permute-done((bf16[64,2048]{1,0:T(8,128)(2,1)}, bf16[64,2048]{1,0:T(8,128)(2,1)S(1)}, u32[]{:S(2)}, u32[]{:S(2)}) %collective-permute-start.3) | collective-permute-done | bytes 262176 | tf_op jit(solution)/shard_map/ppermute | solution.py:241
  16.0 1.8 %shard_map.69 = (bf16[64,2048]{1,0:T(8,128)(2,1)S(1)}, f32[16,8,128]{2,1,0:T(8,128)S(1)}) custom-call(s32[11,128]{1,0:T(8,128)S(1)} %pad_add_fusion.info_ref.table_ref, bf16[16,8,128,128]{3,2,1,0:T(8,128)(2,1)S(1)} %copy-done, bf16[64,2048]{1,0:T(8,128)(2,1)S(1)} %get-tuple-element.18.own_ref, bf16[64,2048]{1,0:T(8,128)(2,1)S(1)} %collective-permute-done.other_ref, ...), custom_call_target="tpu_custom_call" | custom-call | flops 268435456 | bytes 4194304 | tf_op jit(solution)/shard_map/pallas_call | solution.py:225
  17.8 2.4 %collective-permute-start.11 = (bf16[64,2048]{1,0:T(8,128)(2,1)S(1)}, bf16[64,2048]{1,0:T(8,128)(2,1)S(1)}, u32[]{:S(2)}, u32[]{:S(2)}) collective-permute-start(bf16[64,2048]{1,0:T(8,128)(2,1)S(1)} %get-tuple-element.19.v_ref.own_ref), channel_id=1, source_target_pairs={{0,4},{4,0},{8,12},{12,8},{16,20},{20,16},{24,28},{28,24},{1,5},{5... | collective-permute-start | bytes 786440 | tf_op jit(solution)/shard_map/ppermute | solution.py:241
  20.2 0.7 %collective-permute-start.10 = (bf16[64,2048]{1,0:T(8,128)(2,1)S(1)}, bf16[64,2048]{1,0:T(8,128)(2,1)S(1)}, u32[]{:S(2)}, u32[]{:S(2)}) collective-permute-start(bf16[64,2048]{1,0:T(8,128)(2,1)S(1)} %get-tuple-element.19.v_ref.own_ref), channel_id=1, source_target_pairs={{4,8},{12,16},{20,24},{8,4},{16,12},{24,20},{5,9},{13,17},{21,25},... | collective-permute-start | bytes 786440 | tf_op jit(solution)/shard_map/ppermute | solution.py:241
  21.0 1.6 %collective-permute-start.5 = (bf16[48,256]{1,0:T(8,128)(2,1)S(1)}, bf16[48,256]{1,0:T(8,128)(2,1)S(1)}, u32[]{:S(2)}, u32[]{:S(2)}) collective-permute-start(bf16[48,256]{1,0:T(8,128)(2,1)S(1)} %slice.2), channel_id=1, source_target_pairs={{0,2},{1,3},{2,0},{3,1},{4,6},{5,7},{6,4},{7,5},{8,10},{9,11},{10,... | collective-permute-start | bytes 73736 | tf_op jit(solution)/shard_map/ppermute | solution.py:245
  22.8 1.6 %collective-permute-done.6.r3 = bf16[48,256]{1,0:T(8,128)(2,1)S(1)} collective-permute-done((bf16[48,256]{1,0:T(8,128)(2,1)S(1)}, bf16[48,256]{1,0:T(8,128)(2,1)S(1)}, u32[]{:S(2)}, u32[]{:S(2)}) %collective-permute-start.6) | collective-permute-done | bytes 24608 | tf_op jit(solution)/shard_map/ppermute | solution.py:245
  24.9 0.8 %shard_map.70.extra_ref = f32[24,128]{1,0:T(8,128)S(1)} custom-call(s32[11,128]{1,0:T(8,128)S(1)} %pad_add_fusion.info_ref.table_ref, s32[11,128]{1,0:T(8,128)S(1)} %pad_add_fusion.info_ref.table_ref, bf16[48,384]{1,0:T(8,128)(2,1)S(1)} %add_add_fusion.1.r0, bf16[48,256]{1,0:T(8,128)(2,1)S(1)} %collective-permute-done.4.r1, ...), custom_call_target="tpu_custom_call" | custom-call | tf_op jit(solution)/shard_map/pallas_call | solution.py:225
  25.6 0.8 %collective-permute-start.9 = (f32[24,128]{1,0:T(8,128)S(1)}, f32[24,128]{1,0:T(8,128)S(1)}, u32[]{:S(2)}, u32[]{:S(2)}) collective-permute-start(f32[24,128]{1,0:T(8,128)S(1)} %shard_map.70.extra_ref), channel_id=1, source_target_pairs={{0,3},{1,2},{2,1},{3,0},{4,7},{5,6},{6,5},{7,4},{8,11},{9,10},{10,... | collective-permute-start | bytes 36872 | tf_op jit(solution)/shard_map/ppermute | solution.py:245
  26.5 1.2 %collective-permute-start.8 = (f32[24,128]{1,0:T(8,128)S(1)}, f32[24,128]{1,0:T(8,128)S(1)}, u32[]{:S(2)}, u32[]{:S(2)}) collective-permute-start(f32[24,128]{1,0:T(8,128)S(1)} %shard_map.70.extra_ref), channel_id=1, source_target_pairs={{0,2},{1,3},{2,0},{3,1},{4,6},{5,7},{6,4},{7,5},{8,10},{9,11},{10,... | collective-permute-start | bytes 36872 | tf_op jit(solution)/shard_map/ppermute | solution.py:245
  27.6 2.0 %collective-permute-done.11.pair_ref = bf16[64,2048]{1,0:T(8,128)(2,1)S(1)} collective-permute-done((bf16[64,2048]{1,0:T(8,128)(2,1)S(1)}, bf16[64,2048]{1,0:T(8,128)(2,1)S(1)}, u32[]{:S(2)}, u32[]{:S(2)}) %collective-permute-start.11) | collective-permute-done | bytes 262176 | tf_op jit(solution)/shard_map/ppermute | solution.py:241
  29.7 1.7 %shard_map.71.d0 = bf16[64,2048]{1,0:T(8,128)(2,1)S(1)} custom-call(s32[11,128]{1,0:T(8,128)S(1)} %pad_add_fusion.info_ref.table_ref, bf16[16,8,128,128]{3,2,1,0:T(8,128)(2,1)S(1)} %copy-done, bf16[64,2048]{1,0:T(8,128)(2,1)S(1)} %get-tuple-element.19.v_ref.own_ref, bf16[64,2048]{1,0:T(8,128)(2,1)S(1)} %collective-permute-done.10.other_ref, ...), custom_call_target="tpu_custom_call" | custom-call | flops 4294967296 | tf_op jit(solution)/shard_map/pallas_call | solution.py:225
  31.5 3.0 %collective-permute-start.12 = (f32[96,128]{1,0:T(8,128)S(1)}, f32[96,128]{1,0:T(8,128)S(1)}, u32[]{:S(2)}, u32[]{:S(2)}) collective-permute-start(f32[96,128]{1,0:T(8,128)S(1)} %pad_maximum_fusion), channel_id=1, source_target_pairs={{0,4},{4,0},{8,12},{12,8},{16,20},{20,16},{24,28},{28,24},{1,5},{5... | collective-permute-start | bytes 147464 | tf_op jit(solution)/shard_map/ppermute | solution.py:280
  34.5 1.5 %collective-permute-start.17 = (bf16[64,2048]{1,0:T(8,128)(2,1)S(1)}, bf16[64,2048]{1,0:T(8,128)(2,1)S(1)}, u32[]{:S(2)}, u32[]{:S(2)}) collective-permute-start(bf16[64,2048]{1,0:T(8,128)(2,1)S(1)} %shard_map.71.d0), channel_id=1, source_target_pairs={{0,2},{1,3},{2,0},{3,1},{4,6},{5,7},{6,4},{7,5},{8,10},{9,11},{10,... | collective-permute-start | bytes 786440 | tf_op jit(solution)/shard_map/ppermute | solution.py:245
  36.6 4.1 %collective-permute-start.16 = (f32[96,128]{1,0:T(8,128)S(1)}, f32[96,128]{1,0:T(8,128)S(1)}, u32[]{:S(2)}, u32[]{:S(2)}) collective-permute-start(f32[96,128]{1,0:T(8,128)S(1)} %fusion), channel_id=1, source_target_pairs={{0,24},{4,28},{8,16},{12,20},{16,8},{20,12},{24,0},{28,4},{1,25},{... | collective-permute-start | bytes 147464 | tf_op jit(solution)/shard_map/ppermute | solution.py:280
  41.3 1.9 %collective-permute-done.17.d2 = bf16[64,2048]{1,0:T(8,128)(2,1)S(1)} collective-permute-done((bf16[64,2048]{1,0:T(8,128)(2,1)S(1)}, bf16[64,2048]{1,0:T(8,128)(2,1)S(1)}, u32[]{:S(2)}, u32[]{:S(2)}) %collective-permute-start.17) | collective-permute-done | bytes 262176 | tf_op jit(solution)/shard_map/ppermute | solution.py:245
  43.2 2.4 %collective-permute-done.15 = f32[96,128]{1,0:T(8,128)S(1)} collective-permute-done((f32[96,128]{1,0:T(8,128)S(1)}, f32[96,128]{1,0:T(8,128)S(1)}, u32[]{:S(2)}, u32[]{:S(2)}) %collective-permute-start.15) | collective-permute-done | bytes 49184 | tf_op jit(solution)/shard_map/ppermute | solution.py:280
  45.7 2.6 %shard_map.72 = (f32[48,2048]{1,0:T(8,128)}, bf16[64,2048]{1,0:T(8,128)(2,1)}) custom-call(s32[11,128]{1,0:T(8,128)S(1)} %pad_add_fusion.info_ref.table_ref, f32[96,128]{1,0:T(8,128)S(1)} %add_add_fusion.total_ref, bf16[64,2048]{1,0:T(8,128)(2,1)S(1)} %shard_map.71.d0, bf16[64,2048]{1,0:T(8,128)(2,1)S(1)} %collective-permute-done.13.d1, ...), custom_call_target="tpu_custom_call" | custom-call | flops 100663296 | bytes 393216 | tf_op jit(solution)/shard_map/pallas_call | solution.py:225
  (30 shorter events, 2.2 us)
Async XLA Ops:
  0.6 15.4 %collective-permute-start.3 = (bf16[64,2048]{1,0:T(8,128)(2,1)}, bf16[64,2048]{1,0:T(8,128)(2,1)S(1)}, u32[]{:S(2)}, u32[]{:S(2)}) collective-permute-start(bf16[64,2048]{1,0:T(8,128)(2,1)} %v_ref.1), channel_id=1, source_target_pairs={{0,4},{4,0},{8,12},{12,8},{16,20},{20,16},{24,28},{28,24},{1,5},{5... | collective-permute-start | bytes 786440 | tf_op jit(solution)/shard_map/ppermute | solution.py:241
  3.7 12.3 %collective-permute-start = (bf16[64,2048]{1,0:T(8,128)(2,1)}, bf16[64,2048]{1,0:T(8,128)(2,1)S(1)}, u32[]{:S(2)}, u32[]{:S(2)}) collective-permute-start(bf16[64,2048]{1,0:T(8,128)(2,1)} %v_ref.1), channel_id=1, source_target_pairs={{4,8},{12,16},{20,24},{8,4},{16,12},{24,20},{5,9},{13,17},{21,25},... | collective-permute-start | bytes 786440 | tf_op jit(solution)/shard_map/ppermute | solution.py:241
  4.3 11.6 %copy-start = (bf16[16,8,128,128]{3,2,1,0:T(8,128)(2,1)S(1)}, bf16[16,8,128,128]{3,2,1,0:T(8,128)(2,1)}, u32[]{:S(2)}) copy-start(bf16[16,8,128,128]{3,2,1,0:T(8,128)(2,1)} %tiles_ref.5) | copy-start | bytes 12582916
  5.3 1.2 %copy-start.1 = (bf16[64,2048]{1,0:T(8,128)(2,1)S(1)}, bf16[64,2048]{1,0:T(8,128)(2,1)}, u32[]{:S(2)}) copy-start(bf16[64,2048]{1,0:T(8,128)(2,1)} %v_ref.1) | copy-start | bytes 786436
  8.3 12.5 %collective-permute-start.2 = (bf16[48,384]{1,0:T(8,128)(2,1)S(1)}, bf16[48,384]{1,0:T(8,128)(2,1)S(1)}, u32[]{:S(2)}, u32[]{:S(2)}) collective-permute-start(bf16[48,384]{1,0:T(8,128)(2,1)S(1)} %get-tuple-element.17), channel_id=1, source_target_pairs={{4,8},{12,16},{20,24},{8,4},{16,12},{24,20},{5,9},{13,17},{21,25},... | collective-permute-start | bytes 110600 | tf_op jit(solution)/shard_map/ppermute | solution.py:241
  9.0 11.9 %collective-permute-start.1 = (bf16[48,384]{1,0:T(8,128)(2,1)S(1)}, bf16[48,384]{1,0:T(8,128)(2,1)S(1)}, u32[]{:S(2)}, u32[]{:S(2)}) collective-permute-start(bf16[48,384]{1,0:T(8,128)(2,1)S(1)} %get-tuple-element.17), channel_id=1, source_target_pairs={{0,4},{4,0},{8,12},{12,8},{16,20},{20,16},{24,28},{28,24},{1,5},{5... | collective-permute-start | bytes 110600 | tf_op jit(solution)/shard_map/ppermute | solution.py:241
  17.8 11.9 %collective-permute-start.11 = (bf16[64,2048]{1,0:T(8,128)(2,1)S(1)}, bf16[64,2048]{1,0:T(8,128)(2,1)S(1)}, u32[]{:S(2)}, u32[]{:S(2)}) collective-permute-start(bf16[64,2048]{1,0:T(8,128)(2,1)S(1)} %get-tuple-element.19.v_ref.own_ref), channel_id=1, source_target_pairs={{0,4},{4,0},{8,12},{12,8},{16,20},{20,16},{24,28},{28,24},{1,5},{5... | collective-permute-start | bytes 786440 | tf_op jit(solution)/shard_map/ppermute | solution.py:241
  20.2 9.5 %collective-permute-start.10 = (bf16[64,2048]{1,0:T(8,128)(2,1)S(1)}, bf16[64,2048]{1,0:T(8,128)(2,1)S(1)}, u32[]{:S(2)}, u32[]{:S(2)}) collective-permute-start(bf16[64,2048]{1,0:T(8,128)(2,1)S(1)} %get-tuple-element.19.v_ref.own_ref), channel_id=1, source_target_pairs={{4,8},{12,16},{20,24},{8,4},{16,12},{24,20},{5,9},{13,17},{21,25},... | collective-permute-start | bytes 786440 | tf_op jit(solution)/shard_map/ppermute | solution.py:241
  20.9 3.5 %collective-permute-start.6 = (bf16[48,256]{1,0:T(8,128)(2,1)S(1)}, bf16[48,256]{1,0:T(8,128)(2,1)S(1)}, u32[]{:S(2)}, u32[]{:S(2)}) collective-permute-start(bf16[48,256]{1,0:T(8,128)(2,1)S(1)} %slice.2), channel_id=1, source_target_pairs={{0,3},{1,2},{2,1},{3,0},{4,7},{5,6},{6,5},{7,4},{8,11},{9,10},{10,... | collective-permute-start | bytes 73736 | tf_op jit(solution)/shard_map/ppermute | solution.py:245
  21.0 3.9 %collective-permute-start.5 = (bf16[48,256]{1,0:T(8,128)(2,1)S(1)}, bf16[48,256]{1,0:T(8,128)(2,1)S(1)}, u32[]{:S(2)}, u32[]{:S(2)}) collective-permute-start(bf16[48,256]{1,0:T(8,128)(2,1)S(1)} %slice.2), channel_id=1, source_target_pairs={{0,2},{1,3},{2,0},{3,1},{4,6},{5,7},{6,4},{7,5},{8,10},{9,11},{10,... | collective-permute-start | bytes 73736 | tf_op jit(solution)/shard_map/ppermute | solution.py:245
  22.5 2.3 %collective-permute-start.4 = (bf16[48,256]{1,0:T(8,128)(2,1)S(1)}, bf16[48,256]{1,0:T(8,128)(2,1)S(1)}, u32[]{:S(2)}, u32[]{:S(2)}) collective-permute-start(bf16[48,256]{1,0:T(8,128)(2,1)S(1)} %slice.2), channel_id=1, source_target_pairs={{0,1},{1,0},{2,3},{3,2},{4,5},{5,4},{6,7},{7,6},{8,9},{9,8},{10,11... | collective-permute-start | bytes 73736 | tf_op jit(solution)/shard_map/ppermute | solution.py:245
  25.6 5.8 %collective-permute-start.9 = (f32[24,128]{1,0:T(8,128)S(1)}, f32[24,128]{1,0:T(8,128)S(1)}, u32[]{:S(2)}, u32[]{:S(2)}) collective-permute-start(f32[24,128]{1,0:T(8,128)S(1)} %shard_map.70.extra_ref), channel_id=1, source_target_pairs={{0,3},{1,2},{2,1},{3,0},{4,7},{5,6},{6,5},{7,4},{8,11},{9,10},{10,... | collective-permute-start | bytes 36872 | tf_op jit(solution)/shard_map/ppermute | solution.py:245
  26.5 5.0 %collective-permute-start.8 = (f32[24,128]{1,0:T(8,128)S(1)}, f32[24,128]{1,0:T(8,128)S(1)}, u32[]{:S(2)}, u32[]{:S(2)}) collective-permute-start(f32[24,128]{1,0:T(8,128)S(1)} %shard_map.70.extra_ref), channel_id=1, source_target_pairs={{0,2},{1,3},{2,0},{3,1},{4,6},{5,7},{6,4},{7,5},{8,10},{9,11},{10,... | collective-permute-start | bytes 36872 | tf_op jit(solution)/shard_map/ppermute | solution.py:245
  27.6 3.8 %collective-permute-start.7 = (f32[24,128]{1,0:T(8,128)S(1)}, f32[24,128]{1,0:T(8,128)S(1)}, u32[]{:S(2)}, u32[]{:S(2)}) collective-permute-start(f32[24,128]{1,0:T(8,128)S(1)} %shard_map.70.extra_ref), channel_id=1, source_target_pairs={{0,1},{1,0},{2,3},{3,2},{4,5},{5,4},{6,7},{7,6},{8,9},{9,8},{10,11... | collective-permute-start | bytes 36872 | tf_op jit(solution)/shard_map/ppermute | solution.py:245
  31.5 5.1 %collective-permute-start.12 = (f32[96,128]{1,0:T(8,128)S(1)}, f32[96,128]{1,0:T(8,128)S(1)}, u32[]{:S(2)}, u32[]{:S(2)}) collective-permute-start(f32[96,128]{1,0:T(8,128)S(1)} %pad_maximum_fusion), channel_id=1, source_target_pairs={{0,4},{4,0},{8,12},{12,8},{16,20},{20,16},{24,28},{28,24},{1,5},{5... | collective-permute-start | bytes 147464 | tf_op jit(solution)/shard_map/ppermute | solution.py:280
  34.5 2.1 %collective-permute-start.13 = (bf16[64,2048]{1,0:T(8,128)(2,1)S(1)}, bf16[64,2048]{1,0:T(8,128)(2,1)S(1)}, u32[]{:S(2)}, u32[]{:S(2)}) collective-permute-start(bf16[64,2048]{1,0:T(8,128)(2,1)S(1)} %shard_map.71.d0), channel_id=1, source_target_pairs={{0,1},{1,0},{2,3},{3,2},{4,5},{5,4},{6,7},{7,6},{8,9},{9,8},{10,11... | collective-permute-start | bytes 786440 | tf_op jit(solution)/shard_map/ppermute | solution.py:245
  34.5 8.7 %collective-permute-start.17 = (bf16[64,2048]{1,0:T(8,128)(2,1)S(1)}, bf16[64,2048]{1,0:T(8,128)(2,1)S(1)}, u32[]{:S(2)}, u32[]{:S(2)}) collective-permute-start(bf16[64,2048]{1,0:T(8,128)(2,1)S(1)} %shard_map.71.d0), channel_id=1, source_target_pairs={{0,2},{1,3},{2,0},{3,1},{4,6},{5,7},{6,4},{7,5},{8,10},{9,11},{10,... | collective-permute-start | bytes 786440 | tf_op jit(solution)/shard_map/ppermute | solution.py:245
  36.6 6.6 %collective-permute-start.16 = (f32[96,128]{1,0:T(8,128)S(1)}, f32[96,128]{1,0:T(8,128)S(1)}, u32[]{:S(2)}, u32[]{:S(2)}) collective-permute-start(f32[96,128]{1,0:T(8,128)S(1)} %fusion), channel_id=1, source_target_pairs={{0,24},{4,28},{8,16},{12,20},{16,8},{20,12},{24,0},{28,4},{1,25},{... | collective-permute-start | bytes 147464 | tf_op jit(solution)/shard_map/ppermute | solution.py:280
  40.7 5.0 %collective-permute-start.15 = (f32[96,128]{1,0:T(8,128)S(1)}, f32[96,128]{1,0:T(8,128)S(1)}, u32[]{:S(2)}, u32[]{:S(2)}) collective-permute-start(f32[96,128]{1,0:T(8,128)S(1)} %fusion), channel_id=1, source_target_pairs={{0,16},{4,20},{8,24},{12,28},{16,0},{20,4},{24,8},{28,12},{1,17},{... | collective-permute-start | bytes 147464 | tf_op jit(solution)/shard_map/ppermute | solution.py:280
  40.7 5.0 %collective-permute-start.14 = (f32[96,128]{1,0:T(8,128)S(1)}, f32[96,128]{1,0:T(8,128)S(1)}, u32[]{:S(2)}, u32[]{:S(2)}) collective-permute-start(f32[96,128]{1,0:T(8,128)S(1)} %fusion), channel_id=1, source_target_pairs={{0,8},{4,12},{8,0},{12,4},{16,24},{20,28},{24,16},{28,20},{1,9},{5... | collective-permute-start | bytes 147464 | tf_op jit(solution)/shard_map/ppermute | solution.py:280
  43.2 2.5 %collective-permute-start.18 = (bf16[64,2048]{1,0:T(8,128)(2,1)S(1)}, bf16[64,2048]{1,0:T(8,128)(2,1)S(1)}, u32[]{:S(2)}, u32[]{:S(2)}) collective-permute-start(bf16[64,2048]{1,0:T(8,128)(2,1)S(1)} %collective-permute-done.17.d2), channel_id=1, source_target_pairs={{0,1},{1,0},{2,3},{3,2},{4,5},{5,4},{6,7},{7,6},{8,9},{9,8},{10,11... | collective-permute-start | bytes 786440 | tf_op jit(solution)/shard_map/ppermute | solution.py:245
